TPU v7x, 256 devices: a whole 4x4x8 slice. The times are simulated.
256 devices in a mesh: grp: 4 (over z_lo, core), ctx: 16 (over z_hi, y), wid: 4 (over x).
Axes of the slice: x: 4, y: 4, z: 8 (z_hi: 4, z_lo: 2; z = z_hi * 2 + z_lo), core: 2. Of those that a mesh axis runs over, the one named last changes fastest.
Arguments:
- query: bfloat16 [256, 64, 128], P(None, 'wid'), may hold values from -64 to 64
- keys: bfloat16 [4, 4096, 8, 128], P(None, ('grp', 'ctx'), 'wid'), may hold values from -64 to 64
- values: bfloat16 [4, 4096, 8, 128], P(None, ('grp', 'ctx'), 'wid'), may hold values from -6 to 6
- lengths: int32 [4, 64], replicated, may hold values from 32 to 64
- query_pos: int32 [256], replicated, may hold values from 1024 to 4095
- resid: bfloat16 [256, 5120], P('wid', ('grp', 'ctx')), may hold values from -1.1953125 to 1.1953125
- out_weight: bfloat16 [8192, 5120], P('wid', ('grp', 'ctx')), may hold values from -0.0625 to 0.0625
- enc_weight: bfloat16 [5120, 24576], P('wid', ('grp', 'ctx')), may hold values from -0.078125 to 0.078125
- enc_bias: float32 [24576], P(('grp', 'ctx')), may hold values from -3 to 3
- dec_weight: bfloat16 [24576, 5120], P(('grp', 'ctx'), 'wid'), may hold values from -0.078125 to 0.078125
- dec_bias: float32 [5120], P('wid'), may hold values from -3 to 3
Outputs:
- layer_out: bfloat16 [256, 5120], P('wid', ('grp', 'ctx'))
- enc_grad: bfloat16 [5120, 24576], P('wid', ('grp', 'ctx'))
- enc_bias_grad: float32 [24576], P(('grp', 'ctx'))
- dec_grad: bfloat16 [24576, 5120], P(('grp', 'ctx'), 'wid')
- dec_bias_grad: float32 [5120], P('wid')
Inputs may be any that keep to these rules, and one draw needn't show every extreme that they name: `lengths`: live slots of a shard are its first ones.
All inputs are finite; a program needn't handle non-finite values.
Results may differ from a plain program's by a relative error of at most 0.024.
Values may be sent and summed in bfloat16 or wider, within the bound.
No kernel may reach another device: no remote copies, remote signals or barrier semaphores. Data moves between devices by JAX's collectives and lax.ppermute only.
A program may use at most 128 MiB of HBM per device.

v0:
```python
import jax
import jax.numpy as jnp
from jax import lax
from jax.sharding import Mesh
from jax.sharding import PartitionSpec as P

HD = 128
GRP_CTX = ("grp_0", "grp_1", "ctx_0", "ctx_1")


def combined_by_axis(shard, axes, combine):
    for axis in axes:
        pieces = jax.tree.map(
            lambda part, kind: lax.all_gather(part.astype(kind), axis),
            shard,
            (jnp.bfloat16, jnp.bfloat16, jnp.bfloat16),
        )
        widened = [
            jax.tree.map(lambda part, own: part[k].astype(own.dtype), pieces, shard)
            for k in range(lax.axis_size(axis))
        ]
        shard = widened[0]
        for theirs in widened[1:]:
            shard = combine(shard, theirs)
    return shard


def in_blocks(shard, dim, length):
    before, after = (shard.shape[:dim], shard.shape[dim + 1 :])
    return jnp.moveaxis(shard.reshape(*before, length, -1, *after), dim, 0)


def summed_on_arrival(shard, axis, dim):
    length = lax.axis_size(axis)
    blocks = lax.all_to_all(in_blocks(shard, dim, length), axis, 0, 0, tiled=True)
    return jnp.sum(blocks.astype(jnp.float32), axis=0)


def from_everyone(shard, axis):
    copies = jnp.broadcast_to(shard, (lax.axis_size(axis), *shard.shape))
    return lax.all_to_all(copies, axis, split_axis=0, concat_axis=0, tiled=True)


def taken_together(shard, axis):
    everything = from_everyone(shard, axis)
    return jnp.sum(everything.astype(jnp.float32), axis=0)


def sent_and_summed(shard, axis, dim):
    length = lax.axis_size(axis)
    blocks = lax.all_to_all(in_blocks(shard, dim, length), axis, 0, 0, tiled=True)
    return jnp.sum(blocks, axis=0)


def combine(earlier, later):
    peak_a, sum_a, weighted_a = earlier
    peak_b, sum_b, weighted_b = later
    peak = jnp.maximum(peak_a, peak_b)
    factor_a = jnp.exp(peak_a - peak)
    factor_b = jnp.exp(peak_b - peak)
    weight_sum = sum_a * factor_a + sum_b * factor_b
    weighted = weighted_a * factor_a[..., None] + weighted_b * factor_b[..., None]
    return (peak, weight_sum, weighted)


def body(
    query,
    keys,
    values,
    lengths,
    query_pos,
    resid,
    out_weight,
    enc_weight,
    enc_bias,
    dec_weight,
    dec_bias,
):
    seq_count, slot_count, kv_local, head_dim = keys.shape
    row_count = query.shape[0]
    heads_local = query.shape[1]
    group_size = heads_local // kv_local
    rows_each = row_count // seq_count
    shard_pos = lax.axis_index(GRP_CTX)
    shard_ids = jnp.arange(lengths.shape[1], dtype=jnp.int32)
    offset = jnp.sum(jnp.where(shard_ids[None, :] < shard_pos, lengths, 0), axis=1)
    live_count = jnp.sum(jnp.where(shard_ids[None, :] == shard_pos, lengths, 0), axis=1)
    slot_ids = jnp.arange(slot_count, dtype=jnp.int32)
    key_pos = offset[:, None] + slot_ids[None, :]
    live_slot = slot_ids[None, :] < live_count[:, None]
    row_position = query_pos.reshape(seq_count, rows_each)
    visible = live_slot[:, None, :] & (key_pos[:, None, :] <= row_position[:, :, None])
    visible_mask = visible[:, :, None, None, :]
    q_view = query.reshape(seq_count, rows_each, kv_local, group_size, head_dim)
    scores = jnp.einsum(
        "srkgd,sjkd->srkgj", q_view, keys, preferred_element_type=jnp.float32
    ) * HD ** (-0.5)
    local_peak = jnp.max(jnp.where(visible_mask, scores, -1e30), axis=-1)
    weights = jnp.where(visible_mask, jnp.exp(scores - local_peak[..., None]), 0.0)
    weight_sum = jnp.sum(weights, axis=-1)
    weights_low = weights.astype(jnp.bfloat16)
    weighted = jnp.einsum(
        "srkgj,sjkd->srkgd", weights_low, values, preferred_element_type=jnp.float32
    )
    weight_sum, weighted = (weight_sum, weighted)
    peak, weight_sum, weighted = combined_by_axis(
        (local_peak, weight_sum, weighted), GRP_CTX, combine
    )
    attention = (weighted / weight_sum[..., None]).astype(jnp.bfloat16)
    attention = attention.reshape(row_count, heads_local * head_dim)
    projected = jnp.dot(attention, out_weight, preferred_element_type=jnp.float32)
    mixed = summed_on_arrival(projected.astype(jnp.bfloat16), "wid", 0)
    layer_out = (mixed + resid.astype(jnp.float32)).astype(jnp.bfloat16)
    wide_rows = lax.all_gather(layer_out, GRP_CTX, axis=1, tiled=True)
    block = lax.all_to_all(wide_rows, "wid", split_axis=1, concat_axis=0, tiled=True)
    enc_part = jnp.dot(block, enc_weight, preferred_element_type=jnp.float32)
    preact = taken_together(enc_part.astype(jnp.bfloat16), "wid").astype(jnp.float32) + enc_bias
    latents = (jax.nn.softplus(4.0 * preact) * 0.25).astype(jnp.bfloat16)
    row_scale = row_count ** (-0.5)
    recon = sent_and_summed(
        jnp.dot(latents, dec_weight, preferred_element_type=jnp.float32), GRP_CTX, 0
    )
    piece_len = recon.shape[0]
    target = lax.dynamic_slice_in_dim(block, shard_pos * piece_len, piece_len, 0).astype(
        jnp.float32
    )
    scaled_error = ((recon + dec_bias - target) * row_scale).astype(jnp.bfloat16)
    error_all = lax.all_gather(scaled_error, GRP_CTX, axis=0, tiled=True)
    dec_bias_grad = jnp.sum(error_all, axis=0, dtype=jnp.float32)
    latent_part = lax.dot_general(
        error_all, dec_weight, (((1,), (1,)), ((), ())), preferred_element_type=jnp.float32
    )
    dec_grad = lax.dot_general(
        latents, error_all, (((0,), (0,)), ((), ())), preferred_element_type=jnp.float32
    )
    latent_grad = taken_together(latent_part.astype(jnp.bfloat16), "wid").astype(jnp.float32)
    preact_grad = (latent_grad * jax.nn.sigmoid(4.0 * preact)).astype(jnp.bfloat16)
    enc_grad = lax.dot_general(
        block, preact_grad, (((0,), (0,)), ((), ())), preferred_element_type=jnp.float32
    ).astype(jnp.bfloat16)
    enc_bias_grad = jnp.sum(preact_grad, axis=0, dtype=jnp.float32)
    return (layer_out, enc_grad, enc_bias_grad, dec_grad.astype(jnp.bfloat16), dec_bias_grad)


def solution(mesh):
    torus = Mesh(
        mesh.devices.reshape(2, 2, 4, 4, mesh.shape["wid"]),
        ("grp_0", "grp_1", "ctx_0", "ctx_1", "wid"),
    )
    in_specs = (
        P(None, "wid", None),
        P(None, GRP_CTX, "wid", None),
        P(None, GRP_CTX, "wid", None),
        P(),
        P(),
        P("wid", GRP_CTX),
        P("wid", GRP_CTX),
        P("wid", GRP_CTX),
        P(GRP_CTX),
        P(GRP_CTX, "wid"),
        P("wid"),
    )
    out_specs = (P("wid", GRP_CTX), P("wid", GRP_CTX), P(GRP_CTX), P(GRP_CTX, "wid"), P("wid"))
    return jax.shard_map(body, mesh=torus, in_specs=in_specs, out_specs=out_specs, check_vma=False)
```

profile of v0, /device:TPU:1, one launch (start us, length us, event | category | flops | bytes accessed | tf_op | source)
XLA Modules:
  0.0 665.7 jit_solution(17610328824982261202)
XLA Ops:
  14.5 4.2 all-gather.1
  19.1 37.6 %all-gather.16.cloned.1.call-done = bf16[8,64,2,8,128]{4,3,2,1,0:T(8,128)(2,1)} async-done(((bf16[4,64,2,8,128]{4,3,2,1,0:T(8,128)(2,1)}), bf16[8,64,2,8,128]{4,3,2,1,0:T(8,128)(2,1)}) %all-gather.16.cloned.1.call-update) | async-done | bytes 2097168 | tf_op jit(solution)/shard_map/all_gather | solution.py:14
  56.6 3.9 fusion.1
  60.7 3.3 all-gather.2
  64.0 3.3 all_gather.60
  67.6 10.2 %all-gather.10.cloned.1.call-done = bf16[2,4,64,2,8,128]{5,4,3,2,1,0:T(8,128)(2,1)} async-done(((bf16[1,4,64,2,8,128]{5,4,3,2,1,0:T(8,128)(2,1)}), bf16[2,4,64,2,8,128]{5,4,3,2,1,0:T(8,128)(2,1)}) %all-gather.10.cloned.1.call-update) | async-done | bytes 2097168 | tf_op jit(solution)/shard_map/all_gather | solution.py:14
  77.8 4.0 add_convert_fusion.1
  83.7 13.0 %all_gather.62 = bf16[4,4,64,2,8]{2,4,3,1,0:T(8,128)(2,1)S(1)} all-gather(bf16[1,4,64,2,8]{2,4,3,1,0:T(8,128)(2,1)S(1)} %get-tuple-element.34), channel_id=1, replica_groups=mesh['grp_0'=2,'grp_1'=2,'ctx_0'=4,'ctx_1'=4,'wid'=4] {'ctx_0'}, dimensions={0}, use_global_device_ids=true | all-gather | bytes 40960 | tf_op jit(solution)/shard_map/all_gather | solution.py:14
  97.7 65.4 %all-gather.12.cloned.1.call-done = bf16[4,4,64,2,8,128]{5,4,3,2,1,0:T(8,128)(2,1)} async-done(((bf16[1,4,64,2,8,128]{5,4,3,2,1,0:T(8,128)(2,1)}), bf16[4,4,64,2,8,128]{5,4,3,2,1,0:T(8,128)(2,1)}) %all-gather.12.cloned.1.call-update) | async-done | bytes 4194320 | tf_op jit(solution)/shard_map/all_gather | solution.py:14
  163.1 7.6 %add_convert_fusion = bf16[1,4,64,2,8,128]{5,4,3,2,1,0:T(8,128)(2,1)} fusion(bf16[4,4,64,2,8,128]{5,4,3,2,1,0:T(8,128)(2,1)} %all-gather.12.cloned.1.call-done, f32[4,64,2,8]{3,2,1,0:T(2,128)S(1)} %copy.104, f32[4,64,2,8]{3,2,1,0:T(2,128)S(1)} %copy.103, f32[4,64,2,8]{3,2,1,0:T(2,128)S(1)} %copy.102, f32[4,64,2,8]{3,2,1,0:T(2,128)S(1)} %copy.101, ...), kind=kLoop, calls=%fused_computation.12 | loop fusion | flops 7340032 | bytes 5341184 | tf_op jit(solution)/shard_map/convert_element_type | solution.py:14
  170.8 16.0 %all_gather.67 = bf16[4,4,64,2,8]{2,4,3,1,0:T(8,128)(2,1)S(1)} all-gather(bf16[1,4,64,2,8]{2,4,3,1,0:T(8,128)(2,1)S(1)} %get-tuple-element.35), channel_id=1, replica_groups=mesh['grp_0'=2,'grp_1'=2,'ctx_0'=4,'ctx_1'=4,'wid'=4] {'ctx_0'}, dimensions={0}, use_global_device_ids=true | all-gather | bytes 40960 | tf_op jit(solution)/shard_map/all_gather | solution.py:14
  186.8 10.4 %all_gather.64 = bf16[4,4,64,2,8]{2,4,3,1,0:T(8,128)(2,1)S(1)} all-gather(bf16[1,4,64,2,8]{2,4,3,1,0:T(8,128)(2,1)S(1)} %get-tuple-element.28), channel_id=1, replica_groups=mesh['grp_0'=2,'grp_1'=2,'ctx_0'=4,'ctx_1'=4,'wid'=4] {'ctx_1'}, dimensions={0}, use_global_device_ids=true | all-gather | bytes 40960 | tf_op jit(solution)/shard_map/all_gather | solution.py:14
  197.1 10.6 %all_gather.68 = bf16[4,4,64,2,8]{2,4,3,1,0:T(8,128)(2,1)S(1)} all-gather(bf16[1,4,64,2,8]{2,4,3,1,0:T(8,128)(2,1)S(1)} %get-tuple-element.29), channel_id=1, replica_groups=mesh['grp_0'=2,'grp_1'=2,'ctx_0'=4,'ctx_1'=4,'wid'=4] {'ctx_1'}, dimensions={0}, use_global_device_ids=true | all-gather | bytes 40960 | tf_op jit(solution)/shard_map/all_gather | solution.py:14
  226.8 4.9 slice_convert_fusion.3
  241.4 9.3 %convolution_convert_fusion.5 = bf16[256,80]{0,1:T(8,128)(2,1)S(1)} fusion(bf16[2048,80]{0,1:T(8,128)(2,1)S(1)} %copy-done.4, f32[256,2048]{1,0:T(8,128)} %div.15, f32[256,2048]{1,0:T(8,128)} %reshape.395, f32[256,2048]{1,0:T(8,128)} %mul.320, f32[256,2048]{1,0:T(8,128)} %mul.317, f32[256,2048]{1,0:T(8,128)} %reshape.393, f32[256,2048]{1,0:T(8,128)} %mul.314, ...), kind=kOutput, calls=%fused_computation.24 | convolution fusion | flops 89673728 | bytes 23437312 | tf_op jit(solution)/shard_map/dot_general | solution.py:111
  250.8 8.2 %all_to_all.39 = bf16[4,64,80]{2,1,0:T(8,128)(2,1)S(1)} all-to-all(bf16[4,64,80]{2,1,0:T(8,128)(2,1)S(1)} %bitcast.336), channel_id=1, replica_groups=mesh['grp_0'=2,'grp_1'=2,'ctx_0'=4,'ctx_1'=4,'wid'=4] {'wid'}, dimensions={0} | all-to-all | bytes 81920 | tf_op jit(solution)/shard_map/all_to_all | solution.py:35
  259.1 153.5 %all-gather.3 = bf16[64,80,64]{1,2,0:T(8,128)(2,1)S(1)} all-gather(bf16[1,80,64]{1,2,0:T(8,128)(2,1)S(1)} %bitcast.339), channel_id=1, replica_groups=mesh['grp_0'=2,'grp_1'=2,'ctx_0'=4,'ctx_1'=4,'wid'=4] {'grp_0','grp_1','..., dimensions={0}, use_global_device_ids=true | all-gather | bytes 665600 | tf_op jit(solution)/shard_map/all_gather | solution.py:114
  415.4 12.7 %all_to_all.40 = bf16[64,4,1280]{2,0,1:T(8,128)(2,1)S(1)} all-to-all(bf16[64,4,1280]{2,0,1:T(8,128)(2,1)S(1)} %bitcast.335), channel_id=1, replica_groups=mesh['grp_0'=2,'grp_1'=2,'ctx_0'=4,'ctx_1'=4,'wid'=4] {'wid'}, dimensions={1} | all-to-all | bytes 1310720 | tf_op jit(solution)/shard_map/all_to_all | solution.py:115
  428.7 15.1 %all_to_all.41 = bf16[4,256,384]{2,1,0:T(8,128)(2,1)S(1)} all-to-all(bf16[4,256,384]{2,1,0:T(8,128)(2,1)S(1)} %broadcast_in_dim.46), channel_id=1, replica_groups=mesh['grp_0'=2,'grp_1'=2,'ctx_0'=4,'ctx_1'=4,'wid'=4] {'wid'}, dimensions={0} | all-to-all | bytes 1572864 | tf_op jit(solution)/shard_map/all_to_all | solution.py:41
  446.1 13.9 %all-to-all-start.3 = ((f32[64,4,1280]{2,1,0:T(4,128)}), f32[64,4,1280]{2,1,0:T(4,128)S(1)}, u32[]{:S(2)}, u32[]{:S(2)}) async-start(f32[64,4,1280]{2,1,0:T(4,128)} %reshape.379), calls=%async_computation.3 | async-start | bytes 2621440 | tf_op jit(solution)/shard_map/all_to_all | solution.py:51
  460.0 34.4 %all-to-all-done.3 = f32[64,4,1280]{2,1,0:T(4,128)S(1)} async-done(((f32[64,4,1280]{2,1,0:T(4,128)}), f32[64,4,1280]{2,1,0:T(4,128)S(1)}, u32[]{:S(2)}, u32[]{:S(2)}) %all-to-all-start.3) | async-done | bytes 1310752 | tf_op jit(solution)/shard_map/all_to_all | solution.py:51
  494.6 143.3 %all-gather.4 = bf16[64,4,1280]{2,1,0:T(4,128)(2,1)S(1)} all-gather(bf16[1,4,1280]{2,1,0:T(4,128)(2,1)S(1)} %fusion.78), channel_id=1, replica_groups=mesh['grp_0'=2,'grp_1'=2,'ctx_0'=4,'ctx_1'=4,'wid'=4] {'grp_0','grp_1','..., dimensions={0}, use_global_device_ids=true | all-gather | bytes 665600 | tf_op jit(solution)/shard_map/all_gather | solution.py:128
  639.5 4.2 all-to-all-start.4
  646.1 9.7 %all-to-all-done.4 = bf16[4,256,384]{2,1,0:T(8,128)(2,1)} async-done(((bf16[4,256,384]{2,1,0:T(8,128)(2,1)}), bf16[4,256,384]{2,1,0:T(8,128)(2,1)}, u32[]{:S(2)}, u32[]{:S(2)}) %all-to-all-start.4) | async-done | bytes 786464 | tf_op jit(solution)/shard_map/all_to_all | solution.py:41
  (105 shorter events, 52.9 us)
Async XLA Ops:
  7.2 2.0 copy-start
  7.2 49.5 %all-gather.16.cloned.1.call-start = ((), (), s32[]{:S(2)}) async-start(), calls=%async_computation.8 | async-start | bytes 3145728 | tf_op jit(solution)/shard_map/all_gather | solution.py:14
  11.3 1.5 copy-start.5
  14.4 63.4 %all-gather.10.cloned.1.call-start = ((), (), s32[]{:S(2)}) async-start(), calls=%async_computation.5 | async-start | bytes 3145728 | tf_op jit(solution)/shard_map/all_gather | solution.py:14
  60.6 102.5 %all-gather.12.cloned.1.call-start = ((), (), s32[]{:S(2)}) async-start(), calls=%async_computation.6 | async-start | bytes 5242880 | tf_op jit(solution)/shard_map/all_gather | solution.py:14
  81.8 145.0 %all-gather.14.cloned.1.call-start = ((), (), s32[]{:S(2)}) async-start(), calls=%async_computation.7 | async-start | bytes 5242880 | tf_op jit(solution)/shard_map/all_gather | solution.py:14
  239.9 1.5 copy-start.4
  241.4 17.7 %copy-start.7 = (bf16[64,80]{1,0:T(8,128)(2,1)S(1)}, bf16[64,80]{1,0:T(8,128)(2,1)}, u32[]{:S(2)}) copy-start(bf16[64,80]{1,0:T(8,128)(2,1)} %param.16) | copy-start | bytes 30724
  259.1 156.3 %copy-start.6 = (bf16[64,80]{1,0:T(8,128)(2,1)}, bf16[64,80]{1,0:T(8,128)(2,1)S(1)}, u32[]{:S(2)}) copy-start(bf16[64,80]{1,0:T(8,128)(2,1)S(1)} %add_convert_fusion.2) | copy-start | bytes 30724
  413.2 14.9 %copy-start.3 = (bf16[1280,384]{1,0:T(8,128)(2,1)S(1)}, bf16[1280,384]{1,0:T(8,128)(2,1)}, u32[]{:S(2)}) copy-start(bf16[1280,384]{1,0:T(8,128)(2,1)} %param.18) | copy-start | bytes 2949124
  428.6 15.3 %copy-start.2 = (bf16[384,1280]{1,0:T(8,128)(2,1)S(1)}, bf16[384,1280]{1,0:T(8,128)(2,1)}, u32[]{:S(2)}) copy-start(bf16[384,1280]{1,0:T(8,128)(2,1)} %param.20) | copy-start | bytes 2949124
  428.6 15.3 %copy-start.8 = (f32[384]{0:T(512)S(1)}, f32[384]{0:T(512)}, u32[]{:S(2)}) copy-start(f32[384]{0:T(512)} %param.19) | copy-start | bytes 4612
  446.1 48.5 %copy-start.9 = (f32[1280]{0:T(1024)S(1)}, f32[1280]{0:T(1024)}, u32[]{:S(2)}) copy-start(f32[1280]{0:T(1024)} %param.21) | copy-start | bytes 15364
  446.1 48.3 %all-to-all-start.3 = ((f32[64,4,1280]{2,1,0:T(4,128)}), f32[64,4,1280]{2,1,0:T(4,128)S(1)}, u32[]{:S(2)}, u32[]{:S(2)}) async-start(f32[64,4,1280]{2,1,0:T(4,128)} %reshape.379), calls=%async_computation.3 | async-start | bytes 2621440 | tf_op jit(solution)/shard_map/all_to_all | solution.py:51
  639.5 16.2 %all-to-all-start.4 = ((bf16[4,256,384]{2,1,0:T(8,128)(2,1)}), bf16[4,256,384]{2,1,0:T(8,128)(2,1)}, u32[]{:S(2)}, u32[]{:S(2)}) async-start(bf16[4,256,384]{2,1,0:T(8,128)(2,1)} %broadcast_in_dim.78), calls=%async_computation.4 | async-start | bytes 1572864 | tf_op jit(solution)/shard_map/all_to_all | solution.py:41
  644.4 14.8 %copy-start.1 = (bf16[256,16,128]{2,1,0:T(8,128)(2,1)S(1)}, bf16[256,16,128]{2,1,0:T(8,128)(2,1)}, u32[]{:S(2)}) copy-start(bf16[256,16,128]{2,1,0:T(8,128)(2,1)} %param.11) | copy-start | bytes 3145732
Sparse Core Ops, SparseCore 0:
  14.5 42.0 all-gather.15
  60.7 17.0 all-gather.9
  81.9 81.1 all-gather.11
  170.9 55.8 all-gather.13
where the time goes:
time: 676 us; the launch traced here: 666 us
  blocking collectives  395 us (58%)
  waiting for transfers between devices  160 us (24%)
  local copies, waits for them, and re-layouts  35.3 us (5%)
  other arithmetic  25.7 us (4%)
  starting transfers between devices  18.3 us (3%)
  matrix products  16.5 us (2%)
  between operations  14.2 us (2%)
    all_gather x1, blocking collectives, body(): wide_rows = lax.all_gather(layer_out, GRP_CTX, axis=1, tiled=True)  153 us
    all_gather x1, blocking collectives, body(): error_all = lax.all_gather(scaled_error, GRP_CTX, axis=0, tiled=True)  143 us
    all_gather x4, waiting for transfers between devices, combined_by_axis(): lax.all_gather(part.astype(kind), axis)  116 us
    all_gather x8, blocking collectives, combined_by_axis(): lax.all_gather(part.astype(kind), axis)  62.5 us
    all_to_all x1, waiting for transfers between devices, sent_and_summed(): lax.all_to_all(in_blocks(shard, dim, length), axis, 0, 0, tiled=True)  34.4 us
    convert_element_type x7, other arithmetic, combined_by_axis(): part.astype(kind)  15.6 us
    all_to_all x1, blocking collectives, from_everyone(): return lax.all_to_all(copies, axis, split_axis=0, concat_axis=0, tiled=True)  15.1 us
    all_to_all x1, starting transfers between devices, sent_and_summed(): lax.all_to_all(in_blocks(shard, dim, length), axis, 0, 0, tiled=True)  13.9 us
  transfers between devices with their start and end apart: 6, of which 6 were waited for; matrix products, arithmetic and copies ran while one was open for 3% of the time, Pallas kernels for 0%

commit v1 on v0

v1 whole, which is shorter than its diff:
```python
import jax
import jax.numpy as jnp
from jax import lax
from jax.sharding import Mesh
from jax.sharding import PartitionSpec as P

HD = 128
ZL, CO, ZH, Y, X = ("zl", "co", "zh", "y", "x")
SHARD = (ZL, CO, ZH, Y)
F32, BF16 = (jnp.float32, jnp.bfloat16)


def other_core(a):
    return lax.ppermute(a, CO, [(0, 1), (1, 0)])


def shifted(a, axis, k):
    n = lax.axis_size(axis)
    return lax.ppermute(a, axis, [(i, (i + k) % n) for i in range(n)])


def exchanged(a, axes):
    return lax.all_to_all(a, axes, 0, 0, tiled=True)


def gathered(a, axes):
    return exchanged(jnp.broadcast_to(a, (lax.axis_size(axes), *a.shape)), axes)


def rounded(a):
    return lax.reduce_precision(a, exponent_bits=8, mantissa_bits=7)


def dot(a, b, contract):
    return lax.dot_general(a, b, (contract, ((), ())), preferred_element_type=F32)


def body(
    query,
    keys,
    values,
    lengths,
    query_pos,
    resid,
    out_weight,
    enc_weight,
    enc_bias,
    dec_weight,
    dec_bias,
):
    zl, co, zh, y, x = (lax.axis_index(name) for name in (ZL, CO, ZH, Y, X))
    seqs, slots, kv_local, head_dim = keys.shape
    rows = query.shape[0]
    heads = query.shape[1]
    group = heads // kv_local
    half = rows // seqs // 2
    width = kv_local * head_dim
    cols = out_weight.shape[1]
    lat = enc_weight.shape[1]
    feats = enc_weight.shape[0]

    kv = jnp.concatenate(
        [keys.reshape(seqs, slots, width), values.reshape(seqs, slots, width)], axis=1
    )
    kv = exchanged(kv, Y)
    kv = jnp.stack([kv, other_core(kv)])
    shards = 2 * seqs
    k_all = kv[:, :, :slots].reshape(shards * slots, kv_local, head_dim)
    v_all = kv[:, :, slots:].reshape(shards * slots, kv_local, head_dim)

    both = jnp.concatenate([out_weight, resid], axis=0).T
    ring = jnp.stack([both] + [shifted(both, Y, k) for k in (1, 2, 3)])
    proj_mine = jnp.concatenate(
        [lax.dynamic_index_in_dim(ring, (y - j) % 4, 0, keepdims=False) for j in range(4)], axis=0
    )
    proj_other = other_core(proj_mine)
    enc_other = other_core(enc_weight)
    dec_other = other_core(dec_weight)
    bias_both = jnp.concatenate([enc_bias, other_core(enc_bias)])

    first = 2 * half * y + half * co
    q = lax.dynamic_slice_in_dim(query, first, half, 0)
    q = q.reshape(half, kv_local, group, head_dim).transpose(1, 2, 0, 3)
    q = q.reshape(kv_local, group * half, head_dim)
    lens = lax.dynamic_index_in_dim(lengths, y, 0, keepdims=False)
    ids = jnp.arange(lens.shape[0], dtype=jnp.int32)
    offsets = jnp.sum(jnp.where(ids[None, :] < ids[:, None], lens[None, :], 0), axis=1)
    slot_ids = jnp.arange(slots, dtype=jnp.int32)

    def positions(c):
        start = ((zl * 2 + c) * 4 + zh) * 4
        own_offset = lax.dynamic_slice_in_dim(offsets, start, 4, 0)
        own_len = lax.dynamic_slice_in_dim(lens, start, 4, 0)
        return jnp.where(
            slot_ids[None, :] < own_len[:, None], own_offset[:, None] + slot_ids[None, :], 1 << 30
        )

    key_pos = jnp.stack([positions(co), positions(1 - co)]).reshape(-1)
    row_pos = lax.dynamic_slice_in_dim(query_pos, first, half, 0)
    visible = key_pos[None, :] <= row_pos[:, None]
    visible = jnp.broadcast_to(visible[None, None], (kv_local, group, half, shards * slots))
    visible = visible.reshape(kv_local, group * half, shards * slots)
    scores = jnp.einsum("kqd,tkd->kqt", q, k_all, preferred_element_type=F32) * HD ** (-0.5)
    peak = jnp.max(jnp.where(visible, scores, -1e30), axis=-1)
    weights = jnp.where(visible, jnp.exp(scores - peak[..., None]), 0.0)
    weight_sum = jnp.sum(weights, axis=-1)
    weighted = jnp.einsum("kqt,tkd->kqd", weights.astype(BF16), v_all, preferred_element_type=F32)
    some = weight_sum > 0.0
    safe = jnp.where(some, weight_sum, 1.0)
    level = jnp.where(some, peak + jnp.log(safe), -1e30)
    high = rounded(level)
    mid = rounded(level - high)
    low = rounded(level - high - mid)
    extras = jnp.stack([high, mid, low], axis=-1).astype(BF16)
    extras = jnp.pad(extras, ((0, 0), (0, 0), (0, HD - 3)))
    payload = jnp.concatenate([(weighted / safe[..., None]).astype(BF16), extras], axis=-1)
    payload = exchanged(payload.reshape(8, 2 * half, 2 * HD), (ZL, ZH)).astype(F32)
    level = payload[:, :, HD] + payload[:, :, HD + 1] + payload[:, :, HD + 2]
    share = jnp.exp(level - jnp.max(level, axis=0))
    attention = jnp.sum(payload[:, :, :HD] * share[..., None], axis=0)
    attention = (attention / jnp.sum(share, axis=0)[..., None]).astype(BF16)
    attention = gathered(attention, (ZL, ZH))
    attention = attention.reshape(heads, half, HD).transpose(1, 0, 2).reshape(half, heads * HD)

    def projected(proj):
        out = dot(attention, proj[:, : heads * HD], ((1,), (1,)))
        res = lax.dynamic_slice_in_dim(proj[:, heads * HD :], half * co, half, 1)
        return (out + jnp.where(x == y, res.astype(F32).T, 0.0)).astype(BF16)

    mine, others = (projected(proj_mine), projected(proj_other))
    part = jnp.stack([jnp.where(co == 0, mine, others), jnp.where(co == 0, others, mine)])
    part = part.reshape(2, 2, half // 2, 4 * cols).transpose(1, 0, 2, 3)
    part = jnp.where(jnp.arange(2)[None, :, None, None, None] == zl, part[:, None], 0)
    part = exchanged(part.reshape(8, half // 2, 4 * cols), (ZL, X))
    piece = jnp.sum(part.astype(F32), axis=0).astype(BF16)

    block = gathered(piece, (ZH, Y, ZL)).reshape(4, seqs * half, 4 * cols)
    my_rows = seqs * half

    def encoded(weight):
        return jnp.einsum(
            "zrf,zfc->rc", block, weight.reshape(4, feats // 4, lat), preferred_element_type=F32
        )

    part = jnp.concatenate([encoded(enc_weight), encoded(enc_other)], axis=1)
    low = part.astype(BF16)
    preact = part + sum(shifted(low, X, k).astype(F32) for k in (1, 2, 3)) + bias_both
    latents = (jax.nn.softplus(4.0 * preact) * 0.25).astype(BF16)

    block_other = other_core(block)
    latents_other = other_core(latents[:, lat:])
    halves = [lax.dynamic_index_in_dim(b, zh, 0, keepdims=False) for b in (block, block_other)]
    halves = [
        lax.dynamic_slice(b, (half * (2 * zl + co), cols * y), (half, cols)) for b in halves
    ]
    halves = [jnp.where(co == 0, halves[0], halves[1]), jnp.where(co == 0, halves[1], halves[0])]
    layer_out = lax.ppermute(
        jnp.concatenate(halves, axis=0),
        (ZL, CO, X),
        [(b * 4 + a, a * 4 + b) for a in range(4) for b in range(4)],
    )

    wide = feats // 2
    few = my_rows // 16

    def decoded(k):
        piece = slice(k * wide, (k + 1) * wide)
        return dot(latents[:, :lat], dec_weight[:, piece], ((1,), (0,))) + dot(
            latents[:, lat:], dec_other[:, piece], ((1,), (0,))
        )

    recon = jnp.stack([decoded(0), decoded(1)]).astype(BF16).reshape(32, few, wide)
    recon = jnp.sum(exchanged(recon, (ZL, ZH, Y)).astype(F32), axis=0)
    at = (zl * 4 + zh) * 4 + y
    natural = block.transpose(1, 0, 2).reshape(my_rows, feats)
    target = lax.dynamic_slice(natural, (few * (at % 16), wide * (at // 16)), (few, wide))
    target_bias = lax.dynamic_slice_in_dim(dec_bias, wide * (at // 16), wide, 0)
    error = ((recon + target_bias - target.astype(F32)) * rows ** (-0.5)).astype(BF16)
    error = gathered(error, (ZL, ZH, Y)).reshape(2, my_rows, wide)
    error_other = other_core(error)

    def pulled(weight):
        return sum(
            dot(error[k], weight[:, k * wide : (k + 1) * wide], ((1,), (1,))) for k in (0, 1)
        )

    part = jnp.concatenate([pulled(dec_weight), pulled(dec_other)], axis=1)
    low = part.astype(BF16)
    latent_grad = part + sum(shifted(low, X, k).astype(F32) for k in (1, 2, 3))
    preact_grad = (latent_grad * jax.nn.sigmoid(4.0 * preact)).astype(BF16)
    preact_grad_other = other_core(preact_grad[:, lat:])
    preact_grad = preact_grad[:, :lat]

    all_latents = jnp.concatenate([latents[:, :lat], latents_other], axis=0)
    all_error = jnp.concatenate([error, error_other], axis=1)
    all_error = all_error.transpose(1, 0, 2).reshape(rows, feats)
    dec_grad = dot(all_latents, all_error, ((0,), (0,))).astype(BF16)
    dec_bias_grad = jnp.sum(all_error, axis=0, dtype=F32)
    all_grad = jnp.concatenate([preact_grad, preact_grad_other], axis=0)
    all_block = jnp.concatenate([block, block_other], axis=1)
    enc_grad = jnp.einsum("zrf,rc->zfc", all_block, all_grad, preferred_element_type=F32)
    enc_grad = enc_grad.astype(BF16).reshape(feats, lat)
    enc_bias_grad = jnp.sum(all_grad, axis=0, dtype=F32)
    return (layer_out, enc_grad, enc_bias_grad, dec_grad, dec_bias_grad)


def solution(mesh):
    torus = Mesh(mesh.devices.reshape(2, 2, 4, 4, mesh.shape["wid"]), (ZL, CO, ZH, Y, X))
    in_specs = (
        P(None, X, None),
        P(None, SHARD, X, None),
        P(None, SHARD, X, None),
        P(),
        P(),
        P(X, SHARD),
        P(X, SHARD),
        P(X, SHARD),
        P(SHARD),
        P(SHARD, X),
        P(X),
    )
    out_specs = (P(X, SHARD), P(X, SHARD), P(SHARD), P(SHARD, X), P(X))
    return jax.shard_map(body, mesh=torus, in_specs=in_specs, out_specs=out_specs, check_vma=False)
```

time: 676 us -> 188 us (0.28); the launches traced: 666 us -> 186 us
  blocking collectives: 395 us -> 10.8 us
  waiting for transfers between devices: 160 us -> 45 us
  starting transfers between devices: 18.3 us -> 69.2 us
  other arithmetic: 25.7 us -> 12.5 us
  between operations: 14.2 us -> 1.42 us
  local copies, waits for them, and re-layouts: 35.3 us -> 28.4 us
    all_gather x10 -> x0, blocking collectives: 359 us -> none  [the longest x1 153 us: body(): wide_rows = lax.all_gather(layer_out, GRP_CTX, axis=1, tiled=True)]
    all_gather x4 -> x0, waiting for transfers between devices: 116 us -> none  [combined_by_axis(): lax.all_gather(part.astype(kind), axis)]
    ppermute x0 -> x19, starting transfers between devices: none -> 32.1 us  [the longest x9 15.9 us: other_core(): return lax.ppermute(a, CO, [(0, 1), (1, 0)])]
    all_to_all x3 -> x1, blocking collectives: 36.1 us -> 10.8 us  [exchanged(): return lax.all_to_all(a, axes, 0, 0, tiled=True)]
    convert_element_type x10 -> x8, other arithmetic: 21.3 us -> 1.67 us  [the longest x1 0.7 us: body(): ((recon + target_bias - target.astype(F32)) * rows ** (-0.5)).astype(BF16)]
    all_to_all x2 -> x6, starting transfers between devices: 18.1 us -> 37.1 us  [exchanged(): return lax.all_to_all(a, axes, 0, 0, tiled=True)]
    mul x12 -> x0, local copies, waits for them, and re-layouts: 12.7 us -> none  [the longest x6 6.38 us: combine(): weighted_a * factor_a[..., None] + weighted_b * factor_b[..., None]]
    convert_element_type x7 -> x0, local copies, waits for them, and re-layouts: 11.6 us -> none  [the longest x4 9.6 us: combined_by_axis(): part[k].astype(own.dtype)]
  transfers between devices with their start and end apart: 6 -> 25, of which waited for: 6 -> 8; matrix products, arithmetic and copies ran while one was open for 3% -> 22% of each run, Pallas kernels for 0% -> 0%
where the time goes in v1:
time: 188 us; the launch traced here: 186 us
  starting transfers between devices  69.2 us (37%)
  waiting for transfers between devices  45 us (24%)
  local copies, waits for them, and re-layouts  28.4 us (15%)
  matrix products  18.5 us (10%)
  other arithmetic  12.5 us (7%)
  blocking collectives  10.8 us (6%)
    all_to_all x6, waiting for transfers between devices, exchanged(): return lax.all_to_all(a, axes, 0, 0, tiled=True)  43.1 us
    all_to_all x6, starting transfers between devices, exchanged(): return lax.all_to_all(a, axes, 0, 0, tiled=True)  37.1 us
    ppermute x9, starting transfers between devices, other_core(): return lax.ppermute(a, CO, [(0, 1), (1, 0)])  15.9 us
    all_to_all x1, blocking collectives, exchanged(): return lax.all_to_all(a, axes, 0, 0, tiled=True)  10.8 us
    dot_general x11, matrix products, dot(): lax.dot_general(a, b, (contract, ((), ())), preferred_element_type=F32)  10 us
    ppermute x9, starting transfers between devices, shifted(): return lax.ppermute(a, axis, [(i, (i + k) % n) for i in range(n)])  9.5 us
    ppermute x1, starting transfers between devices, body(): lax.ppermute(jnp.concatenate(halves, axis=0), (ZL, CO, X), [(b * 4 + a, a...  6.74 us
    dynamic_slice x5, local copies, waits for them, and re-layouts, body(): lax.dynamic_index_in_dim(ring, (y - j) % 4, 0, keepdims=False)  6.55 us
  transfers between devices with their start and end apart: 25, of which 8 were waited for; matrix products, arithmetic and copies ran while one was open for 22% of the time, Pallas kernels for 0%

profile of v1, /device:TPU:1, one launch (start us, length us, event | category | flops | bytes accessed | tf_op | source)
XLA Modules:
  0.0 185.8 jit_solution(7605050194932713233)
XLA Ops:
  2.6 3.6 %collective-permute-start.3 = (bf16[80,2112]{1,0:T(8,128)(2,1)S(1)}, bf16[80,2112]{1,0:T(8,128)(2,1)S(1)}, u32[]{:S(2)}, u32[]{:S(2)}) collective-permute-start(bf16[80,2112]{1,0:T(8,128)(2,1)S(1)} %get-tuple-element.48), channel_id=1, source_target_pairs={{0,12},{4,0},{8,4},{12,8},{1,13},{5,1},{9,5},{13,9},{2,14},{6,2},{... | collective-permute-start | bytes 1013768 | tf_op jit(solution)/shard_map/ppermute | solution.py:19
  9.1 3.4 %all-to-all-start = ((bf16[4,128,256]{2,1,0:T(8,128)(2,1)}), bf16[4,128,256]{2,1,0:T(8,128)(2,1)S(1)}, u32[]{:S(2)}, u32[]{:S(2)}) async-start(bf16[4,128,256]{2,1,0:T(8,128)(2,1)} %pad_maximum_fusion.7), calls=%async_computation | async-start | bytes 524288 | tf_op jit(solution)/shard_map/all_to_all | solution.py:23
  14.0 13.4 %all-to-all-done = bf16[4,128,256]{2,1,0:T(8,128)(2,1)S(1)} async-done(((bf16[4,128,256]{2,1,0:T(8,128)(2,1)}), bf16[4,128,256]{2,1,0:T(8,128)(2,1)S(1)}, u32[]{:S(2)}, u32[]{:S(2)}) %all-to-all-start) | async-done | bytes 262176 | tf_op jit(solution)/shard_map/all_to_all | solution.py:23
  39.0 8.2 %all-to-all-start.1 = ((bf16[8,64,256]{2,1,0:T(8,128)(2,1)}), bf16[8,64,256]{2,1,0:T(8,128)(2,1)S(1)}, u32[]{:S(2)}, u32[]{:S(2)}) async-start(bf16[8,64,256]{2,1,0:T(8,128)(2,1)} %bitcast.11), calls=%async_computation.1 | async-start | bytes 524288 | tf_op jit(solution)/shard_map/all_to_all | solution.py:23
  49.6 2.0 %copy.116 = bf16[1,80,2112]{1,2,0:T(8,128)(2,1)} copy(bf16[1,80,2112]{2,1,0:T(8,128)(2,1)} %get-tuple-element.41) | data formatting | bytes 675840 | tf_op jit(solution)/shard_map/jit(dynamic_index_in_dim)/dynamic_slice | solution.py:74
  53.8 2.5 %pad_maximum_fusion = bf16[320,2112]{0,1:T(8,128)(2,1)S(1)} fusion(bf16[80,2112]{0,1:T(8,128)(2,1)S(1)} %bitcast.121, bf16[80,2112]{0,1:T(8,128)(2,1)} %bitcast.122, bf16[80,2112]{0,1:T(8,128)(2,1)} %bitcast.123, bf16[80,2112]{0,1:T(8,128)(2,1)} %bitcast.124), kind=kLoop, calls=%fused_computation.1 | loop fusion | flops 5406720 | bytes 2703360 | tf_op jit(solution)/shard_map/concatenate | solution.py:73
  56.3 2.9 %copy.118 = bf16[320,2112]{1,0:T(8,128)(2,1)} copy(bf16[320,2112]{0,1:T(8,128)(2,1)S(1)} %pad_maximum_fusion) | data formatting | bytes 2703360 | tf_op jit(solution)/shard_map/concatenate | solution.py:73
  61.0 6.9 %all-to-all-start.2 = ((bf16[8,64,128]{2,1,0:T(8,128)(2,1)}), bf16[8,64,128]{2,1,0:T(8,128)(2,1)S(1)}, u32[]{:S(2)}, u32[]{:S(2)}) async-start(bf16[8,64,128]{2,1,0:T(8,128)(2,1)} %broadcast_in_dim.121), calls=%async_computation.2 | async-start | bytes 262144 | tf_op jit(solution)/shard_map/all_to_all | solution.py:23
  68.4 6.7 %all-to-all-done.2 = bf16[8,64,128]{2,1,0:T(8,128)(2,1)S(1)} async-done(((bf16[8,64,128]{2,1,0:T(8,128)(2,1)}), bf16[8,64,128]{2,1,0:T(8,128)(2,1)S(1)}, u32[]{:S(2)}, u32[]{:S(2)}) %all-to-all-start.2) | async-done | bytes 131104 | tf_op jit(solution)/shard_map/all_to_all | solution.py:23
  76.5 1.9 %broadcast_select_fusion.1 = (bf16[32,320]{1,0:T(8,128)(2,1)S(1)}, bf16[32,320]{1,0:T(8,128)(2,1)S(1)}) fusion(bf16[32,320]{1,0:T(8,128)(2,1)S(1)} %fusion.17, pred[]{:T(512)S(6)} %eq.27, bf16[320,32]{0,1:T(8,128)(2,1)S(1)} %copy.133, pred[]{:T(512)S(6)} %eq.30, bf16[320,2112]{1,0:T(8,128)(2,1)} %collective-permute-done.4, ...), kind=kOutput, calls=%fused_computation.103 | convolution fusion | flops 42004480 | bytes 1523714 | tf_op jit(solution)/shard_map/dot_general | solution.py:35
  78.5 10.8 %all_to_all.35 = bf16[8,16,320]{2,1,0:T(8,128)(2,1)S(1)} all-to-all(bf16[8,16,320]{2,1,0:T(8,128)(2,1)S(1)} %bitcast_select_fusion), channel_id=1, replica_groups=mesh['zl'=2,'co'=2,'zh'=4,'y'=4,'x'=4] {'zl','x'}, dimensions={0} | all-to-all | bytes 163840 | tf_op jit(solution)/shard_map/all_to_all | solution.py:23
  90.1 3.9 %all-to-all-start.4 = ((bf16[32,16,320]{2,1,0:T(8,128)(2,1)}), bf16[32,16,320]{2,1,0:T(8,128)(2,1)S(1)}, u32[]{:S(2)}, u32[]{:S(2)}) async-start(bf16[32,16,320]{2,1,0:T(8,128)(2,1)} %broadcast_in_dim.126), calls=%async_computation.4 | async-start | bytes 786432 | tf_op jit(solution)/shard_map/all_to_all | solution.py:23
  94.0 2.7 %collective-permute-start.12 = (bf16[384,1280]{1,0:T(8,128)(2,1)S(1)}, bf16[384,1280]{1,0:T(8,128)(2,1)}, u32[]{:S(2)}, u32[]{:S(2)}) collective-permute-start(bf16[384,1280]{1,0:T(8,128)(2,1)S(1)} %copy-done.1), channel_id=1, source_target_pairs={{0,64},{64,0},{1,65},{65,1},{2,66},{66,2},{3,67},{67,3},{4,68},{68... | collective-permute-start | bytes 2949128 | tf_op jit(solution)/shard_map/ppermute | solution.py:14
  96.7 8.6 %all-to-all-done.4 = bf16[32,16,320]{2,1,0:T(8,128)(2,1)S(1)} async-done(((bf16[32,16,320]{2,1,0:T(8,128)(2,1)}), bf16[32,16,320]{2,1,0:T(8,128)(2,1)S(1)}, u32[]{:S(2)}, u32[]{:S(2)}) %all-to-all-start.4) | async-done | bytes 327712 | tf_op jit(solution)/shard_map/all_to_all | solution.py:23
  110.6 5.2 %collective-permute-start.11 = (f32[384]{0:T(512)S(1)}, f32[384]{0:T(512)S(1)}, u32[]{:S(2)}, u32[]{:S(2)}) collective-permute-start(f32[384]{0:T(512)S(1)} %copy-done.16), channel_id=1, source_target_pairs={{0,64},{64,0},{1,65},{65,1},{2,66},{66,2},{3,67},{67,3},{4,68},{68... | collective-permute-start | bytes 4616 | tf_op jit(solution)/shard_map/ppermute | solution.py:14
  121.9 9.3 %all-to-all-start.5 = ((bf16[32,8,640]{2,1,0:T(8,128)(2,1)}), bf16[32,8,640]{2,1,0:T(8,128)(2,1)S(1)}, u32[]{:S(2)}, u32[]{:S(2)}) async-start(bf16[32,8,640]{2,1,0:T(8,128)(2,1)} %bitcast.125), calls=%async_computation.5 | async-start | bytes 655360 | tf_op jit(solution)/shard_map/all_to_all | solution.py:23
  135.5 6.8 %all-to-all-done.5 = bf16[32,8,640]{2,1,0:T(8,128)(2,1)S(1)} async-done(((bf16[32,8,640]{2,1,0:T(8,128)(2,1)}), bf16[32,8,640]{2,1,0:T(8,128)(2,1)S(1)}, u32[]{:S(2)}, u32[]{:S(2)}) %all-to-all-start.5) | async-done | bytes 327712 | tf_op jit(solution)/shard_map/all_to_all | solution.py:23
  143.8 5.4 %all-to-all-start.6 = ((bf16[32,8,640]{2,1,0:T(8,128)(2,1)}), bf16[32,8,640]{2,1,0:T(8,128)(2,1)S(1)}, u32[]{:S(2)}, u32[]{:S(2)}) async-start(bf16[32,8,640]{2,1,0:T(8,128)(2,1)} %broadcast_in_dim.127), calls=%async_computation.6 | async-start | bytes 655360 | tf_op jit(solution)/shard_map/all_to_all | solution.py:23
  150.1 2.7 %collective-permute-start.5 = (bf16[4,128,320]{1,2,0:T(8,128)(2,1)}, bf16[4,128,320]{1,2,0:T(8,128)(2,1)}, u32[]{:S(2)}, u32[]{:S(2)}) collective-permute-start(bf16[4,128,320]{1,2,0:T(8,128)(2,1)} %copy.121), channel_id=1, source_target_pairs={{0,64},{64,0},{1,65},{65,1},{2,66},{66,2},{3,67},{67,3},{4,68},{68... | collective-permute-start | bytes 983048 | tf_op jit(solution)/shard_map/ppermute | solution.py:14
  152.8 7.6 %all-to-all-done.6 = bf16[32,8,640]{2,1,0:T(8,128)(2,1)S(1)} async-done(((bf16[32,8,640]{2,1,0:T(8,128)(2,1)}), bf16[32,8,640]{2,1,0:T(8,128)(2,1)S(1)}, u32[]{:S(2)}, u32[]{:S(2)}) %all-to-all-start.6) | async-done | bytes 327712 | tf_op jit(solution)/shard_map/all_to_all | solution.py:23
  163.9 1.8 collective-permute-start.14
  167.4 6.7 %collective-permute-start.6 = (bf16[64,80]{0,1:T(8,128)(2,1)S(1)}, bf16[64,80]{0,1:T(8,128)(2,1)S(1)}, u32[]{:S(2)}, u32[]{:S(2)}) collective-permute-start(bf16[64,80]{0,1:T(8,128)(2,1)S(1)} %pad_maximum_fusion.11), channel_id=1, source_target_pairs={{0,0},{64,1},{128,2},{192,3},{1,64},{65,65},{129,66},{193,67},{2,1... | collective-permute-start | bytes 30728 | tf_op jit(solution)/shard_map/ppermute | solution.py:157
  174.6 3.3 %collective-permute-start.16 = (bf16[128,384]{1,0:T(8,128)(2,1)S(1)}, bf16[128,384]{1,0:T(8,128)(2,1)S(1)}, u32[]{:S(2)}, u32[]{:S(2)}) collective-permute-start(bf16[128,384]{1,0:T(8,128)(2,1)S(1)} %get-tuple-element.52), channel_id=1, source_target_pairs={{0,64},{64,0},{1,65},{65,1},{2,66},{66,2},{3,67},{67,3},{4,68},{68... | collective-permute-start | bytes 294920 | tf_op jit(solution)/shard_map/ppermute | solution.py:14
  179.4 2.4 %convolution_convert_fusion.1 = bf16[4,320,384]{2,1,0:T(8,128)(2,1)} fusion(bf16[4,128,320]{1,2,0:T(8,128)(2,1)} %collective-permute-done.5, bf16[4,128,320]{1,2,0:T(8,128)(2,1)S(1)} %copy-done.11, bf16[128,384]{1,0:T(8,128)(2,1)S(1)} %collective-permute-done.16, bf16[128,384]{1,0:T(8,128)(2,1)S(1)} %get-tuple-element.51), kind=kOutput, calls=%fused_computation.4 | convolution fusion | flops 253853696 | bytes 1835008 | tf_op jit(solution)/shard_map/zrf,rc->zfc/dot_general | solution.py:201
  (157 shorter events, 55.6 us)
Async XLA Ops:
  2.6 26.0 %collective-permute-start.3 = (bf16[80,2112]{1,0:T(8,128)(2,1)S(1)}, bf16[80,2112]{1,0:T(8,128)(2,1)S(1)}, u32[]{:S(2)}, u32[]{:S(2)}) collective-permute-start(bf16[80,2112]{1,0:T(8,128)(2,1)S(1)} %get-tuple-element.48), channel_id=1, source_target_pairs={{0,12},{4,0},{8,4},{12,8},{1,13},{5,1},{9,5},{13,9},{2,14},{6,2},{... | collective-permute-start | bytes 1013768 | tf_op jit(solution)/shard_map/ppermute | solution.py:19
  6.3 22.4 %collective-permute-start.2 = (bf16[80,2112]{1,0:T(8,128)(2,1)S(1)}, bf16[80,2112]{1,0:T(8,128)(2,1)S(1)}, u32[]{:S(2)}, u32[]{:S(2)}) collective-permute-start(bf16[80,2112]{1,0:T(8,128)(2,1)S(1)} %get-tuple-element.48), channel_id=1, source_target_pairs={{0,8},{4,12},{8,0},{12,4},{1,9},{5,13},{9,1},{13,5},{2,10},{6,14},... | collective-permute-start | bytes 1013768 | tf_op jit(solution)/shard_map/ppermute | solution.py:19
  6.6 22.0 %collective-permute-start.1 = (bf16[80,2112]{1,0:T(8,128)(2,1)S(1)}, bf16[80,2112]{1,0:T(8,128)(2,1)S(1)}, u32[]{:S(2)}, u32[]{:S(2)}) collective-permute-start(bf16[80,2112]{1,0:T(8,128)(2,1)S(1)} %get-tuple-element.48), channel_id=1, source_target_pairs={{0,4},{4,8},{8,12},{12,0},{1,5},{5,9},{9,13},{13,1},{2,6},{6,10},{... | collective-permute-start | bytes 1013768 | tf_op jit(solution)/shard_map/ppermute | solution.py:19
  9.1 18.3 %all-to-all-start = ((bf16[4,128,256]{2,1,0:T(8,128)(2,1)}), bf16[4,128,256]{2,1,0:T(8,128)(2,1)S(1)}, u32[]{:S(2)}, u32[]{:S(2)}) async-start(bf16[4,128,256]{2,1,0:T(8,128)(2,1)} %pad_maximum_fusion.7), calls=%async_computation | async-start | bytes 524288 | tf_op jit(solution)/shard_map/all_to_all | solution.py:23
  39.0 20.4 %all-to-all-start.1 = ((bf16[8,64,256]{2,1,0:T(8,128)(2,1)}), bf16[8,64,256]{2,1,0:T(8,128)(2,1)S(1)}, u32[]{:S(2)}, u32[]{:S(2)}) async-start(bf16[8,64,256]{2,1,0:T(8,128)(2,1)} %bitcast.11), calls=%async_computation.1 | async-start | bytes 524288 | tf_op jit(solution)/shard_map/all_to_all | solution.py:23
  59.2 16.2 %collective-permute-start.4 = (bf16[320,2112]{1,0:T(8,128)(2,1)}, bf16[320,2112]{1,0:T(8,128)(2,1)}, u32[]{:S(2)}, u32[]{:S(2)}) collective-permute-start(bf16[320,2112]{1,0:T(8,128)(2,1)} %copy.118), channel_id=1, source_target_pairs={{0,64},{64,0},{1,65},{65,1},{2,66},{66,2},{3,67},{67,3},{4,68},{68... | collective-permute-start | bytes 4055048 | tf_op jit(solution)/shard_map/ppermute | solution.py:14
  61.0 14.1 %all-to-all-start.2 = ((bf16[8,64,128]{2,1,0:T(8,128)(2,1)}), bf16[8,64,128]{2,1,0:T(8,128)(2,1)S(1)}, u32[]{:S(2)}, u32[]{:S(2)}) async-start(bf16[8,64,128]{2,1,0:T(8,128)(2,1)} %broadcast_in_dim.121), calls=%async_computation.2 | async-start | bytes 262144 | tf_op jit(solution)/shard_map/all_to_all | solution.py:23
  67.9 28.8 %collective-permute-start.7 = (bf16[1280,384]{1,0:T(8,128)(2,1)}, bf16[1280,384]{1,0:T(8,128)(2,1)}, u32[]{:S(2)}, u32[]{:S(2)}) collective-permute-start(bf16[1280,384]{1,0:T(8,128)(2,1)} %param.18), channel_id=1, source_target_pairs={{0,64},{64,0},{1,65},{65,1},{2,66},{66,2},{3,67},{67,3},{4,68},{68... | collective-permute-start | bytes 2949128 | tf_op jit(solution)/shard_map/ppermute | solution.py:14
  90.1 15.3 %all-to-all-start.4 = ((bf16[32,16,320]{2,1,0:T(8,128)(2,1)}), bf16[32,16,320]{2,1,0:T(8,128)(2,1)S(1)}, u32[]{:S(2)}, u32[]{:S(2)}) async-start(bf16[32,16,320]{2,1,0:T(8,128)(2,1)} %broadcast_in_dim.126), calls=%async_computation.4 | async-start | bytes 786432 | tf_op jit(solution)/shard_map/all_to_all | solution.py:23
  94.0 24.5 %collective-permute-start.12 = (bf16[384,1280]{1,0:T(8,128)(2,1)S(1)}, bf16[384,1280]{1,0:T(8,128)(2,1)}, u32[]{:S(2)}, u32[]{:S(2)}) collective-permute-start(bf16[384,1280]{1,0:T(8,128)(2,1)S(1)} %copy-done.1), channel_id=1, source_target_pairs={{0,64},{64,0},{1,65},{65,1},{2,66},{66,2},{3,67},{67,3},{4,68},{68... | collective-permute-start | bytes 2949128 | tf_op jit(solution)/shard_map/ppermute | solution.py:14
  108.5 8.2 %collective-permute-start.10 = (bf16[128,768]{1,0:T(8,128)(2,1)S(1)}, bf16[128,768]{1,0:T(8,128)(2,1)S(1)}, u32[]{:S(2)}, u32[]{:S(2)}) collective-permute-start(bf16[128,768]{1,0:T(8,128)(2,1)S(1)} %fusion.45), channel_id=1, source_target_pairs={{0,3},{1,0},{2,1},{3,2},{4,7},{5,4},{6,5},{7,6},{8,11},{9,8},{10,9... | collective-permute-start | bytes 589832 | tf_op jit(solution)/shard_map/ppermute | solution.py:19
  109.4 7.2 %collective-permute-start.9 = (bf16[128,768]{1,0:T(8,128)(2,1)S(1)}, bf16[128,768]{1,0:T(8,128)(2,1)S(1)}, u32[]{:S(2)}, u32[]{:S(2)}) collective-permute-start(bf16[128,768]{1,0:T(8,128)(2,1)S(1)} %fusion.45), channel_id=1, source_target_pairs={{0,2},{1,3},{2,0},{3,1},{4,6},{5,7},{6,4},{7,5},{8,10},{9,11},{10,... | collective-permute-start | bytes 589832 | tf_op jit(solution)/shard_map/ppermute | solution.py:19
  110.6 6.9 %collective-permute-start.8 = (bf16[128,768]{1,0:T(8,128)(2,1)S(1)}, bf16[128,768]{1,0:T(8,128)(2,1)S(1)}, u32[]{:S(2)}, u32[]{:S(2)}) collective-permute-start(bf16[128,768]{1,0:T(8,128)(2,1)S(1)} %fusion.45), channel_id=1, source_target_pairs={{0,1},{1,2},{2,3},{3,0},{4,5},{5,6},{6,7},{7,4},{8,9},{9,10},{10,1... | collective-permute-start | bytes 589832 | tf_op jit(solution)/shard_map/ppermute | solution.py:19
  110.6 6.0 %collective-permute-start.11 = (f32[384]{0:T(512)S(1)}, f32[384]{0:T(512)S(1)}, u32[]{:S(2)}, u32[]{:S(2)}) collective-permute-start(f32[384]{0:T(512)S(1)} %copy-done.16), channel_id=1, source_target_pairs={{0,64},{64,0},{1,65},{65,1},{2,66},{66,2},{3,67},{67,3},{4,68},{68... | collective-permute-start | bytes 4616 | tf_op jit(solution)/shard_map/ppermute | solution.py:14
  121.9 20.4 %all-to-all-start.5 = ((bf16[32,8,640]{2,1,0:T(8,128)(2,1)}), bf16[32,8,640]{2,1,0:T(8,128)(2,1)S(1)}, u32[]{:S(2)}, u32[]{:S(2)}) async-start(bf16[32,8,640]{2,1,0:T(8,128)(2,1)} %bitcast.125), calls=%async_computation.5 | async-start | bytes 655360 | tf_op jit(solution)/shard_map/all_to_all | solution.py:23
  143.8 16.6 %all-to-all-start.6 = ((bf16[32,8,640]{2,1,0:T(8,128)(2,1)}), bf16[32,8,640]{2,1,0:T(8,128)(2,1)S(1)}, u32[]{:S(2)}, u32[]{:S(2)}) async-start(bf16[32,8,640]{2,1,0:T(8,128)(2,1)} %broadcast_in_dim.127), calls=%async_computation.6 | async-start | bytes 655360 | tf_op jit(solution)/shard_map/all_to_all | solution.py:23
  150.1 16.3 %collective-permute-start.5 = (bf16[4,128,320]{1,2,0:T(8,128)(2,1)}, bf16[4,128,320]{1,2,0:T(8,128)(2,1)}, u32[]{:S(2)}, u32[]{:S(2)}) collective-permute-start(bf16[4,128,320]{1,2,0:T(8,128)(2,1)} %copy.121), channel_id=1, source_target_pairs={{0,64},{64,0},{1,65},{65,1},{2,66},{66,2},{3,67},{67,3},{4,68},{68... | collective-permute-start | bytes 983048 | tf_op jit(solution)/shard_map/ppermute | solution.py:14
  163.8 10.5 %collective-permute-start.15 = (bf16[128,768]{1,0:T(8,128)(2,1)S(1)}, bf16[128,768]{1,0:T(8,128)(2,1)S(1)}, u32[]{:S(2)}, u32[]{:S(2)}) collective-permute-start(bf16[128,768]{1,0:T(8,128)(2,1)S(1)} %fusion.44), channel_id=1, source_target_pairs={{0,3},{1,0},{2,1},{3,2},{4,7},{5,4},{6,5},{7,6},{8,11},{9,8},{10,9... | collective-permute-start | bytes 589832 | tf_op jit(solution)/shard_map/ppermute | solution.py:19
  163.9 10.4 %collective-permute-start.14 = (bf16[128,768]{1,0:T(8,128)(2,1)S(1)}, bf16[128,768]{1,0:T(8,128)(2,1)S(1)}, u32[]{:S(2)}, u32[]{:S(2)}) collective-permute-start(bf16[128,768]{1,0:T(8,128)(2,1)S(1)} %fusion.44), channel_id=1, source_target_pairs={{0,2},{1,3},{2,0},{3,1},{4,6},{5,7},{6,4},{7,5},{8,10},{9,11},{10,... | collective-permute-start | bytes 589832 | tf_op jit(solution)/shard_map/ppermute | solution.py:19
  165.7 8.6 %collective-permute-start.13 = (bf16[128,768]{1,0:T(8,128)(2,1)S(1)}, bf16[128,768]{1,0:T(8,128)(2,1)S(1)}, u32[]{:S(2)}, u32[]{:S(2)}) collective-permute-start(bf16[128,768]{1,0:T(8,128)(2,1)S(1)} %fusion.44), channel_id=1, source_target_pairs={{0,1},{1,2},{2,3},{3,0},{4,5},{5,6},{6,7},{7,4},{8,9},{9,10},{10,1... | collective-permute-start | bytes 589832 | tf_op jit(solution)/shard_map/ppermute | solution.py:19
  167.4 10.6 %collective-permute-start.6 = (bf16[64,80]{0,1:T(8,128)(2,1)S(1)}, bf16[64,80]{0,1:T(8,128)(2,1)S(1)}, u32[]{:S(2)}, u32[]{:S(2)}) collective-permute-start(bf16[64,80]{0,1:T(8,128)(2,1)S(1)} %pad_maximum_fusion.11), channel_id=1, source_target_pairs={{0,0},{64,1},{128,2},{192,3},{1,64},{65,65},{129,66},{193,67},{2,1... | collective-permute-start | bytes 30728 | tf_op jit(solution)/shard_map/ppermute | solution.py:157
  174.1 7.7 %collective-permute-start.18 = (bf16[2,128,640]{2,1,0:T(8,128)(2,1)S(1)}, bf16[2,128,640]{2,1,0:T(8,128)(2,1)S(1)}, u32[]{:S(2)}, u32[]{:S(2)}) collective-permute-start(bf16[2,128,640]{2,1,0:T(8,128)(2,1)S(1)} %bitcast.117), channel_id=1, source_target_pairs={{0,64},{64,0},{1,65},{65,1},{2,66},{66,2},{3,67},{67,3},{4,68},{68... | collective-permute-start | bytes 983048 | tf_op jit(solution)/shard_map/ppermute | solution.py:14
  174.6 4.2 %collective-permute-start.16 = (bf16[128,384]{1,0:T(8,128)(2,1)S(1)}, bf16[128,384]{1,0:T(8,128)(2,1)S(1)}, u32[]{:S(2)}, u32[]{:S(2)}) collective-permute-start(bf16[128,384]{1,0:T(8,128)(2,1)S(1)} %get-tuple-element.52), channel_id=1, source_target_pairs={{0,64},{64,0},{1,65},{65,1},{2,66},{66,2},{3,67},{67,3},{4,68},{68... | collective-permute-start | bytes 294920 | tf_op jit(solution)/shard_map/ppermute | solution.py:14
  177.9 6.5 %collective-permute-start.17 = (bf16[128,384]{1,0:T(8,128)(2,1)S(1)}, bf16[128,384]{1,0:T(8,128)(2,1)S(1)}, u32[]{:S(2)}, u32[]{:S(2)}) collective-permute-start(bf16[128,384]{1,0:T(8,128)(2,1)S(1)} %get-tuple-element.50), channel_id=1, source_target_pairs={{0,64},{64,0},{1,65},{65,1},{2,66},{66,2},{3,67},{67,3},{4,68},{68... | collective-permute-start | bytes 294920 | tf_op jit(solution)/shard_map/ppermute | solution.py:14
  (20 other events, 124.3 us)

commit v2 on v1

v2 whole, which is shorter than its diff:
```python
import jax
import jax.numpy as jnp
from jax import lax
from jax.experimental import pallas as pl
from jax.experimental.pallas import tpu as pltpu
from jax.sharding import Mesh
from jax.sharding import PartitionSpec as P

HD = 128
ZL, CO, ZH, Y, X = ("zl", "co", "zh", "y", "x")
SHARD = (ZL, CO, ZH, Y)
F32, BF16 = (jnp.float32, jnp.bfloat16)


def other_core(a):
    return lax.ppermute(a, CO, [(0, 1), (1, 0)])


def shifted(a, axis, k):
    n = lax.axis_size(axis)
    return lax.ppermute(a, axis, [(i, (i + k) % n) for i in range(n)])


def exchanged(a, axes):
    return lax.all_to_all(a, axes, 0, 0, tiled=True)


def gathered(a, axes):
    return exchanged(jnp.broadcast_to(a, (lax.axis_size(axes), *a.shape)), axes)


def dot(a, b, contract):
    return lax.dot_general(a, b, (contract, ((), ())), preferred_element_type=F32)


def attend(q_ref, kv_ref, other_ref, key_ref, row_ref, out_ref):
    slots = kv_ref.shape[1] // 2
    visible = key_ref[...] <= row_ref[...]
    lane = lax.broadcasted_iota(jnp.int32, (q_ref.shape[1], HD), 1)
    for k in range(q_ref.shape[0]):
        across = slice(k * HD, (k + 1) * HD)
        keys, values = (
            jnp.concatenate([ref[j, lo : lo + slots, across] for ref in (kv_ref, other_ref) for j in range(4)])
            for lo in (0, slots)
        )
        scores = dot(q_ref[k], keys, ((1,), (1,))) * HD ** (-0.5)
        peak = jnp.max(jnp.where(visible, scores, -1e30), axis=1, keepdims=True)
        weights = jnp.where(visible, jnp.exp(scores - peak), 0.0)
        weight_sum = jnp.sum(weights, axis=1, keepdims=True)
        weighted = dot(weights.astype(BF16), values, ((1,), (0,)))
        some = weight_sum > 0.0
        safe = jnp.where(some, weight_sum, 1.0)
        level = jnp.where(some, peak + jnp.log(safe), -1e30)
        high = level.astype(BF16).astype(F32)
        mid = (level - high).astype(BF16).astype(F32)
        low = level - high - mid
        extra = jnp.where(lane == 0, high, jnp.where(lane == 1, mid, jnp.where(lane == 2, low, 0.0)))
        parts = out_ref.shape[0] // q_ref.shape[0]
        where = slice(k * parts, (k + 1) * parts)
        out_ref[where, :, :HD] = (weighted / safe).astype(BF16).reshape(parts, -1, HD)
        out_ref[where, :, HD:] = extra.astype(BF16).reshape(parts, -1, HD)


def project(core_ref, message_ref, mine_ref, other_ref, res_mine_ref, res_other_ref, out_ref):
    message = message_ref[...].astype(F32)
    level = jnp.sum(message[:, :, HD:], axis=2, keepdims=True)
    share = jnp.exp(level - jnp.max(level, axis=0, keepdims=True))
    attention = jnp.sum(message[:, :, :HD] * share, axis=0) / jnp.sum(share, axis=0)
    half = attention.shape[0] // 2
    attention = jnp.concatenate([attention[:half], attention[half:]], axis=1).astype(BF16)
    core = core_ref[0]
    wide = out_ref.shape[-1]
    for high in range(2):
        for weight, res, low in ((mine_ref, res_mine_ref, core), (other_ref, res_other_ref, 1 - core)):
            out = dot(attention, weight[high], ((1,), (1,))) + res[high].astype(F32)
            out = out.astype(BF16)
            for cb in range(2):
                for rb in range(4):
                    out_ref[cb, rb, 2 * high + low] = out[8 * rb : 8 * rb + 8, wide * cb : wide * (cb + 1)]


def body(
    query,
    keys,
    values,
    lengths,
    query_pos,
    resid,
    out_weight,
    enc_weight,
    enc_bias,
    dec_weight,
    dec_bias,
):
    zl, co, zh, y, x = (lax.axis_index(name) for name in (ZL, CO, ZH, Y, X))
    seqs, slots, kv_local, head_dim = keys.shape
    rows = query.shape[0]
    heads = query.shape[1]
    group = heads // kv_local
    half = rows // seqs // 2
    width = kv_local * head_dim
    cols = out_weight.shape[1]
    lat = enc_weight.shape[1]
    feats = enc_weight.shape[0]

    kv = jnp.concatenate(
        [keys.reshape(seqs, slots, width), values.reshape(seqs, slots, width)], axis=1
    )
    own = lax.dynamic_index_in_dim(kv, y, 0, keepdims=False)
    kv = [own] + [
        shifted(lax.dynamic_index_in_dim(kv, (y + k) % 4, 0, keepdims=False), Y, k)
        for k in (1, 2, 3)
    ]
    kv = jnp.stack(kv)
    kv_other = other_core(kv)

    proj = out_weight.reshape(8, 2 * HD, cols).transpose(0, 2, 1)
    res = jnp.pad(resid.reshape(8, 8, cols), ((0, 0), (0, 8), (0, 2 * HD - cols)))
    proj = exchanged(jnp.concatenate([proj, res], axis=1), (ZL, ZH))
    proj, kv, kv_other = lax.optimization_barrier((proj, kv, kv_other))
    ring = jnp.stack([proj] + [shifted(proj, Y, k) for k in (1, 2, 3)])
    ring = jnp.stack(
        [lax.dynamic_index_in_dim(ring, (y - j) % 4, 0, keepdims=False) for j in range(4)], axis=1
    )
    ring_other = other_core(ring)
    at = zl * 4 + zh

    def split(ring):
        weight = ring[:, :, :cols].reshape(2, feats, 2 * HD)
        res = ring[:, :, cols : cols + 8, :cols].reshape(2, 4, 4, 8, cols)
        res = res.transpose(0, 3, 1, 2, 4).reshape(2, 1, 8, feats)
        here = (jnp.arange(4) == at % 4) & (x == y) & (co == at // 4)
        return weight, jnp.where(here[None, :, None, None], res, 0).reshape(2, half, feats)

    proj_mine, res_mine = split(ring)
    proj_other, res_other = split(ring_other)
    enc_other = other_core(enc_weight)
    dec_other = other_core(dec_weight)
    bias_both = jnp.concatenate([enc_bias, other_core(enc_bias)])

    first = 2 * half * y + half * co
    q = lax.dynamic_slice_in_dim(query, first, half, 0)
    q = q.reshape(half, kv_local, group, head_dim).transpose(1, 2, 0, 3)
    q = q.reshape(kv_local, group * half, head_dim)
    lens = lax.dynamic_index_in_dim(lengths, y, 0, keepdims=False)
    ids = jnp.arange(lens.shape[0], dtype=jnp.int32)
    offsets = jnp.sum(jnp.where(ids[None, :] < ids[:, None], lens[None, :], 0), axis=1)
    slot_ids = jnp.arange(slots, dtype=jnp.int32)
    turn = (y - jnp.arange(4)) % 4
    shard = ((zl * 2 + jnp.stack([co, 1 - co])[:, None]) * 4 + zh) * 4 + turn[None, :]
    pick = shard[..., None] == ids
    own_offset = jnp.sum(jnp.where(pick, offsets, 0), axis=-1)[..., None]
    own_len = jnp.sum(jnp.where(pick, lens, 0), axis=-1)[..., None]
    key_pos = jnp.where(slot_ids < own_len, own_offset + slot_ids, 1 << 30)
    row_pos = lax.dynamic_slice_in_dim(query_pos, first, half, 0)
    row_pos = jnp.broadcast_to(row_pos[None, :], (group, half)).reshape(-1, 1)

    message = pl.pallas_call(
        attend, out_shape=jax.ShapeDtypeStruct((8, 2 * half, 2 * HD), BF16), name="attend"
    )(q, kv, kv_other, key_pos.reshape(1, -1), row_pos)
    message = exchanged(message, (ZL, ZH))
    part = pl.pallas_call(
        project,
        out_shape=jax.ShapeDtypeStruct((2, 4, 4, 8, feats // 2), BF16),
        in_specs=[pl.BlockSpec(memory_space=pltpu.SMEM)]
        + [pl.BlockSpec(memory_space=pltpu.VMEM)] * 5,
        compiler_params=pltpu.CompilerParams(vmem_limit_bytes=32 * 2**20),
        name="project",
    )(co.reshape(1), message, proj_mine, proj_other, res_mine, res_other)
    part = exchanged(part.reshape(32, 8, feats // 2), (ZL, ZH, X))
    piece = jnp.sum(part.astype(F32), axis=0).astype(BF16)

    my_rows = seqs * half
    wide = feats // 2
    few = my_rows // 16
    block = gathered(piece, (ZL, Y, ZH)).reshape(2, my_rows, wide)

    def encoded(weight):
        return jnp.einsum(
            "zrf,zfc->rc", block, weight.reshape(2, wide, lat), preferred_element_type=F32
        )

    part = jnp.concatenate([encoded(enc_weight), encoded(enc_other)], axis=1)
    low = part.astype(BF16)
    preact = part + sum(shifted(low, X, k).astype(F32) for k in (1, 2, 3)) + bias_both
    latents = (jax.nn.softplus(4.0 * preact) * 0.25).astype(BF16)

    block_other = other_core(block)
    latents_other = other_core(latents[:, lat:])
    halves = [lax.dynamic_index_in_dim(b, zh // 2, 0, keepdims=False) for b in (block, block_other)]
    spot = (half * (2 * zl + co), 4 * cols * (zh % 2) + cols * y)
    halves = [lax.dynamic_slice(b, spot, (half, cols)) for b in halves]
    halves = [jnp.where(co == 0, halves[0], halves[1]), jnp.where(co == 0, halves[1], halves[0])]
    layer_out = lax.ppermute(
        jnp.concatenate(halves, axis=0),
        (ZL, CO, X),
        [(b * 4 + a, a * 4 + b) for a in range(4) for b in range(4)],
    )

    def decoded(k):
        piece = slice(k * wide, (k + 1) * wide)
        return dot(latents[:, :lat], dec_weight[:, piece], ((1,), (0,))) + dot(
            latents[:, lat:], dec_other[:, piece], ((1,), (0,))
        )

    recon = jnp.stack([decoded(0), decoded(1)]).astype(BF16).reshape(32, few, wide)
    recon = jnp.sum(exchanged(recon, (ZL, Y, ZH)).astype(F32), axis=0)
    target_bias = lax.dynamic_slice_in_dim(dec_bias, wide * zl, wide, 0)
    error = ((recon + target_bias - piece.astype(F32)) * rows ** (-0.5)).astype(BF16)
    error = gathered(error, (ZL, Y, ZH)).reshape(2, my_rows, wide)
    error_other = other_core(error)

    def pulled(weight):
        return sum(
            dot(error[k], weight[:, k * wide : (k + 1) * wide], ((1,), (1,))) for k in (0, 1)
        )

    part = jnp.concatenate([pulled(dec_weight), pulled(dec_other)], axis=1)
    low = part.astype(BF16)
    latent_grad = part + sum(shifted(low, X, k).astype(F32) for k in (1, 2, 3))
    preact_grad = (latent_grad * jax.nn.sigmoid(4.0 * preact)).astype(BF16)
    preact_grad_other = other_core(preact_grad[:, lat:])
    preact_grad = preact_grad[:, :lat]

    all_latents = jnp.concatenate([latents[:, :lat], latents_other], axis=0)
    all_error = jnp.concatenate([error, error_other], axis=1)
    all_error = all_error.transpose(1, 0, 2).reshape(rows, feats)
    dec_grad = dot(all_latents, all_error, ((0,), (0,))).astype(BF16)
    dec_bias_grad = jnp.sum(all_error, axis=0, dtype=F32)
    all_grad = jnp.concatenate([preact_grad, preact_grad_other], axis=0)
    all_block = jnp.concatenate([block, block_other], axis=1)
    enc_grad = jnp.einsum("zrf,rc->zfc", all_block, all_grad, preferred_element_type=F32)
    enc_grad = enc_grad.astype(BF16).reshape(feats, lat)
    enc_bias_grad = jnp.sum(all_grad, axis=0, dtype=F32)
    return (layer_out, enc_grad, enc_bias_grad, dec_grad, dec_bias_grad)


def solution(mesh):
    torus = Mesh(mesh.devices.reshape(2, 2, 4, 4, mesh.shape["wid"]), (ZL, CO, ZH, Y, X))
    in_specs = (
        P(None, X, None),
        P(None, SHARD, X, None),
        P(None, SHARD, X, None),
        P(),
        P(),
        P(X, SHARD),
        P(X, SHARD),
        P(X, SHARD),
        P(SHARD),
        P(SHARD, X),
        P(X),
    )
    out_specs = (P(X, SHARD), P(X, SHARD), P(SHARD), P(SHARD, X), P(X))
    return jax.shard_map(body, mesh=torus, in_specs=in_specs, out_specs=out_specs, check_vma=False)
```

time: 188 us -> 185 us (0.984)
  starting transfers between devices: 69.2 us -> 85.5 us
  waiting for transfers between devices: 45 us -> 60.5 us
  blocking collectives: 10.8 us -> 0 us
  local copies, waits for them, and re-layouts: 28.4 us -> 17.8 us
  matrix products: 18.5 us -> 8.12 us
  other arithmetic: 12.5 us -> 6.17 us
  Pallas kernels: 0 us -> 4.46 us
    ppermute x9 -> x12, waiting for transfers between devices: 0.93 us -> 20.2 us  [shifted(): return lax.ppermute(a, axis, [(i, (i + k) % n) for i in range(n)])]
    all_to_all x1 -> x0, blocking collectives: 10.8 us -> none  [exchanged(): return lax.all_to_all(a, axes, 0, 0, tiled=True)]
    dynamic_slice x10 -> x2, local copies, waits for them, and re-layouts: 9.17 us -> 1.4 us  [the longest x1 1.37 us: body(): target_bias = lax.dynamic_slice_in_dim(dec_bias, wide * zl, wide, 0)]
    ppermute x9 -> x12, starting transfers between devices: 9.5 us -> 16.9 us  [shifted(): return lax.ppermute(a, axis, [(i, (i + k) % n) for i in range(n)])]
    dot_general x11 -> x9, matrix products: 10 us -> 3.65 us  [dot(): lax.dot_general(a, b, (contract, ((), ())), preferred_element_type=F32)]
    all_to_all x6, starting transfers between devices: 37.1 us -> 42.8 us  [exchanged(): return lax.all_to_all(a, axes, 0, 0, tiled=True)]
    all_to_all x6, waiting for transfers between devices: 43.1 us -> 37.5 us  [exchanged(): return lax.all_to_all(a, axes, 0, 0, tiled=True)]
    slice x2 -> x4, local copies, waits for them, and re-layouts: 0.9 us -> 5.58 us  [the longest x2 3.89 us: split(): weight = ring[:, :, :cols].reshape(2, feats, 2 * HD)]
  transfers between devices with their start and end apart: 25 -> 28, of which waited for: 8 -> 12; matrix products, arithmetic and copies ran while one was open for 22% -> 12% of each run, Pallas kernels for 0% -> 2%
where the time goes in v2:
time: 185 us; the launch traced here: 184 us
  starting transfers between devices  85.5 us (46%)
  waiting for transfers between devices  60.5 us (33%)
  local copies, waits for them, and re-layouts  17.8 us (10%)
  matrix products  8.12 us (4%)
  other arithmetic  6.17 us (3%)
  Pallas kernels  4.46 us (2%)
    all_to_all x6, starting transfers between devices, exchanged(): return lax.all_to_all(a, axes, 0, 0, tiled=True)  42.8 us
    all_to_all x6, waiting for transfers between devices, exchanged(): return lax.all_to_all(a, axes, 0, 0, tiled=True)  37.5 us
    ppermute x12, waiting for transfers between devices, shifted(): return lax.ppermute(a, axis, [(i, (i + k) % n) for i in range(n)])  20.2 us
    ppermute x9, starting transfers between devices, other_core(): return lax.ppermute(a, CO, [(0, 1), (1, 0)])  17.5 us
    ppermute x12, starting transfers between devices, shifted(): return lax.ppermute(a, axis, [(i, (i + k) % n) for i in range(n)])  16.9 us
    ppermute x1, starting transfers between devices, body(): lax.ppermute(jnp.concatenate(halves, axis=0), (ZL, CO, X), [(b * 4 + a, a...  8.28 us
    slice x2, local copies, waits for them, and re-layouts, split(): weight = ring[:, :, :cols].reshape(2, feats, 2 * HD)  3.89 us
  transfers between devices with their start and end apart: 28, of which 12 were waited for; matrix products, arithmetic and copies ran while one was open for 12% of the time, Pallas kernels for 2%

profile of v2, /device:TPU:1, one launch (start us, length us, event | category | flops | bytes accessed | tf_op | source)
XLA Modules:
  0.0 184.0 jit_solution(6233958454354404365)
XLA Ops:
  3.4 9.0 %all-to-all-start = ((bf16[8,96,256]{2,1,0:T(8,128)(2,1)}), bf16[8,96,256]{2,1,0:T(8,128)(2,1)S(1)}, u32[]{:S(2)}, u32[]{:S(2)}) async-start(bf16[8,96,256]{2,1,0:T(8,128)(2,1)} %copy.68), calls=%async_computation | async-start | bytes 786432 | tf_op jit(solution)/shard_map/all_to_all | solution.py:25
  12.8 2.8 %collective-permute-start.2 = (bf16[128,256]{1,0:T(8,128)(2,1)S(1)}, bf16[128,256]{1,0:T(8,128)(2,1)S(1)}, u32[]{:S(2)}, u32[]{:S(2)}) collective-permute-start(bf16[128,256]{1,0:T(8,128)(2,1)S(1)} %get-tuple-element.20), channel_id=1, source_target_pairs={{0,12},{4,0},{8,4},{12,8},{1,13},{5,1},{9,5},{13,9},{2,14},{6,2},{... | collective-permute-start | bytes 196616 | tf_op jit(solution)/shard_map/ppermute | solution.py:21
  17.2 3.6 %collective-permute-done = bf16[128,256]{1,0:T(8,128)(2,1)S(1)} collective-permute-done((bf16[128,256]{1,0:T(8,128)(2,1)S(1)}, bf16[128,256]{1,0:T(8,128)(2,1)S(1)}, u32[]{:S(2)}, u32[]{:S(2)}) %collective-permute-start) | collective-permute-done | bytes 65568 | tf_op jit(solution)/shard_map/ppermute | solution.py:21
  21.0 2.2 %collective-permute-start.3 = (bf16[4,128,256]{2,1,0:T(8,128)(2,1)S(1)}, bf16[4,128,256]{2,1,0:T(8,128)(2,1)S(1)}, u32[]{:S(2)}, u32[]{:S(2)}) collective-permute-start(bf16[4,128,256]{2,1,0:T(8,128)(2,1)S(1)} %pad_maximum_fusion.5.kv_ref), channel_id=1, source_target_pairs={{0,64},{64,0},{1,65},{65,1},{2,66},{66,2},{3,67},{67,3},{4,68},{68... | collective-permute-start | bytes 786440 | tf_op jit(solution)/shard_map/ppermute | solution.py:16
  24.3 3.7 %collective-permute-start.5 = (bf16[8,96,256]{2,1,0:T(8,128)(2,1)S(1)}, bf16[8,96,256]{2,1,0:T(8,128)(2,1)S(1)}, u32[]{:S(2)}, u32[]{:S(2)}) collective-permute-start(bf16[8,96,256]{2,1,0:T(8,128)(2,1)S(1)} %all-to-all-done), channel_id=1, source_target_pairs={{0,8},{4,12},{8,0},{12,4},{1,9},{5,13},{9,1},{13,5},{2,10},{6,14},... | collective-permute-start | bytes 1179656 | tf_op jit(solution)/shard_map/ppermute | solution.py:21
  28.1 7.0 %collective-permute-done.4 = bf16[8,96,256]{2,1,0:T(8,128)(2,1)S(1)} collective-permute-done((bf16[8,96,256]{2,1,0:T(8,128)(2,1)S(1)}, bf16[8,96,256]{2,1,0:T(8,128)(2,1)S(1)}, u32[]{:S(2)}, u32[]{:S(2)}) %collective-permute-start.4) | collective-permute-done | bytes 393248 | tf_op jit(solution)/shard_map/ppermute | solution.py:21
  35.1 9.3 %collective-permute-done.5 = bf16[8,96,256]{2,1,0:T(8,128)(2,1)S(1)} collective-permute-done((bf16[8,96,256]{2,1,0:T(8,128)(2,1)S(1)}, bf16[8,96,256]{2,1,0:T(8,128)(2,1)S(1)}, u32[]{:S(2)}, u32[]{:S(2)}) %collective-permute-start.5) | collective-permute-done | bytes 393248 | tf_op jit(solution)/shard_map/ppermute | solution.py:21
  51.9 2.8 %attend.1 = bf16[8,64,256]{2,1,0:T(8,128)(2,1)} custom-call(bf16[2,256,128]{2,1,0:T(8,128)(2,1)} %bitcast.104, bf16[4,128,256]{2,1,0:T(8,128)(2,1)} %copy-done.9, bf16[4,128,256]{2,1,0:T(8,128)(2,1)} %copy-done.17, s32[1,512]{1,0:T(1,128)} %select_n.184.key_ref, s32[256,1]{1,0:T(8,128)} %reshape.244.row_ref), custom_call_target="tpu_custom_call" | custom-call | tf_op jit(solution)/shard_map/attend/pallas_call | solution.py:158
  54.7 6.9 %all-to-all-start.1 = ((bf16[8,64,256]{2,1,0:T(8,128)(2,1)}), bf16[8,64,256]{2,1,0:T(8,128)(2,1)S(1)}, u32[]{:S(2)}, u32[]{:S(2)}) async-start(bf16[8,64,256]{2,1,0:T(8,128)(2,1)} %attend.1), calls=%async_computation.1 | async-start | bytes 524288 | tf_op jit(solution)/shard_map/all_to_all | solution.py:25
  65.1 2.5 %slice.69 = bf16[8,4,80,256]{3,2,1,0:T(8,128)(2,1)} slice(bf16[8,4,96,256]{3,2,1,0:T(8,128)(2,1)} %collective-permute-done.7), slice={[0:8], [0:4], [0:80], [0:256]} | slice | bytes 2621440 | tf_op jit(solution)/shard_map/slice | solution.py:129
  72.7 8.5 %all-to-all-start.2 = ((bf16[32,8,640]{2,1,0:T(8,128)(2,1)}), bf16[32,8,640]{2,1,0:T(8,128)(2,1)S(1)}, u32[]{:S(2)}, u32[]{:S(2)}) async-start(bf16[32,8,640]{2,1,0:T(8,128)(2,1)} %bitcast.30), calls=%async_computation.2 | async-start | bytes 655360 | tf_op jit(solution)/shard_map/all_to_all | solution.py:25
  82.4 11.0 %all-to-all-done.2 = bf16[32,8,640]{2,1,0:T(8,128)(2,1)S(1)} async-done(((bf16[32,8,640]{2,1,0:T(8,128)(2,1)}), bf16[32,8,640]{2,1,0:T(8,128)(2,1)S(1)}, u32[]{:S(2)}, u32[]{:S(2)}) %all-to-all-start.2) | async-done | bytes 327712 | tf_op jit(solution)/shard_map/all_to_all | solution.py:25
  94.2 5.5 %all-to-all-start.3 = ((bf16[32,8,640]{2,1,0:T(8,128)(2,1)}), bf16[32,8,640]{2,1,0:T(8,128)(2,1)S(1)}, u32[]{:S(2)}, u32[]{:S(2)}) async-start(bf16[32,8,640]{2,1,0:T(8,128)(2,1)} %broadcast_in_dim.113), calls=%async_computation.3 | async-start | bytes 655360 | tf_op jit(solution)/shard_map/all_to_all | solution.py:25
  99.7 2.2 %collective-permute-start.15 = (bf16[384,1280]{1,0:T(8,128)(2,1)S(1)}, bf16[384,1280]{1,0:T(8,128)(2,1)S(1)}, u32[]{:S(2)}, u32[]{:S(2)}) collective-permute-start(bf16[384,1280]{1,0:T(8,128)(2,1)S(1)} %copy-done.2), channel_id=1, source_target_pairs={{0,64},{64,0},{1,65},{65,1},{2,66},{66,2},{3,67},{67,3},{4,68},{68... | collective-permute-start | bytes 2949128 | tf_op jit(solution)/shard_map/ppermute | solution.py:16
  101.9 8.3 %all-to-all-done.3 = bf16[32,8,640]{2,1,0:T(8,128)(2,1)S(1)} async-done(((bf16[32,8,640]{2,1,0:T(8,128)(2,1)}), bf16[32,8,640]{2,1,0:T(8,128)(2,1)S(1)}, u32[]{:S(2)}, u32[]{:S(2)}) %all-to-all-start.3) | async-done | bytes 327712 | tf_op jit(solution)/shard_map/all_to_all | solution.py:25
  115.8 5.0 %collective-permute-start.14 = (f32[384]{0:T(512)S(1)}, f32[384]{0:T(512)S(1)}, u32[]{:S(2)}, u32[]{:S(2)}) collective-permute-start(f32[384]{0:T(512)S(1)} %copy-done.20), channel_id=1, source_target_pairs={{0,64},{64,0},{1,65},{65,1},{2,66},{66,2},{3,67},{67,3},{4,68},{68... | collective-permute-start | bytes 4616 | tf_op jit(solution)/shard_map/ppermute | solution.py:16
  123.9 7.7 %all-to-all-start.4 = ((bf16[32,8,640]{2,1,0:T(8,128)(2,1)}), bf16[32,8,640]{2,1,0:T(8,128)(2,1)S(1)}, u32[]{:S(2)}, u32[]{:S(2)}) async-start(bf16[32,8,640]{2,1,0:T(8,128)(2,1)} %bitcast.101), calls=%async_computation.4 | async-start | bytes 655360 | tf_op jit(solution)/shard_map/all_to_all | solution.py:25
  133.1 9.2 %all-to-all-done.4 = bf16[32,8,640]{2,1,0:T(8,128)(2,1)S(1)} async-done(((bf16[32,8,640]{2,1,0:T(8,128)(2,1)}), bf16[32,8,640]{2,1,0:T(8,128)(2,1)S(1)}, u32[]{:S(2)}, u32[]{:S(2)}) %all-to-all-start.4) | async-done | bytes 327712 | tf_op jit(solution)/shard_map/all_to_all | solution.py:25
  143.8 5.1 %all-to-all-start.5 = ((bf16[32,8,640]{2,1,0:T(8,128)(2,1)}), bf16[32,8,640]{2,1,0:T(8,128)(2,1)S(1)}, u32[]{:S(2)}, u32[]{:S(2)}) async-start(bf16[32,8,640]{2,1,0:T(8,128)(2,1)} %broadcast_in_dim.114), calls=%async_computation.5 | async-start | bytes 655360 | tf_op jit(solution)/shard_map/all_to_all | solution.py:25
  148.9 3.5 %collective-permute-start.8 = (bf16[2,128,640]{2,1,0:T(8,128)(2,1)}, bf16[2,128,640]{2,1,0:T(8,128)(2,1)}, u32[]{:S(2)}, u32[]{:S(2)}) collective-permute-start(bf16[2,128,640]{2,1,0:T(8,128)(2,1)} %bitcast.96), channel_id=1, source_target_pairs={{0,64},{64,0},{1,65},{65,1},{2,66},{66,2},{3,67},{67,3},{4,68},{68... | collective-permute-start | bytes 983048 | tf_op jit(solution)/shard_map/ppermute | solution.py:16
  152.3 7.1 %all-to-all-done.5 = bf16[32,8,640]{2,1,0:T(8,128)(2,1)S(1)} async-done(((bf16[32,8,640]{2,1,0:T(8,128)(2,1)}), bf16[32,8,640]{2,1,0:T(8,128)(2,1)S(1)}, u32[]{:S(2)}, u32[]{:S(2)}) %all-to-all-start.5) | async-done | bytes 327712 | tf_op jit(solution)/shard_map/all_to_all | solution.py:25
  161.9 4.1 %collective-permute-start.17 = (bf16[128,768]{1,0:T(8,128)(2,1)S(1)}, bf16[128,768]{1,0:T(8,128)(2,1)S(1)}, u32[]{:S(2)}, u32[]{:S(2)}) collective-permute-start(bf16[128,768]{1,0:T(8,128)(2,1)S(1)} %fusion.23), channel_id=1, source_target_pairs={{0,2},{1,3},{2,0},{3,1},{4,6},{5,7},{6,4},{7,5},{8,10},{9,11},{10,... | collective-permute-start | bytes 589832 | tf_op jit(solution)/shard_map/ppermute | solution.py:21
  166.8 8.3 %collective-permute-start.9 = (bf16[64,80]{1,0:T(8,128)(2,1)S(1)}, bf16[64,80]{1,0:T(8,128)(2,1)S(1)}, u32[]{:S(2)}, u32[]{:S(2)}) collective-permute-start(bf16[64,80]{1,0:T(8,128)(2,1)S(1)} %pad_maximum_fusion.8), channel_id=1, source_target_pairs={{0,0},{64,1},{128,2},{192,3},{1,64},{65,65},{129,66},{193,67},{2,1... | collective-permute-start | bytes 30728 | tf_op jit(solution)/shard_map/ppermute | solution.py:194
  178.5 2.5 %convolution_convert_fusion.1 = bf16[2,640,384]{2,1,0:T(8,128)(2,1)} fusion(bf16[2,128,640]{2,1,0:T(8,128)(2,1)} %collective-permute-done.8, bf16[2,128,640]{2,1,0:T(8,128)(2,1)S(1)} %bitcast.98, bf16[128,384]{1,0:T(8,128)(2,1)S(1)} %collective-permute-done.19, bf16[128,384]{1,0:T(8,128)(2,1)S(1)} %get-tuple-element.25), kind=kOutput, calls=%fused_computation.3 | convolution fusion | flops 253853696 | bytes 1835008 | tf_op jit(solution)/shard_map/zrf,rc->zfc/dot_general | solution.py:232
  (150 shorter events, 45.0 us)
Async XLA Ops:
  3.4 20.9 %all-to-all-start = ((bf16[8,96,256]{2,1,0:T(8,128)(2,1)}), bf16[8,96,256]{2,1,0:T(8,128)(2,1)S(1)}, u32[]{:S(2)}, u32[]{:S(2)}) async-start(bf16[8,96,256]{2,1,0:T(8,128)(2,1)} %copy.68), calls=%async_computation | async-start | bytes 786432 | tf_op jit(solution)/shard_map/all_to_all | solution.py:25
  15.6 5.3 %collective-permute-start = (bf16[128,256]{1,0:T(8,128)(2,1)S(1)}, bf16[128,256]{1,0:T(8,128)(2,1)S(1)}, u32[]{:S(2)}, u32[]{:S(2)}) collective-permute-start(bf16[128,256]{1,0:T(8,128)(2,1)S(1)} %get-tuple-element.22), channel_id=1, source_target_pairs={{0,4},{4,8},{8,12},{12,0},{1,5},{5,9},{9,13},{13,1},{2,6},{6,10},{... | collective-permute-start | bytes 196616 | tf_op jit(solution)/shard_map/ppermute | solution.py:21
  15.6 5.3 %collective-permute-start.1 = (bf16[128,256]{1,0:T(8,128)(2,1)S(1)}, bf16[128,256]{1,0:T(8,128)(2,1)S(1)}, u32[]{:S(2)}, u32[]{:S(2)}) collective-permute-start(bf16[128,256]{1,0:T(8,128)(2,1)S(1)} %get-tuple-element.21), channel_id=1, source_target_pairs={{0,8},{4,12},{8,0},{12,4},{1,9},{5,13},{9,1},{13,5},{2,10},{6,14},... | collective-permute-start | bytes 196616 | tf_op jit(solution)/shard_map/ppermute | solution.py:21
  24.3 10.8 %collective-permute-start.4 = (bf16[8,96,256]{2,1,0:T(8,128)(2,1)S(1)}, bf16[8,96,256]{2,1,0:T(8,128)(2,1)S(1)}, u32[]{:S(2)}, u32[]{:S(2)}) collective-permute-start(bf16[8,96,256]{2,1,0:T(8,128)(2,1)S(1)} %all-to-all-done), channel_id=1, source_target_pairs={{0,4},{4,8},{8,12},{12,0},{1,5},{5,9},{9,13},{13,1},{2,6},{6,10},{... | collective-permute-start | bytes 1179656 | tf_op jit(solution)/shard_map/ppermute | solution.py:21
  24.3 20.0 %collective-permute-start.5 = (bf16[8,96,256]{2,1,0:T(8,128)(2,1)S(1)}, bf16[8,96,256]{2,1,0:T(8,128)(2,1)S(1)}, u32[]{:S(2)}, u32[]{:S(2)}) collective-permute-start(bf16[8,96,256]{2,1,0:T(8,128)(2,1)S(1)} %all-to-all-done), channel_id=1, source_target_pairs={{0,8},{4,12},{8,0},{12,4},{1,9},{5,13},{9,1},{13,5},{2,10},{6,14},... | collective-permute-start | bytes 1179656 | tf_op jit(solution)/shard_map/ppermute | solution.py:21
  28.0 16.5 %collective-permute-start.6 = (bf16[8,96,256]{2,1,0:T(8,128)(2,1)S(1)}, bf16[8,96,256]{2,1,0:T(8,128)(2,1)S(1)}, u32[]{:S(2)}, u32[]{:S(2)}) collective-permute-start(bf16[8,96,256]{2,1,0:T(8,128)(2,1)S(1)} %all-to-all-done), channel_id=1, source_target_pairs={{0,12},{4,0},{8,4},{12,8},{1,13},{5,1},{9,5},{13,9},{2,14},{6,2},{... | collective-permute-start | bytes 1179656 | tf_op jit(solution)/shard_map/ppermute | solution.py:21
  46.3 17.8 %collective-permute-start.7 = (bf16[8,4,96,256]{3,2,1,0:T(8,128)(2,1)}, bf16[8,4,96,256]{3,2,1,0:T(8,128)(2,1)}, u32[]{:S(2)}, u32[]{:S(2)}) collective-permute-start(bf16[8,4,96,256]{3,2,1,0:T(8,128)(2,1)} %pad_maximum_fusion.1), channel_id=1, source_target_pairs={{0,64},{64,0},{1,65},{65,1},{2,66},{66,2},{3,67},{67,3},{4,68},{68... | collective-permute-start | bytes 4718600 | tf_op jit(solution)/shard_map/ppermute | solution.py:16
  54.7 15.0 %all-to-all-start.1 = ((bf16[8,64,256]{2,1,0:T(8,128)(2,1)}), bf16[8,64,256]{2,1,0:T(8,128)(2,1)S(1)}, u32[]{:S(2)}, u32[]{:S(2)}) async-start(bf16[8,64,256]{2,1,0:T(8,128)(2,1)} %attend.1), calls=%async_computation.1 | async-start | bytes 524288 | tf_op jit(solution)/shard_map/all_to_all | solution.py:25
  72.7 20.6 %all-to-all-start.2 = ((bf16[32,8,640]{2,1,0:T(8,128)(2,1)}), bf16[32,8,640]{2,1,0:T(8,128)(2,1)S(1)}, u32[]{:S(2)}, u32[]{:S(2)}) async-start(bf16[32,8,640]{2,1,0:T(8,128)(2,1)} %bitcast.30), calls=%async_computation.2 | async-start | bytes 655360 | tf_op jit(solution)/shard_map/all_to_all | solution.py:25
  81.2 20.7 %collective-permute-start.10 = (bf16[1280,384]{1,0:T(8,128)(2,1)}, bf16[1280,384]{1,0:T(8,128)(2,1)}, u32[]{:S(2)}, u32[]{:S(2)}) collective-permute-start(bf16[1280,384]{1,0:T(8,128)(2,1)} %param.18), channel_id=1, source_target_pairs={{0,64},{64,0},{1,65},{65,1},{2,66},{66,2},{3,67},{67,3},{4,68},{68... | collective-permute-start | bytes 2949128 | tf_op jit(solution)/shard_map/ppermute | solution.py:16
  94.2 16.0 %all-to-all-start.3 = ((bf16[32,8,640]{2,1,0:T(8,128)(2,1)}), bf16[32,8,640]{2,1,0:T(8,128)(2,1)S(1)}, u32[]{:S(2)}, u32[]{:S(2)}) async-start(bf16[32,8,640]{2,1,0:T(8,128)(2,1)} %broadcast_in_dim.113), calls=%async_computation.3 | async-start | bytes 655360 | tf_op jit(solution)/shard_map/all_to_all | solution.py:25
  99.7 22.9 %collective-permute-start.15 = (bf16[384,1280]{1,0:T(8,128)(2,1)S(1)}, bf16[384,1280]{1,0:T(8,128)(2,1)S(1)}, u32[]{:S(2)}, u32[]{:S(2)}) collective-permute-start(bf16[384,1280]{1,0:T(8,128)(2,1)S(1)} %copy-done.2), channel_id=1, source_target_pairs={{0,64},{64,0},{1,65},{65,1},{2,66},{66,2},{3,67},{67,3},{4,68},{68... | collective-permute-start | bytes 2949128 | tf_op jit(solution)/shard_map/ppermute | solution.py:16
  112.3 9.3 %collective-permute-start.11 = (bf16[128,768]{1,0:T(8,128)(2,1)S(1)}, bf16[128,768]{1,0:T(8,128)(2,1)S(1)}, u32[]{:S(2)}, u32[]{:S(2)}) collective-permute-start(bf16[128,768]{1,0:T(8,128)(2,1)S(1)} %fusion.24), channel_id=1, source_target_pairs={{0,1},{1,2},{2,3},{3,0},{4,5},{5,6},{6,7},{7,4},{8,9},{9,10},{10,1... | collective-permute-start | bytes 589832 | tf_op jit(solution)/shard_map/ppermute | solution.py:21
  112.6 9.0 %collective-permute-start.12 = (bf16[128,768]{1,0:T(8,128)(2,1)S(1)}, bf16[128,768]{1,0:T(8,128)(2,1)S(1)}, u32[]{:S(2)}, u32[]{:S(2)}) collective-permute-start(bf16[128,768]{1,0:T(8,128)(2,1)S(1)} %fusion.24), channel_id=1, source_target_pairs={{0,2},{1,3},{2,0},{3,1},{4,6},{5,7},{6,4},{7,5},{8,10},{9,11},{10,... | collective-permute-start | bytes 589832 | tf_op jit(solution)/shard_map/ppermute | solution.py:21
  114.5 7.2 %collective-permute-start.13 = (bf16[128,768]{1,0:T(8,128)(2,1)S(1)}, bf16[128,768]{1,0:T(8,128)(2,1)S(1)}, u32[]{:S(2)}, u32[]{:S(2)}) collective-permute-start(bf16[128,768]{1,0:T(8,128)(2,1)S(1)} %fusion.24), channel_id=1, source_target_pairs={{0,3},{1,0},{2,1},{3,2},{4,7},{5,4},{6,5},{7,6},{8,11},{9,8},{10,9... | collective-permute-start | bytes 589832 | tf_op jit(solution)/shard_map/ppermute | solution.py:21
  115.8 5.9 %collective-permute-start.14 = (f32[384]{0:T(512)S(1)}, f32[384]{0:T(512)S(1)}, u32[]{:S(2)}, u32[]{:S(2)}) collective-permute-start(f32[384]{0:T(512)S(1)} %copy-done.20), channel_id=1, source_target_pairs={{0,64},{64,0},{1,65},{65,1},{2,66},{66,2},{3,67},{67,3},{4,68},{68... | collective-permute-start | bytes 4616 | tf_op jit(solution)/shard_map/ppermute | solution.py:16
  123.9 18.3 %all-to-all-start.4 = ((bf16[32,8,640]{2,1,0:T(8,128)(2,1)}), bf16[32,8,640]{2,1,0:T(8,128)(2,1)S(1)}, u32[]{:S(2)}, u32[]{:S(2)}) async-start(bf16[32,8,640]{2,1,0:T(8,128)(2,1)} %bitcast.101), calls=%async_computation.4 | async-start | bytes 655360 | tf_op jit(solution)/shard_map/all_to_all | solution.py:25
  143.8 15.6 %all-to-all-start.5 = ((bf16[32,8,640]{2,1,0:T(8,128)(2,1)}), bf16[32,8,640]{2,1,0:T(8,128)(2,1)S(1)}, u32[]{:S(2)}, u32[]{:S(2)}) async-start(bf16[32,8,640]{2,1,0:T(8,128)(2,1)} %broadcast_in_dim.114), calls=%async_computation.5 | async-start | bytes 655360 | tf_op jit(solution)/shard_map/all_to_all | solution.py:25
  148.9 17.1 %collective-permute-start.8 = (bf16[2,128,640]{2,1,0:T(8,128)(2,1)}, bf16[2,128,640]{2,1,0:T(8,128)(2,1)}, u32[]{:S(2)}, u32[]{:S(2)}) collective-permute-start(bf16[2,128,640]{2,1,0:T(8,128)(2,1)} %bitcast.96), channel_id=1, source_target_pairs={{0,64},{64,0},{1,65},{65,1},{2,66},{66,2},{3,67},{67,3},{4,68},{68... | collective-permute-start | bytes 983048 | tf_op jit(solution)/shard_map/ppermute | solution.py:16
  160.7 14.5 %collective-permute-start.16 = (bf16[128,768]{1,0:T(8,128)(2,1)S(1)}, bf16[128,768]{1,0:T(8,128)(2,1)S(1)}, u32[]{:S(2)}, u32[]{:S(2)}) collective-permute-start(bf16[128,768]{1,0:T(8,128)(2,1)S(1)} %fusion.23), channel_id=1, source_target_pairs={{0,1},{1,2},{2,3},{3,0},{4,5},{5,6},{6,7},{7,4},{8,9},{9,10},{10,1... | collective-permute-start | bytes 589832 | tf_op jit(solution)/shard_map/ppermute | solution.py:21
  161.9 13.3 %collective-permute-start.17 = (bf16[128,768]{1,0:T(8,128)(2,1)S(1)}, bf16[128,768]{1,0:T(8,128)(2,1)S(1)}, u32[]{:S(2)}, u32[]{:S(2)}) collective-permute-start(bf16[128,768]{1,0:T(8,128)(2,1)S(1)} %fusion.23), channel_id=1, source_target_pairs={{0,2},{1,3},{2,0},{3,1},{4,6},{5,7},{6,4},{7,5},{8,10},{9,11},{10,... | collective-permute-start | bytes 589832 | tf_op jit(solution)/shard_map/ppermute | solution.py:21
  166.0 9.3 %collective-permute-start.18 = (bf16[128,768]{1,0:T(8,128)(2,1)S(1)}, bf16[128,768]{1,0:T(8,128)(2,1)S(1)}, u32[]{:S(2)}, u32[]{:S(2)}) collective-permute-start(bf16[128,768]{1,0:T(8,128)(2,1)S(1)} %fusion.23), channel_id=1, source_target_pairs={{0,3},{1,0},{2,1},{3,2},{4,7},{5,4},{6,5},{7,6},{8,11},{9,8},{10,9... | collective-permute-start | bytes 589832 | tf_op jit(solution)/shard_map/ppermute | solution.py:21
  166.8 10.2 %collective-permute-start.9 = (bf16[64,80]{1,0:T(8,128)(2,1)S(1)}, bf16[64,80]{1,0:T(8,128)(2,1)S(1)}, u32[]{:S(2)}, u32[]{:S(2)}) collective-permute-start(bf16[64,80]{1,0:T(8,128)(2,1)S(1)} %pad_maximum_fusion.8), channel_id=1, source_target_pairs={{0,0},{64,1},{128,2},{192,3},{1,64},{65,65},{129,66},{193,67},{2,1... | collective-permute-start | bytes 30728 | tf_op jit(solution)/shard_map/ppermute | solution.py:194
  175.1 5.8 %collective-permute-start.21 = (bf16[2,128,640]{2,1,0:T(8,128)(2,1)S(1)}, bf16[2,128,640]{2,1,0:T(8,128)(2,1)S(1)}, u32[]{:S(2)}, u32[]{:S(2)}) collective-permute-start(bf16[2,128,640]{2,1,0:T(8,128)(2,1)S(1)} %bitcast.91), channel_id=1, source_target_pairs={{0,64},{64,0},{1,65},{65,1},{2,66},{66,2},{3,67},{67,3},{4,68},{68... | collective-permute-start | bytes 983048 | tf_op jit(solution)/shard_map/ppermute | solution.py:16
  (26 other events, 293.8 us)

commit v3 on v2

--- a/solution.py
+++ b/solution.py
@@ -61,22 +61,30 @@
         out_ref[where, :, HD:] = extra.astype(BF16).reshape(parts, -1, HD)
 
 
-def project(core_ref, message_ref, mine_ref, other_ref, res_mine_ref, res_other_ref, out_ref):
+def combine(message_ref, out_ref):
     message = message_ref[...].astype(F32)
     level = jnp.sum(message[:, :, HD:], axis=2, keepdims=True)
     share = jnp.exp(level - jnp.max(level, axis=0, keepdims=True))
     attention = jnp.sum(message[:, :, :HD] * share, axis=0) / jnp.sum(share, axis=0)
     half = attention.shape[0] // 2
-    attention = jnp.concatenate([attention[:half], attention[half:]], axis=1).astype(BF16)
-    core = core_ref[0]
-    wide = out_ref.shape[-1]
+    out_ref[:, :HD] = attention[:half].astype(BF16)
+    out_ref[:, HD:] = attention[half:].astype(BF16)
+
+
+def project(at_ref, a_ref, b_ref, c_ref, d_ref, mine_ref, other_ref, res_mine_ref, res_other_ref, out_ref):
+    attention = jnp.concatenate([ref[...] for ref in (a_ref, b_ref, c_ref, d_ref)])
+    few, cols = (out_ref.shape[2], out_ref.shape[3] // 4)
+    turn, core = (at_ref[0], at_ref[1])
     for high in range(2):
-        for weight, res, low in ((mine_ref, res_mine_ref, core), (other_ref, res_other_ref, 1 - core)):
-            out = dot(attention, weight[high], ((1,), (1,))) + res[high].astype(F32)
+        for ref, res, low in ((mine_ref, res_mine_ref, core), (other_ref, res_other_ref, 1 - core)):
+            weight = jnp.concatenate([ref[4 * high + j, :cols] for j in range(4)])
+            out = dot(attention, weight, ((1,), (1,))) + res[high].astype(F32)
             out = out.astype(BF16)
-            for cb in range(2):
-                for rb in range(4):
-                    out_ref[cb, rb, 2 * high + low] = out[8 * rb : 8 * rb + 8, wide * cb : wide * (cb + 1)]
+            for k in range(4):
+                seq = lax.rem(turn - k + 4, 4)
+                for r in range(2):
+                    start = few * (2 * k + r)
+                    out_ref[2 * seq + r, 2 * high + low] = out[start : start + few]
 
 
 def body(
@@ -106,48 +114,42 @@
     kv = jnp.concatenate(
         [keys.reshape(seqs, slots, width), values.reshape(seqs, slots, width)], axis=1
     )
-    own = lax.dynamic_index_in_dim(kv, y, 0, keepdims=False)
-    kv = [own] + [
-        shifted(lax.dynamic_index_in_dim(kv, (y + k) % 4, 0, keepdims=False), Y, k)
+    ring = [lax.dynamic_index_in_dim(kv, zh, 0, keepdims=False)] + [
+        shifted(lax.dynamic_index_in_dim(kv, (zh + k) % 4, 0, keepdims=False), ZH, k)
         for k in (1, 2, 3)
     ]
-    kv = jnp.stack(kv)
-    kv_other = other_core(kv)
 
     proj = out_weight.reshape(8, 2 * HD, cols).transpose(0, 2, 1)
     res = jnp.pad(resid.reshape(8, 8, cols), ((0, 0), (0, 8), (0, 2 * HD - cols)))
-    proj = exchanged(jnp.concatenate([proj, res], axis=1), (ZL, ZH))
-    proj, kv, kv_other = lax.optimization_barrier((proj, kv, kv_other))
-    ring = jnp.stack([proj] + [shifted(proj, Y, k) for k in (1, 2, 3)])
-    ring = jnp.stack(
-        [lax.dynamic_index_in_dim(ring, (y - j) % 4, 0, keepdims=False) for j in range(4)], axis=1
-    )
-    ring_other = other_core(ring)
-    at = zl * 4 + zh
-
-    def split(ring):
-        weight = ring[:, :, :cols].reshape(2, feats, 2 * HD)
-        res = ring[:, :, cols : cols + 8, :cols].reshape(2, 4, 4, 8, cols)
-        res = res.transpose(0, 3, 1, 2, 4).reshape(2, 1, 8, feats)
-        here = (jnp.arange(4) == at % 4) & (x == y) & (co == at // 4)
-        return weight, jnp.where(here[None, :, None, None], res, 0).reshape(2, half, feats)
-
-    proj_mine, res_mine = split(ring)
-    proj_other, res_other = split(ring_other)
+    proj = jnp.concatenate([proj, res], axis=1)
+    ring[1], proj = lax.optimization_barrier((ring[1], proj))
+    proj_mine = exchanged(proj, (ZL, Y))
+    kv = jnp.stack(ring)
+    kv_other = other_core(kv)
+    proj_other = other_core(proj_mine)
+    at = zl * 4 + y
+    turn = (zh - jnp.arange(4)) % 4
+
+    def residual(proj):
+        res = proj[:, cols : cols + 8, :cols].reshape(2, 4, 8, cols)
+        res = res.transpose(0, 2, 1, 3).reshape(2, 1, 1, 8, 4 * cols)
+        here = (jnp.arange(4) == at % 4) & (turn == x)[:, None] & (co == at // 4)
+        return jnp.where(here[None, :, :, None, None], res, 0).reshape(2, seqs * half, 4 * cols)
+
+    res_mine, res_other = (residual(proj_mine), residual(proj_other))
     enc_other = other_core(enc_weight)
     dec_other = other_core(dec_weight)
     bias_both = jnp.concatenate([enc_bias, other_core(enc_bias)])
 
-    first = 2 * half * y + half * co
+    first = 2 * half * zh + half * co
     q = lax.dynamic_slice_in_dim(query, first, half, 0)
     q = q.reshape(half, kv_local, group, head_dim).transpose(1, 2, 0, 3)
     q = q.reshape(kv_local, group * half, head_dim)
-    lens = lax.dynamic_index_in_dim(lengths, y, 0, keepdims=False)
+    lens = lax.dynamic_index_in_dim(lengths, zh, 0, keepdims=False)
     ids = jnp.arange(lens.shape[0], dtype=jnp.int32)
     offsets = jnp.sum(jnp.where(ids[None, :] < ids[:, None], lens[None, :], 0), axis=1)
     slot_ids = jnp.arange(slots, dtype=jnp.int32)
-    turn = (y - jnp.arange(4)) % 4
-    shard = ((zl * 2 + jnp.stack([co, 1 - co])[:, None]) * 4 + zh) * 4 + turn[None, :]
+    shard = ((zl * 2 + jnp.stack([co, 1 - co])[:, None]) * 4 + turn[None, :]) * 4 + y
     pick = shard[..., None] == ids
     own_offset = jnp.sum(jnp.where(pick, offsets, 0), axis=-1)[..., None]
     own_len = jnp.sum(jnp.where(pick, lens, 0), axis=-1)[..., None]
@@ -158,26 +160,29 @@
     message = pl.pallas_call(
         attend, out_shape=jax.ShapeDtypeStruct((8, 2 * half, 2 * HD), BF16), name="attend"
     )(q, kv, kv_other, key_pos.reshape(1, -1), row_pos)
-    message = exchanged(message, (ZL, ZH))
+    message = exchanged(message, (ZL, Y))
+    attention = pl.pallas_call(
+        combine, out_shape=jax.ShapeDtypeStruct((half, 2 * HD), BF16), name="combine"
+    )(message)
+    ring = [attention] + [shifted(attention, ZH, k) for k in (1, 2, 3)]
     part = pl.pallas_call(
         project,
-        out_shape=jax.ShapeDtypeStruct((2, 4, 4, 8, feats // 2), BF16),
+        out_shape=jax.ShapeDtypeStruct((8, 4, half // 2, 4 * cols), BF16),
         in_specs=[pl.BlockSpec(memory_space=pltpu.SMEM)]
-        + [pl.BlockSpec(memory_space=pltpu.VMEM)] * 5,
-        compiler_params=pltpu.CompilerParams(vmem_limit_bytes=32 * 2**20),
+        + [pl.BlockSpec(memory_space=pltpu.VMEM)] * 8,
         name="project",
-    )(co.reshape(1), message, proj_mine, proj_other, res_mine, res_other)
-    part = exchanged(part.reshape(32, 8, feats // 2), (ZL, ZH, X))
+    )(jnp.stack([zh, co]), *ring, proj_mine, proj_other, res_mine, res_other)
+    part = exchanged(part.reshape(32, half // 2, 4 * cols), (ZL, Y, X))
     piece = jnp.sum(part.astype(F32), axis=0).astype(BF16)
 
     my_rows = seqs * half
     wide = feats // 2
     few = my_rows // 16
-    block = gathered(piece, (ZL, Y, ZH)).reshape(2, my_rows, wide)
+    block = gathered(piece, (ZH, ZL, Y)).reshape(4, my_rows, 4 * cols)
 
     def encoded(weight):
         return jnp.einsum(
-            "zrf,zfc->rc", block, weight.reshape(2, wide, lat), preferred_element_type=F32
+            "zrf,zfc->rc", block, weight.reshape(4, feats // 4, lat), preferred_element_type=F32
         )
 
     part = jnp.concatenate([encoded(enc_weight), encoded(enc_other)], axis=1)
@@ -187,8 +192,8 @@
 
     block_other = other_core(block)
     latents_other = other_core(latents[:, lat:])
-    halves = [lax.dynamic_index_in_dim(b, zh // 2, 0, keepdims=False) for b in (block, block_other)]
-    spot = (half * (2 * zl + co), 4 * cols * (zh % 2) + cols * y)
+    halves = [lax.dynamic_index_in_dim(b, zh, 0, keepdims=False) for b in (block, block_other)]
+    spot = (half * (2 * zl + co), cols * y)
     halves = [lax.dynamic_slice(b, spot, (half, cols)) for b in halves]
     halves = [jnp.where(co == 0, halves[0], halves[1]), jnp.where(co == 0, halves[1], halves[0])]
     layer_out = lax.ppermute(
@@ -204,10 +209,13 @@
         )
 
     recon = jnp.stack([decoded(0), decoded(1)]).astype(BF16).reshape(32, few, wide)
-    recon = jnp.sum(exchanged(recon, (ZL, Y, ZH)).astype(F32), axis=0)
-    target_bias = lax.dynamic_slice_in_dim(dec_bias, wide * zl, wide, 0)
-    error = ((recon + target_bias - piece.astype(F32)) * rows ** (-0.5)).astype(BF16)
-    error = gathered(error, (ZL, Y, ZH)).reshape(2, my_rows, wide)
+    recon = jnp.sum(exchanged(recon, (ZL, ZH, Y)).astype(F32), axis=0)
+    at = (zl * 4 + zh) * 4 + y
+    natural = block.transpose(1, 0, 2).reshape(my_rows, feats)
+    target = lax.dynamic_slice(natural, (few * (at % 16), wide * (at // 16)), (few, wide))
+    target_bias = lax.dynamic_slice_in_dim(dec_bias, wide * (at // 16), wide, 0)
+    error = ((recon + target_bias - target.astype(F32)) * rows ** (-0.5)).astype(BF16)
+    error = gathered(error, (ZL, ZH, Y)).reshape(2, my_rows, wide)
     error_other = other_core(error)
 
     def pulled(weight):

time: 185 us -> 172 us (0.930)
  waiting for transfers between devices: 60.5 us -> 34.5 us
  matrix products: 8.12 us -> 13.2 us
  starting transfers between devices: 85.5 us -> 90.3 us
  Pallas kernels: 4.46 us -> 6.98 us
    ppermute x12, waiting for transfers between devices: 20.2 us -> 4.44 us  [shifted(): return lax.ppermute(a, axis, [(i, (i + k) % n) for i in range(n)])]
    all_to_all x6, starting transfers between devices: 42.8 us -> 30.3 us  [exchanged(): return lax.all_to_all(a, axes, 0, 0, tiled=True)]
    ppermute x9, starting transfers between devices: 17.5 us -> 26.1 us  [other_core(): return lax.ppermute(a, CO, [(0, 1), (1, 0)])]
    all_to_all x6, waiting for transfers between devices: 37.5 us -> 29.2 us  [exchanged(): return lax.all_to_all(a, axes, 0, 0, tiled=True)]
    ppermute x12, starting transfers between devices: 16.9 us -> 23.2 us  [shifted(): return lax.ppermute(a, axis, [(i, (i + k) % n) for i in range(n)])]
    slice x4 -> x2, local copies, waits for them, and re-layouts: 5.58 us -> 0.01 us  [residual(): res = proj[:, cols:cols + 8, :cols].reshape(2, 4, 8, cols)]
    dot_general x9, matrix products: 3.65 us -> 7.76 us  [dot(): lax.dot_general(a, b, (contract, ((), ())), preferred_element_type=F32)]
    pallas_call x1 -> x2, Pallas kernels: 1.66 us -> 4.19 us  [the longest x1 2.41 us: body(): pl.pallas_call(project, out_shape=jax.ShapeDtypeStruct((8, 4, half // 2,...]
  transfers between devices with their start and end apart: 28 -> 28, of which waited for: 12 -> 8; matrix products, arithmetic and copies ran while one was open for 12% -> 15% of each run, Pallas kernels for 2% -> 3%
where the time goes in v3:
time: 172 us; the launch traced here: 171 us
  starting transfers between devices  90.3 us (52%)
  waiting for transfers between devices  34.5 us (20%)
  local copies, waits for them, and re-layouts  18 us (10%)
  matrix products  13.2 us (8%)
  Pallas kernels  6.98 us (4%)
  other arithmetic  6.9 us (4%)
    all_to_all x6, starting transfers between devices, exchanged(): return lax.all_to_all(a, axes, 0, 0, tiled=True)  30.3 us
    all_to_all x6, waiting for transfers between devices, exchanged(): return lax.all_to_all(a, axes, 0, 0, tiled=True)  29.2 us
    ppermute x9, starting transfers between devices, other_core(): return lax.ppermute(a, CO, [(0, 1), (1, 0)])  26.1 us
    ppermute x12, starting transfers between devices, shifted(): return lax.ppermute(a, axis, [(i, (i + k) % n) for i in range(n)])  23.2 us
    ppermute x1, starting transfers between devices, body(): lax.ppermute(jnp.concatenate(halves, axis=0), (ZL, CO, X), [(b * 4 + a, a...  10.7 us
    dot_general x9, matrix products, dot(): lax.dot_general(a, b, (contract, ((), ())), preferred_element_type=F32)  7.76 us
    unnamed x47, local copies, waits for them, and re-layouts  5.24 us
    ppermute x12, waiting for transfers between devices, shifted(): return lax.ppermute(a, axis, [(i, (i + k) % n) for i in range(n)])  4.44 us
  transfers between devices with their start and end apart: 28, of which 8 were waited for; matrix products, arithmetic and copies ran while one was open for 15% of the time, Pallas kernels for 3%

profile of v3, /device:TPU:1, one launch (start us, length us, event | category | flops | bytes accessed | tf_op | source)
XLA Modules:
  0.0 171.2 jit_solution(3345414867220508681)
XLA Ops:
  2.9 6.9 %collective-permute-start.2 = (bf16[128,256]{1,0:T(8,128)(2,1)S(1)}, bf16[128,256]{1,0:T(8,128)(2,1)S(1)}, u32[]{:S(2)}, u32[]{:S(2)}) collective-permute-start(bf16[128,256]{1,0:T(8,128)(2,1)S(1)} %get-tuple-element.39), channel_id=1, source_target_pairs={{0,48},{16,0},{32,16},{48,32},{1,49},{17,1},{33,17},{49,33},{2,50}... | collective-permute-start | bytes 196616 | tf_op jit(solution)/shard_map/ppermute | solution.py:21
  14.1 3.7 %collective-permute-done = bf16[128,256]{1,0:T(8,128)(2,1)S(1)} collective-permute-done((bf16[128,256]{1,0:T(8,128)(2,1)S(1)}, bf16[128,256]{1,0:T(8,128)(2,1)S(1)}, u32[]{:S(2)}, u32[]{:S(2)}) %collective-permute-start) | collective-permute-done | bytes 65568 | tf_op jit(solution)/shard_map/ppermute | solution.py:21
  17.8 4.2 %all-to-all-start.1 = ((bf16[8,96,256]{2,1,0:T(8,128)(2,1)}), bf16[8,96,256]{2,1,0:T(8,128)(2,1)S(1)}, u32[]{:S(2)}, u32[]{:S(2)}) async-start(bf16[8,96,256]{2,1,0:T(8,128)(2,1)} %fusion.20), calls=%async_computation.1 | async-start | bytes 786432 | tf_op jit(solution)/shard_map/all_to_all | solution.py:25
  22.9 3.6 %collective-permute-start.3 = (bf16[4,128,256]{2,1,0:T(8,128)(2,1)S(1)}, bf16[4,128,256]{2,1,0:T(8,128)(2,1)S(1)}, u32[]{:S(2)}, u32[]{:S(2)}) collective-permute-start(bf16[4,128,256]{2,1,0:T(8,128)(2,1)S(1)} %pad_maximum_fusion.3.kv_ref), channel_id=1, source_target_pairs={{0,64},{64,0},{1,65},{65,1},{2,66},{66,2},{3,67},{67,3},{4,68},{68... | collective-permute-start | bytes 786440 | tf_op jit(solution)/shard_map/ppermute | solution.py:16
  29.7 2.8 %attend.1 = bf16[8,64,256]{2,1,0:T(8,128)(2,1)} custom-call(bf16[2,256,128]{2,1,0:T(8,128)(2,1)} %bitcast.95, bf16[4,128,256]{2,1,0:T(8,128)(2,1)} %copy-done.6, bf16[4,128,256]{2,1,0:T(8,128)(2,1)} %copy-done.14, s32[1,512]{1,0:T(1,128)} %select_n.161.key_ref, s32[256,1]{1,0:T(8,128)} %reshape.276.row_ref), custom_call_target="tpu_custom_call" | custom-call | tf_op jit(solution)/shard_map/attend/pallas_call | solution.py:160
  32.5 5.4 %all-to-all-start = ((bf16[8,64,256]{2,1,0:T(8,128)(2,1)}), bf16[8,64,256]{2,1,0:T(8,128)(2,1)S(1)}, u32[]{:S(2)}, u32[]{:S(2)}) async-start(bf16[8,64,256]{2,1,0:T(8,128)(2,1)} %attend.1), calls=%async_computation | async-start | bytes 524288 | tf_op jit(solution)/shard_map/all_to_all | solution.py:25
  38.3 5.7 %all-to-all-done.message_ref = bf16[8,64,256]{2,1,0:T(8,128)(2,1)S(1)} async-done(((bf16[8,64,256]{2,1,0:T(8,128)(2,1)}), bf16[8,64,256]{2,1,0:T(8,128)(2,1)S(1)}, u32[]{:S(2)}, u32[]{:S(2)}) %all-to-all-start) | async-done | bytes 262176 | tf_op jit(solution)/shard_map/all_to_all | solution.py:25
  46.9 4.0 %collective-permute-start.5 = (bf16[32,256]{1,0:T(8,128)(2,1)}, bf16[32,256]{1,0:T(8,128)(2,1)S(1)}, u32[]{:S(2)}, u32[]{:S(2)}) collective-permute-start(bf16[32,256]{1,0:T(8,128)(2,1)} %combine.1.a_ref), channel_id=1, source_target_pairs={{0,32},{16,48},{32,0},{48,16},{1,33},{17,49},{33,1},{49,17},{2,34}... | collective-permute-start | bytes 49160 | tf_op jit(solution)/shard_map/ppermute | solution.py:21
  50.8 3.1 %collective-permute-start.6 = (bf16[32,256]{1,0:T(8,128)(2,1)}, bf16[32,256]{1,0:T(8,128)(2,1)S(1)}, u32[]{:S(2)}, u32[]{:S(2)}) collective-permute-start(bf16[32,256]{1,0:T(8,128)(2,1)} %combine.1.a_ref), channel_id=1, source_target_pairs={{0,48},{16,0},{32,16},{48,32},{1,49},{17,1},{33,17},{49,33},{2,50}... | collective-permute-start | bytes 49160 | tf_op jit(solution)/shard_map/ppermute | solution.py:21
  56.4 2.4 %project.1 = bf16[8,4,16,320]{3,2,1,0:T(8,128)(2,1)} custom-call(s32[2]{0:T(128)} %pad_add_fusion.at_ref, bf16[32,256]{1,0:T(8,128)(2,1)} %combine.1.a_ref, bf16[32,256]{1,0:T(8,128)(2,1)} %copy-done.15, bf16[32,256]{1,0:T(8,128)(2,1)} %copy-done.16, bf16[32,256]{1,0:T(8,128)(2,1)} %copy-done.17, bf16[8,96,256]{2,1,0:T(8,128)(2,1)} %copy-done.2, ...), custom_call_target="tpu_custom_call" | custom-call | tf_op jit(solution)/shard_map/project/pallas_call | solution.py:168
  58.9 7.1 %all-to-all-start.2 = ((bf16[32,16,320]{2,1,0:T(8,128)(2,1)}), bf16[32,16,320]{2,1,0:T(8,128)(2,1)S(1)}, u32[]{:S(2)}, u32[]{:S(2)}) async-start(bf16[32,16,320]{2,1,0:T(8,128)(2,1)} %bitcast.90), calls=%async_computation.2 | async-start | bytes 786432 | tf_op jit(solution)/shard_map/all_to_all | solution.py:25
  67.6 6.9 %all-to-all-done.2 = bf16[32,16,320]{2,1,0:T(8,128)(2,1)S(1)} async-done(((bf16[32,16,320]{2,1,0:T(8,128)(2,1)}), bf16[32,16,320]{2,1,0:T(8,128)(2,1)S(1)}, u32[]{:S(2)}, u32[]{:S(2)}) %all-to-all-start.2) | async-done | bytes 327712 | tf_op jit(solution)/shard_map/all_to_all | solution.py:25
  75.3 5.7 %all-to-all-start.3 = ((bf16[32,16,320]{2,1,0:T(8,128)(2,1)}), bf16[32,16,320]{2,1,0:T(8,128)(2,1)S(1)}, u32[]{:S(2)}, u32[]{:S(2)}) async-start(bf16[32,16,320]{2,1,0:T(8,128)(2,1)} %broadcast_in_dim.117), calls=%async_computation.3 | async-start | bytes 786432 | tf_op jit(solution)/shard_map/all_to_all | solution.py:25
  81.0 4.0 %collective-permute-start.15 = (bf16[384,1280]{1,0:T(8,128)(2,1)S(1)}, bf16[384,1280]{1,0:T(8,128)(2,1)}, u32[]{:S(2)}, u32[]{:S(2)}) collective-permute-start(bf16[384,1280]{1,0:T(8,128)(2,1)S(1)} %copy-done.1), channel_id=1, source_target_pairs={{0,64},{64,0},{1,65},{65,1},{2,66},{66,2},{3,67},{67,3},{4,68},{68... | collective-permute-start | bytes 2949128 | tf_op jit(solution)/shard_map/ppermute | solution.py:16
  85.0 7.5 %all-to-all-done.3 = bf16[32,16,320]{2,1,0:T(8,128)(2,1)S(1)} async-done(((bf16[32,16,320]{2,1,0:T(8,128)(2,1)}), bf16[32,16,320]{2,1,0:T(8,128)(2,1)S(1)}, u32[]{:S(2)}, u32[]{:S(2)}) %all-to-all-start.3) | async-done | bytes 327712 | tf_op jit(solution)/shard_map/all_to_all | solution.py:25
  97.7 5.7 %collective-permute-start.14 = (f32[384]{0:T(512)S(1)}, f32[384]{0:T(512)S(1)}, u32[]{:S(2)}, u32[]{:S(2)}) collective-permute-start(f32[384]{0:T(512)S(1)} %copy-done.20), channel_id=1, source_target_pairs={{0,64},{64,0},{1,65},{65,1},{2,66},{66,2},{3,67},{67,3},{4,68},{68... | collective-permute-start | bytes 4616 | tf_op jit(solution)/shard_map/ppermute | solution.py:16
  109.3 4.1 %all-to-all-start.4 = ((bf16[32,8,640]{2,1,0:T(8,128)(2,1)}), bf16[32,8,640]{2,1,0:T(8,128)(2,1)S(1)}, u32[]{:S(2)}, u32[]{:S(2)}) async-start(bf16[32,8,640]{2,1,0:T(8,128)(2,1)} %bitcast.91), calls=%async_computation.4 | async-start | bytes 655360 | tf_op jit(solution)/shard_map/all_to_all | solution.py:25
  117.7 6.6 %all-to-all-done.4 = bf16[32,8,640]{2,1,0:T(8,128)(2,1)S(1)} async-done(((bf16[32,8,640]{2,1,0:T(8,128)(2,1)}), bf16[32,8,640]{2,1,0:T(8,128)(2,1)S(1)}, u32[]{:S(2)}, u32[]{:S(2)}) %all-to-all-start.4) | async-done | bytes 327712 | tf_op jit(solution)/shard_map/all_to_all | solution.py:25
  125.8 3.9 %all-to-all-start.5 = ((bf16[32,8,640]{2,1,0:T(8,128)(2,1)}), bf16[32,8,640]{2,1,0:T(8,128)(2,1)S(1)}, u32[]{:S(2)}, u32[]{:S(2)}) async-start(bf16[32,8,640]{2,1,0:T(8,128)(2,1)} %broadcast_in_dim.118), calls=%async_computation.5 | async-start | bytes 655360 | tf_op jit(solution)/shard_map/all_to_all | solution.py:25
  130.6 7.5 %collective-permute-start.8 = (bf16[4,128,320]{1,2,0:T(8,128)(2,1)}, bf16[4,128,320]{1,2,0:T(8,128)(2,1)}, u32[]{:S(2)}, u32[]{:S(2)}) collective-permute-start(bf16[4,128,320]{1,2,0:T(8,128)(2,1)} %copy.62), channel_id=1, source_target_pairs={{0,64},{64,0},{1,65},{65,1},{2,66},{66,2},{3,67},{67,3},{4,68},{68... | collective-permute-start | bytes 983048 | tf_op jit(solution)/shard_map/ppermute | solution.py:16
  138.1 2.6 %all-to-all-done.5 = bf16[32,8,640]{2,1,0:T(8,128)(2,1)S(1)} async-done(((bf16[32,8,640]{2,1,0:T(8,128)(2,1)}), bf16[32,8,640]{2,1,0:T(8,128)(2,1)S(1)}, u32[]{:S(2)}, u32[]{:S(2)}) %all-to-all-start.5) | async-done | bytes 327712 | tf_op jit(solution)/shard_map/all_to_all | solution.py:25
  148.4 10.7 %collective-permute-start.9 = (bf16[64,80]{0,1:T(8,128)(2,1)S(1)}, bf16[64,80]{0,1:T(8,128)(2,1)S(1)}, u32[]{:S(2)}, u32[]{:S(2)}) collective-permute-start(bf16[64,80]{0,1:T(8,128)(2,1)S(1)} %pad_maximum_fusion.6), channel_id=1, source_target_pairs={{0,0},{64,1},{128,2},{192,3},{1,64},{65,65},{129,66},{193,67},{2,1... | collective-permute-start | bytes 30728 | tf_op jit(solution)/shard_map/ppermute | solution.py:199
  159.6 3.3 %collective-permute-start.19 = (bf16[128,384]{1,0:T(8,128)(2,1)S(1)}, bf16[128,384]{1,0:T(8,128)(2,1)S(1)}, u32[]{:S(2)}, u32[]{:S(2)}) collective-permute-start(bf16[128,384]{1,0:T(8,128)(2,1)S(1)} %get-tuple-element.45), channel_id=1, source_target_pairs={{0,64},{64,0},{1,65},{65,1},{2,66},{66,2},{3,67},{67,3},{4,68},{68... | collective-permute-start | bytes 294920 | tf_op jit(solution)/shard_map/ppermute | solution.py:16
  164.9 2.4 %convolution_convert_fusion.1 = bf16[4,320,384]{2,1,0:T(8,128)(2,1)} fusion(bf16[4,128,320]{1,2,0:T(8,128)(2,1)} %collective-permute-done.8, bf16[4,128,320]{1,2,0:T(8,128)(2,1)S(1)} %copy-done.12, bf16[128,384]{1,0:T(8,128)(2,1)S(1)} %collective-permute-done.19, bf16[128,384]{1,0:T(8,128)(2,1)S(1)} %get-tuple-element.44), kind=kOutput, calls=%fused_computation.1 | convolution fusion | flops 253853696 | bytes 1835008 | tf_op jit(solution)/shard_map/zrf,rc->zfc/dot_general | solution.py:240
  (150 shorter events, 50.4 us)
Async XLA Ops:
  2.9 19.9 %collective-permute-start.2 = (bf16[128,256]{1,0:T(8,128)(2,1)S(1)}, bf16[128,256]{1,0:T(8,128)(2,1)S(1)}, u32[]{:S(2)}, u32[]{:S(2)}) collective-permute-start(bf16[128,256]{1,0:T(8,128)(2,1)S(1)} %get-tuple-element.39), channel_id=1, source_target_pairs={{0,48},{16,0},{32,16},{48,32},{1,49},{17,1},{33,17},{49,33},{2,50}... | collective-permute-start | bytes 196616 | tf_op jit(solution)/shard_map/ppermute | solution.py:21
  9.8 13.0 %collective-permute-start.1 = (bf16[128,256]{1,0:T(8,128)(2,1)S(1)}, bf16[128,256]{1,0:T(8,128)(2,1)S(1)}, u32[]{:S(2)}, u32[]{:S(2)}) collective-permute-start(bf16[128,256]{1,0:T(8,128)(2,1)S(1)} %get-tuple-element.40), channel_id=1, source_target_pairs={{0,32},{16,48},{32,0},{48,16},{1,33},{17,49},{33,1},{49,17},{2,34}... | collective-permute-start | bytes 196616 | tf_op jit(solution)/shard_map/ppermute | solution.py:21
  10.8 6.9 %collective-permute-start = (bf16[128,256]{1,0:T(8,128)(2,1)S(1)}, bf16[128,256]{1,0:T(8,128)(2,1)S(1)}, u32[]{:S(2)}, u32[]{:S(2)}) collective-permute-start(bf16[128,256]{1,0:T(8,128)(2,1)S(1)} %get-tuple-element.41), channel_id=1, source_target_pairs={{0,16},{16,32},{32,48},{48,0},{1,17},{17,33},{33,49},{49,1},{2,18}... | collective-permute-start | bytes 196616 | tf_op jit(solution)/shard_map/ppermute | solution.py:21
  17.8 14.7 %all-to-all-start.1 = ((bf16[8,96,256]{2,1,0:T(8,128)(2,1)}), bf16[8,96,256]{2,1,0:T(8,128)(2,1)S(1)}, u32[]{:S(2)}, u32[]{:S(2)}) async-start(bf16[8,96,256]{2,1,0:T(8,128)(2,1)} %fusion.20), calls=%async_computation.1 | async-start | bytes 786432 | tf_op jit(solution)/shard_map/all_to_all | solution.py:25
  32.5 11.6 %all-to-all-start = ((bf16[8,64,256]{2,1,0:T(8,128)(2,1)}), bf16[8,64,256]{2,1,0:T(8,128)(2,1)S(1)}, u32[]{:S(2)}, u32[]{:S(2)}) async-start(bf16[8,64,256]{2,1,0:T(8,128)(2,1)} %attend.1), calls=%async_computation | async-start | bytes 524288 | tf_op jit(solution)/shard_map/all_to_all | solution.py:25
  37.9 16.9 %collective-permute-start.7 = (bf16[8,96,256]{2,1,0:T(8,128)(2,1)S(1)}, bf16[8,96,256]{2,1,0:T(8,128)(2,1)S(1)}, u32[]{:S(2)}, u32[]{:S(2)}) collective-permute-start(bf16[8,96,256]{2,1,0:T(8,128)(2,1)S(1)} %all-to-all-done.1.mine_ref), channel_id=1, source_target_pairs={{0,64},{64,0},{1,65},{65,1},{2,66},{66,2},{3,67},{67,3},{4,68},{68... | collective-permute-start | bytes 1179656 | tf_op jit(solution)/shard_map/ppermute | solution.py:16
  46.5 9.3 %collective-permute-start.4 = (bf16[32,256]{1,0:T(8,128)(2,1)}, bf16[32,256]{1,0:T(8,128)(2,1)S(1)}, u32[]{:S(2)}, u32[]{:S(2)}) collective-permute-start(bf16[32,256]{1,0:T(8,128)(2,1)} %combine.1.a_ref), channel_id=1, source_target_pairs={{0,16},{16,32},{32,48},{48,0},{1,17},{17,33},{33,49},{49,1},{2,18}... | collective-permute-start | bytes 49160 | tf_op jit(solution)/shard_map/ppermute | solution.py:21
  46.9 9.0 %collective-permute-start.5 = (bf16[32,256]{1,0:T(8,128)(2,1)}, bf16[32,256]{1,0:T(8,128)(2,1)S(1)}, u32[]{:S(2)}, u32[]{:S(2)}) collective-permute-start(bf16[32,256]{1,0:T(8,128)(2,1)} %combine.1.a_ref), channel_id=1, source_target_pairs={{0,32},{16,48},{32,0},{48,16},{1,33},{17,49},{33,1},{49,17},{2,34}... | collective-permute-start | bytes 49160 | tf_op jit(solution)/shard_map/ppermute | solution.py:21
  58.9 15.6 %all-to-all-start.2 = ((bf16[32,16,320]{2,1,0:T(8,128)(2,1)}), bf16[32,16,320]{2,1,0:T(8,128)(2,1)S(1)}, u32[]{:S(2)}, u32[]{:S(2)}) async-start(bf16[32,16,320]{2,1,0:T(8,128)(2,1)} %bitcast.90), calls=%async_computation.2 | async-start | bytes 786432 | tf_op jit(solution)/shard_map/all_to_all | solution.py:25
  65.9 19.0 %collective-permute-start.10 = (bf16[1280,384]{1,0:T(8,128)(2,1)}, bf16[1280,384]{1,0:T(8,128)(2,1)}, u32[]{:S(2)}, u32[]{:S(2)}) collective-permute-start(bf16[1280,384]{1,0:T(8,128)(2,1)} %param.18), channel_id=1, source_target_pairs={{0,64},{64,0},{1,65},{65,1},{2,66},{66,2},{3,67},{67,3},{4,68},{68... | collective-permute-start | bytes 2949128 | tf_op jit(solution)/shard_map/ppermute | solution.py:16
  75.3 17.1 %all-to-all-start.3 = ((bf16[32,16,320]{2,1,0:T(8,128)(2,1)}), bf16[32,16,320]{2,1,0:T(8,128)(2,1)S(1)}, u32[]{:S(2)}, u32[]{:S(2)}) async-start(bf16[32,16,320]{2,1,0:T(8,128)(2,1)} %broadcast_in_dim.117), calls=%async_computation.3 | async-start | bytes 786432 | tf_op jit(solution)/shard_map/all_to_all | solution.py:25
  81.0 24.9 %collective-permute-start.15 = (bf16[384,1280]{1,0:T(8,128)(2,1)S(1)}, bf16[384,1280]{1,0:T(8,128)(2,1)}, u32[]{:S(2)}, u32[]{:S(2)}) collective-permute-start(bf16[384,1280]{1,0:T(8,128)(2,1)S(1)} %copy-done.1), channel_id=1, source_target_pairs={{0,64},{64,0},{1,65},{65,1},{2,66},{66,2},{3,67},{67,3},{4,68},{68... | collective-permute-start | bytes 2949128 | tf_op jit(solution)/shard_map/ppermute | solution.py:16
  95.6 8.6 %collective-permute-start.13 = (bf16[128,768]{1,0:T(8,128)(2,1)S(1)}, bf16[128,768]{1,0:T(8,128)(2,1)S(1)}, u32[]{:S(2)}, u32[]{:S(2)}) collective-permute-start(bf16[128,768]{1,0:T(8,128)(2,1)S(1)} %fusion.24), channel_id=1, source_target_pairs={{0,3},{1,0},{2,1},{3,2},{4,7},{5,4},{6,5},{7,6},{8,11},{9,8},{10,9... | collective-permute-start | bytes 589832 | tf_op jit(solution)/shard_map/ppermute | solution.py:21
  96.8 7.4 %collective-permute-start.12 = (bf16[128,768]{1,0:T(8,128)(2,1)S(1)}, bf16[128,768]{1,0:T(8,128)(2,1)S(1)}, u32[]{:S(2)}, u32[]{:S(2)}) collective-permute-start(bf16[128,768]{1,0:T(8,128)(2,1)S(1)} %fusion.24), channel_id=1, source_target_pairs={{0,2},{1,3},{2,0},{3,1},{4,6},{5,7},{6,4},{7,5},{8,10},{9,11},{10,... | collective-permute-start | bytes 589832 | tf_op jit(solution)/shard_map/ppermute | solution.py:21
  97.5 7.4 %collective-permute-start.11 = (bf16[128,768]{1,0:T(8,128)(2,1)S(1)}, bf16[128,768]{1,0:T(8,128)(2,1)S(1)}, u32[]{:S(2)}, u32[]{:S(2)}) collective-permute-start(bf16[128,768]{1,0:T(8,128)(2,1)S(1)} %fusion.24), channel_id=1, source_target_pairs={{0,1},{1,2},{2,3},{3,0},{4,5},{5,6},{6,7},{7,4},{8,9},{9,10},{10,1... | collective-permute-start | bytes 589832 | tf_op jit(solution)/shard_map/ppermute | solution.py:21
  97.7 6.5 %collective-permute-start.14 = (f32[384]{0:T(512)S(1)}, f32[384]{0:T(512)S(1)}, u32[]{:S(2)}, u32[]{:S(2)}) collective-permute-start(f32[384]{0:T(512)S(1)} %copy-done.20), channel_id=1, source_target_pairs={{0,64},{64,0},{1,65},{65,1},{2,66},{66,2},{3,67},{67,3},{4,68},{68... | collective-permute-start | bytes 4616 | tf_op jit(solution)/shard_map/ppermute | solution.py:16
  109.3 15.0 %all-to-all-start.4 = ((bf16[32,8,640]{2,1,0:T(8,128)(2,1)}), bf16[32,8,640]{2,1,0:T(8,128)(2,1)S(1)}, u32[]{:S(2)}, u32[]{:S(2)}) async-start(bf16[32,8,640]{2,1,0:T(8,128)(2,1)} %bitcast.91), calls=%async_computation.4 | async-start | bytes 655360 | tf_op jit(solution)/shard_map/all_to_all | solution.py:25
  125.8 14.9 %all-to-all-start.5 = ((bf16[32,8,640]{2,1,0:T(8,128)(2,1)}), bf16[32,8,640]{2,1,0:T(8,128)(2,1)S(1)}, u32[]{:S(2)}, u32[]{:S(2)}) async-start(bf16[32,8,640]{2,1,0:T(8,128)(2,1)} %broadcast_in_dim.118), calls=%async_computation.5 | async-start | bytes 655360 | tf_op jit(solution)/shard_map/all_to_all | solution.py:25
  130.6 16.9 %collective-permute-start.8 = (bf16[4,128,320]{1,2,0:T(8,128)(2,1)}, bf16[4,128,320]{1,2,0:T(8,128)(2,1)}, u32[]{:S(2)}, u32[]{:S(2)}) collective-permute-start(bf16[4,128,320]{1,2,0:T(8,128)(2,1)} %copy.62), channel_id=1, source_target_pairs={{0,64},{64,0},{1,65},{65,1},{2,66},{66,2},{3,67},{67,3},{4,68},{68... | collective-permute-start | bytes 983048 | tf_op jit(solution)/shard_map/ppermute | solution.py:16
  144.0 15.2 %collective-permute-start.18 = (bf16[128,768]{1,0:T(8,128)(2,1)S(1)}, bf16[128,768]{1,0:T(8,128)(2,1)S(1)}, u32[]{:S(2)}, u32[]{:S(2)}) collective-permute-start(bf16[128,768]{1,0:T(8,128)(2,1)S(1)} %fusion.23), channel_id=1, source_target_pairs={{0,3},{1,0},{2,1},{3,2},{4,7},{5,4},{6,5},{7,6},{8,11},{9,8},{10,9... | collective-permute-start | bytes 589832 | tf_op jit(solution)/shard_map/ppermute | solution.py:21
  146.1 13.1 %collective-permute-start.17 = (bf16[128,768]{1,0:T(8,128)(2,1)S(1)}, bf16[128,768]{1,0:T(8,128)(2,1)S(1)}, u32[]{:S(2)}, u32[]{:S(2)}) collective-permute-start(bf16[128,768]{1,0:T(8,128)(2,1)S(1)} %fusion.23), channel_id=1, source_target_pairs={{0,2},{1,3},{2,0},{3,1},{4,6},{5,7},{6,4},{7,5},{8,10},{9,11},{10,... | collective-permute-start | bytes 589832 | tf_op jit(solution)/shard_map/ppermute | solution.py:21
  147.0 12.2 %collective-permute-start.16 = (bf16[128,768]{1,0:T(8,128)(2,1)S(1)}, bf16[128,768]{1,0:T(8,128)(2,1)S(1)}, u32[]{:S(2)}, u32[]{:S(2)}) collective-permute-start(bf16[128,768]{1,0:T(8,128)(2,1)S(1)} %fusion.23), channel_id=1, source_target_pairs={{0,1},{1,2},{2,3},{3,0},{4,5},{5,6},{6,7},{7,4},{8,9},{9,10},{10,1... | collective-permute-start | bytes 589832 | tf_op jit(solution)/shard_map/ppermute | solution.py:21
  148.4 15.1 %collective-permute-start.9 = (bf16[64,80]{0,1:T(8,128)(2,1)S(1)}, bf16[64,80]{0,1:T(8,128)(2,1)S(1)}, u32[]{:S(2)}, u32[]{:S(2)}) collective-permute-start(bf16[64,80]{0,1:T(8,128)(2,1)S(1)} %pad_maximum_fusion.6), channel_id=1, source_target_pairs={{0,0},{64,1},{128,2},{192,3},{1,64},{65,65},{129,66},{193,67},{2,1... | collective-permute-start | bytes 30728 | tf_op jit(solution)/shard_map/ppermute | solution.py:199
  159.1 8.2 %collective-permute-start.21 = (bf16[2,128,640]{2,1,0:T(8,128)(2,1)S(1)}, bf16[2,128,640]{2,1,0:T(8,128)(2,1)S(1)}, u32[]{:S(2)}, u32[]{:S(2)}) collective-permute-start(bf16[2,128,640]{2,1,0:T(8,128)(2,1)S(1)} %bitcast.86), channel_id=1, source_target_pairs={{0,64},{64,0},{1,65},{65,1},{2,66},{66,2},{3,67},{67,3},{4,68},{68... | collective-permute-start | bytes 983048 | tf_op jit(solution)/shard_map/ppermute | solution.py:16
  (26 other events, 188.6 us)

commit v4 on v3

--- a/solution.py
+++ b/solution.py
@@ -33,7 +33,10 @@
     return lax.dot_general(a, b, (contract, ((), ())), preferred_element_type=F32)
 
 
-def attend(q_ref, kv_ref, other_ref, key_ref, row_ref, out_ref):
+def attend(q_ref, kv_ref, other_ref, key_ref, row_ref, proj_ref, out_ref):
+    rest = proj_ref.shape[1]
+    few = out_ref.shape[1] - rest
+    out_ref[:, few:] = proj_ref[...]
     slots = kv_ref.shape[1] // 2
     visible = key_ref[...] <= row_ref[...]
     lane = lax.broadcasted_iota(jnp.int32, (q_ref.shape[1], HD), 1)
@@ -57,16 +60,16 @@
         extra = jnp.where(lane == 0, high, jnp.where(lane == 1, mid, jnp.where(lane == 2, low, 0.0)))
         parts = out_ref.shape[0] // q_ref.shape[0]
         where = slice(k * parts, (k + 1) * parts)
-        out_ref[where, :, :HD] = (weighted / safe).astype(BF16).reshape(parts, -1, HD)
-        out_ref[where, :, HD:] = extra.astype(BF16).reshape(parts, -1, HD)
+        out_ref[where, :few, :HD] = (weighted / safe).astype(BF16).reshape(parts, -1, HD)
+        out_ref[where, :few, HD:] = extra.astype(BF16).reshape(parts, -1, HD)
 
 
 def combine(message_ref, out_ref):
-    message = message_ref[...].astype(F32)
+    half = out_ref.shape[0]
+    message = message_ref[:, : 2 * half].astype(F32)
     level = jnp.sum(message[:, :, HD:], axis=2, keepdims=True)
     share = jnp.exp(level - jnp.max(level, axis=0, keepdims=True))
     attention = jnp.sum(message[:, :, :HD] * share, axis=0) / jnp.sum(share, axis=0)
-    half = attention.shape[0] // 2
     out_ref[:, :HD] = attention[:half].astype(BF16)
     out_ref[:, HD:] = attention[half:].astype(BF16)
 
@@ -77,7 +80,8 @@
     turn, core = (at_ref[0], at_ref[1])
     for high in range(2):
         for ref, res, low in ((mine_ref, res_mine_ref, core), (other_ref, res_other_ref, 1 - core)):
-            weight = jnp.concatenate([ref[4 * high + j, :cols] for j in range(4)])
+            top = ref.shape[1] - other_ref.shape[1]
+            weight = jnp.concatenate([ref[4 * high + j, top : top + cols] for j in range(4)])
             out = dot(attention, weight, ((1,), (1,))) + res[high].astype(F32)
             out = out.astype(BF16)
             for k in range(4):
@@ -122,24 +126,9 @@
     proj = out_weight.reshape(8, 2 * HD, cols).transpose(0, 2, 1)
     res = jnp.pad(resid.reshape(8, 8, cols), ((0, 0), (0, 8), (0, 2 * HD - cols)))
     proj = jnp.concatenate([proj, res], axis=1)
-    ring[1], proj = lax.optimization_barrier((ring[1], proj))
-    proj_mine = exchanged(proj, (ZL, Y))
     kv = jnp.stack(ring)
     kv_other = other_core(kv)
-    proj_other = other_core(proj_mine)
-    at = zl * 4 + y
     turn = (zh - jnp.arange(4)) % 4
-
-    def residual(proj):
-        res = proj[:, cols : cols + 8, :cols].reshape(2, 4, 8, cols)
-        res = res.transpose(0, 2, 1, 3).reshape(2, 1, 1, 8, 4 * cols)
-        here = (jnp.arange(4) == at % 4) & (turn == x)[:, None] & (co == at // 4)
-        return jnp.where(here[None, :, :, None, None], res, 0).reshape(2, seqs * half, 4 * cols)
-
-    res_mine, res_other = (residual(proj_mine), residual(proj_other))
-    enc_other = other_core(enc_weight)
-    dec_other = other_core(dec_weight)
-    bias_both = jnp.concatenate([enc_bias, other_core(enc_bias)])
 
     first = 2 * half * zh + half * co
     q = lax.dynamic_slice_in_dim(query, first, half, 0)
@@ -158,9 +147,22 @@
     row_pos = jnp.broadcast_to(row_pos[None, :], (group, half)).reshape(-1, 1)
 
     message = pl.pallas_call(
-        attend, out_shape=jax.ShapeDtypeStruct((8, 2 * half, 2 * HD), BF16), name="attend"
-    )(q, kv, kv_other, key_pos.reshape(1, -1), row_pos)
+        attend,
+        out_shape=jax.ShapeDtypeStruct((8, 2 * half + proj.shape[1], 2 * HD), BF16),
+        name="attend",
+    )(q, kv, kv_other, key_pos.reshape(1, -1), row_pos, proj)
     message = exchanged(message, (ZL, Y))
+    proj_mine = message[:, 2 * half :]
+    proj_other = other_core(proj_mine)
+    at = zl * 4 + y
+
+    def residual(proj):
+        res = proj[:, cols : cols + 8, :cols].reshape(2, 4, 8, cols)
+        res = res.transpose(0, 2, 1, 3).reshape(2, 1, 1, 8, 4 * cols)
+        here = (jnp.arange(4) == at % 4) & (turn == x)[:, None] & (co == at // 4)
+        return jnp.where(here[None, :, :, None, None], res, 0).reshape(2, seqs * half, 4 * cols)
+
+    res_mine, res_other = (residual(proj_mine), residual(proj_other))
     attention = pl.pallas_call(
         combine, out_shape=jax.ShapeDtypeStruct((half, 2 * HD), BF16), name="combine"
     )(message)
@@ -171,7 +173,13 @@
         in_specs=[pl.BlockSpec(memory_space=pltpu.SMEM)]
         + [pl.BlockSpec(memory_space=pltpu.VMEM)] * 8,
         name="project",
-    )(jnp.stack([zh, co]), *ring, proj_mine, proj_other, res_mine, res_other)
+    )(jnp.stack([zh, co]), *ring, message, proj_other, res_mine, res_other)
+    part, enc_ready, dec_ready, bias_ready = lax.optimization_barrier(
+        (part, enc_weight, dec_weight, enc_bias)
+    )
+    enc_other = other_core(enc_ready)
+    dec_other = other_core(dec_ready)
+    bias_other = other_core(bias_ready)
     part = exchanged(part.reshape(32, half // 2, 4 * cols), (ZL, Y, X))
     piece = jnp.sum(part.astype(F32), axis=0).astype(BF16)
 
@@ -179,6 +187,8 @@
     wide = feats // 2
     few = my_rows // 16
     block = gathered(piece, (ZH, ZL, Y)).reshape(4, my_rows, 4 * cols)
+    block, enc_other, bias_other = lax.optimization_barrier((block, enc_other, bias_other))
+    bias_both = jnp.concatenate([enc_bias, bias_other])
 
     def encoded(weight):
         return jnp.einsum(
@@ -190,11 +200,11 @@
     preact = part + sum(shifted(low, X, k).astype(F32) for k in (1, 2, 3)) + bias_both
     latents = (jax.nn.softplus(4.0 * preact) * 0.25).astype(BF16)
 
-    block_other = other_core(block)
+    natural = block.transpose(1, 0, 2).reshape(my_rows, feats)
+    natural_other = other_core(natural)
     latents_other = other_core(latents[:, lat:])
-    halves = [lax.dynamic_index_in_dim(b, zh, 0, keepdims=False) for b in (block, block_other)]
-    spot = (half * (2 * zl + co), cols * y)
-    halves = [lax.dynamic_slice(b, spot, (half, cols)) for b in halves]
+    spot = (half * (2 * zl + co), 4 * cols * zh + cols * y)
+    halves = [lax.dynamic_slice(b, spot, (half, cols)) for b in (natural, natural_other)]
     halves = [jnp.where(co == 0, halves[0], halves[1]), jnp.where(co == 0, halves[1], halves[0])]
     layer_out = lax.ppermute(
         jnp.concatenate(halves, axis=0),
@@ -211,11 +221,18 @@
     recon = jnp.stack([decoded(0), decoded(1)]).astype(BF16).reshape(32, few, wide)
     recon = jnp.sum(exchanged(recon, (ZL, ZH, Y)).astype(F32), axis=0)
     at = (zl * 4 + zh) * 4 + y
-    natural = block.transpose(1, 0, 2).reshape(my_rows, feats)
     target = lax.dynamic_slice(natural, (few * (at % 16), wide * (at // 16)), (few, wide))
     target_bias = lax.dynamic_slice_in_dim(dec_bias, wide * (at // 16), wide, 0)
     error = ((recon + target_bias - target.astype(F32)) * rows ** (-0.5)).astype(BF16)
+    error, natural_other, latents_other = lax.optimization_barrier(
+        (error, natural_other, latents_other)
+    )
     error = gathered(error, (ZL, ZH, Y)).reshape(2, my_rows, wide)
+    all_natural = jnp.concatenate([natural, natural_other], axis=0).T
+    all_latents = jnp.concatenate([latents[:, :lat], latents_other], axis=0).T
+    error, layer_out, all_natural, all_latents = lax.optimization_barrier(
+        (error, layer_out, all_natural, all_latents)
+    )
     error_other = other_core(error)
 
     def pulled(weight):
@@ -230,15 +247,12 @@
     preact_grad_other = other_core(preact_grad[:, lat:])
     preact_grad = preact_grad[:, :lat]
 
-    all_latents = jnp.concatenate([latents[:, :lat], latents_other], axis=0)
     all_error = jnp.concatenate([error, error_other], axis=1)
     all_error = all_error.transpose(1, 0, 2).reshape(rows, feats)
-    dec_grad = dot(all_latents, all_error, ((0,), (0,))).astype(BF16)
+    dec_grad = dot(all_latents, all_error, ((1,), (0,))).astype(BF16)
     dec_bias_grad = jnp.sum(all_error, axis=0, dtype=F32)
     all_grad = jnp.concatenate([preact_grad, preact_grad_other], axis=0)
-    all_block = jnp.concatenate([block, block_other], axis=1)
-    enc_grad = jnp.einsum("zrf,rc->zfc", all_block, all_grad, preferred_element_type=F32)
-    enc_grad = enc_grad.astype(BF16).reshape(feats, lat)
+    enc_grad = dot(all_natural, all_grad, ((1,), (0,))).astype(BF16)
     enc_bias_grad = jnp.sum(all_grad, axis=0, dtype=F32)
     return (layer_out, enc_grad, enc_bias_grad, dec_grad, dec_bias_grad)
 

time: 172 us -> 167 us (0.971)
  starting transfers between devices: 90.3 us -> 77.1 us
  waiting for transfers between devices: 34.5 us -> 46.2 us
  matrix products: 13.2 us -> 8.23 us
  other arithmetic: 6.9 us -> 10.1 us
  local copies, waits for them, and re-layouts: 18 us -> 15.3 us
    ppermute x12, waiting for transfers between devices: 4.44 us -> 16.8 us  [shifted(): return lax.ppermute(a, axis, [(i, (i + k) % n) for i in range(n)])]
    ppermute x1, starting transfers between devices: 10.7 us -> 3.43 us  [body(): lax.ppermute(jnp.concatenate(halves, axis=0), (ZL, CO, X), [(b * 4 + a, a...]
    ppermute x9, starting transfers between devices: 26.1 us -> 22.3 us  [other_core(): return lax.ppermute(a, CO, [(0, 1), (1, 0)])]
    transpose x0 -> x2, other arithmetic: none -> 2.89 us  [the longest x1 1.98 us: body(): all_natural = jnp.concatenate([natural, natural_other], axis=0).T]
    dot_general x9 -> x10, matrix products: 7.76 us -> 5.08 us  [dot(): lax.dot_general(a, b, (contract, ((), ())), preferred_element_type=F32)]
    dot_general x1 -> x0, matrix products: 2.42 us -> none  [body(): jnp.einsum('zrf,rc->zfc', all_block, all_grad, preferred_element_type=F32)]
    unnamed x47 -> x61, local copies, waits for them, and re-layouts: 5.24 us -> 3 us
    ppermute x12, starting transfers between devices: 23.2 us -> 21.4 us  [shifted(): return lax.ppermute(a, axis, [(i, (i + k) % n) for i in range(n)])]
  transfers between devices with their start and end apart: 28 -> 27, of which waited for: 8 -> 14; matrix products, arithmetic and copies ran while one was open for 15% -> 14% of each run, Pallas kernels for 3% -> 1%
where the time goes in v4:
time: 167 us; the launch traced here: 166 us
  starting transfers between devices  77.1 us (46%)
  waiting for transfers between devices  46.2 us (28%)
  local copies, waits for them, and re-layouts  15.3 us (9%)
  other arithmetic  10.1 us (6%)
  matrix products  8.23 us (5%)
  Pallas kernels  7.48 us (4%)
    all_to_all x5, starting transfers between devices, exchanged(): return lax.all_to_all(a, axes, 0, 0, tiled=True)  30 us
    all_to_all x5, waiting for transfers between devices, exchanged(): return lax.all_to_all(a, axes, 0, 0, tiled=True)  28.6 us
    ppermute x9, starting transfers between devices, other_core(): return lax.ppermute(a, CO, [(0, 1), (1, 0)])  22.3 us
    ppermute x12, starting transfers between devices, shifted(): return lax.ppermute(a, axis, [(i, (i + k) % n) for i in range(n)])  21.4 us
    ppermute x12, waiting for transfers between devices, shifted(): return lax.ppermute(a, axis, [(i, (i + k) % n) for i in range(n)])  16.8 us
    dot_general x10, matrix products, dot(): lax.dot_general(a, b, (contract, ((), ())), preferred_element_type=F32)  5.08 us
    ppermute x1, starting transfers between devices, body(): lax.ppermute(jnp.concatenate(halves, axis=0), (ZL, CO, X), [(b * 4 + a, a...  3.43 us
  transfers between devices with their start and end apart: 27, of which 14 were waited for; matrix products, arithmetic and copies ran while one was open for 14% of the time, Pallas kernels for 1%

profile of v4, /device:TPU:1, one launch (start us, length us, event | category | flops | bytes accessed | tf_op | source)
XLA Modules:
  0.0 165.7 jit_solution(3396401220049185181)
XLA Ops:
  2.9 6.9 %collective-permute-start.2 = (bf16[128,256]{1,0:T(8,128)(2,1)S(1)}, bf16[128,256]{1,0:T(8,128)(2,1)S(1)}, u32[]{:S(2)}, u32[]{:S(2)}) collective-permute-start(bf16[128,256]{1,0:T(8,128)(2,1)S(1)} %get-tuple-element.58), channel_id=1, source_target_pairs={{0,48},{16,0},{32,16},{48,32},{1,49},{17,1},{33,17},{49,33},{2,50}... | collective-permute-start | bytes 196616 | tf_op jit(solution)/shard_map/ppermute | solution.py:21
  10.8 2.3 %collective-permute-start = (bf16[128,256]{1,0:T(8,128)(2,1)S(1)}, bf16[128,256]{1,0:T(8,128)(2,1)S(1)}, u32[]{:S(2)}, u32[]{:S(2)}) collective-permute-start(bf16[128,256]{1,0:T(8,128)(2,1)S(1)} %get-tuple-element.60), channel_id=1, source_target_pairs={{0,16},{16,32},{32,48},{48,0},{1,17},{17,33},{33,49},{49,1},{2,18}... | collective-permute-start | bytes 196616 | tf_op jit(solution)/shard_map/ppermute | solution.py:21
  15.0 2.1 %collective-permute-done.1 = bf16[128,256]{1,0:T(8,128)(2,1)S(1)} collective-permute-done((bf16[128,256]{1,0:T(8,128)(2,1)S(1)}, bf16[128,256]{1,0:T(8,128)(2,1)S(1)}, u32[]{:S(2)}, u32[]{:S(2)}) %collective-permute-start.1) | collective-permute-done | bytes 65568 | tf_op jit(solution)/shard_map/ppermute | solution.py:21
  17.8 2.7 %collective-permute-start.3 = (bf16[4,128,256]{2,1,0:T(8,128)(2,1)S(1)}, bf16[4,128,256]{2,1,0:T(8,128)(2,1)S(1)}, u32[]{:S(2)}, u32[]{:S(2)}) collective-permute-start(bf16[4,128,256]{2,1,0:T(8,128)(2,1)S(1)} %pad_maximum_fusion.3.kv_ref), channel_id=1, source_target_pairs={{0,64},{64,0},{1,65},{65,1},{2,66},{66,2},{3,67},{67,3},{4,68},{68... | collective-permute-start | bytes 786440 | tf_op jit(solution)/shard_map/ppermute | solution.py:16
  23.7 3.1 %attend.1 = bf16[8,160,256]{2,1,0:T(8,128)(2,1)} custom-call(bf16[2,256,128]{2,1,0:T(8,128)(2,1)} %bitcast.99, bf16[4,128,256]{2,1,0:T(8,128)(2,1)} %copy-done.9, bf16[4,128,256]{2,1,0:T(8,128)(2,1)} %copy-done.19, s32[1,512]{1,0:T(1,128)} %select_n.145.key_ref, s32[256,1]{1,0:T(8,128)} %reshape.261.row_ref, bf16[8,96,256]{2,1,0:T(8,128)(2,1)} %fusion.17.proj_ref), custom_call_target="tpu_custom_call" | custom-call | tf_op jit(solution)/shard_map/attend/pallas_call | solution.py:149
  26.7 4.8 %all-to-all-start = ((bf16[8,160,256]{2,1,0:T(8,128)(2,1)}), bf16[8,160,256]{2,1,0:T(8,128)(2,1)S(1)}, u32[]{:S(2)}, u32[]{:S(2)}) async-start(bf16[8,160,256]{2,1,0:T(8,128)(2,1)} %attend.1), calls=%async_computation | async-start | bytes 1310720 | tf_op jit(solution)/shard_map/all_to_all | solution.py:25
  31.5 10.5 %all-to-all-done.message_ref.mine_ref = bf16[8,160,256]{2,1,0:T(8,128)(2,1)S(1)} async-done(((bf16[8,160,256]{2,1,0:T(8,128)(2,1)}), bf16[8,160,256]{2,1,0:T(8,128)(2,1)S(1)}, u32[]{:S(2)}, u32[]{:S(2)}) %all-to-all-start) | async-done | bytes 655392 | tf_op jit(solution)/shard_map/all_to_all | solution.py:25
  45.6 4.0 %collective-permute-start.5 = (bf16[32,256]{1,0:T(8,128)(2,1)}, bf16[32,256]{1,0:T(8,128)(2,1)S(1)}, u32[]{:S(2)}, u32[]{:S(2)}) collective-permute-start(bf16[32,256]{1,0:T(8,128)(2,1)} %combine.1.a_ref), channel_id=1, source_target_pairs={{0,32},{16,48},{32,0},{48,16},{1,33},{17,49},{33,1},{49,17},{2,34}... | collective-permute-start | bytes 49160 | tf_op jit(solution)/shard_map/ppermute | solution.py:21
  49.5 3.1 %collective-permute-start.6 = (bf16[32,256]{1,0:T(8,128)(2,1)}, bf16[32,256]{1,0:T(8,128)(2,1)S(1)}, u32[]{:S(2)}, u32[]{:S(2)}) collective-permute-start(bf16[32,256]{1,0:T(8,128)(2,1)} %combine.1.a_ref), channel_id=1, source_target_pairs={{0,48},{16,0},{32,16},{48,32},{1,49},{17,1},{33,17},{49,33},{2,50}... | collective-permute-start | bytes 49160 | tf_op jit(solution)/shard_map/ppermute | solution.py:21
  55.8 2.5 %project.1 = bf16[8,4,16,320]{3,2,1,0:T(8,128)(2,1)} custom-call(s32[2]{0:T(128)} %pad_add_fusion.at_ref, bf16[32,256]{1,0:T(8,128)(2,1)} %combine.1.a_ref, bf16[32,256]{1,0:T(8,128)(2,1)} %copy-done.22, bf16[32,256]{1,0:T(8,128)(2,1)} %copy-done.23, bf16[32,256]{1,0:T(8,128)(2,1)} %copy-done.24, bf16[8,160,256]{2,1,0:T(8,128)(2,1)} %copy-done.1, ...), custom_call_target="tpu_custom_call" | custom-call | tf_op jit(solution)/shard_map/project/pallas_call | solution.py:170
  58.3 6.5 %all-to-all-start.1 = ((bf16[32,16,320]{2,1,0:T(8,128)(2,1)}), bf16[32,16,320]{2,1,0:T(8,128)(2,1)S(1)}, u32[]{:S(2)}, u32[]{:S(2)}) async-start(bf16[32,16,320]{2,1,0:T(8,128)(2,1)} %bitcast.96), calls=%async_computation.1 | async-start | bytes 786432 | tf_op jit(solution)/shard_map/all_to_all | solution.py:25
  66.5 6.9 %all-to-all-done.1 = bf16[32,16,320]{2,1,0:T(8,128)(2,1)S(1)} async-done(((bf16[32,16,320]{2,1,0:T(8,128)(2,1)}), bf16[32,16,320]{2,1,0:T(8,128)(2,1)S(1)}, u32[]{:S(2)}, u32[]{:S(2)}) %all-to-all-start.1) | async-done | bytes 327712 | tf_op jit(solution)/shard_map/all_to_all | solution.py:25
  74.2 5.0 %all-to-all-start.2 = ((bf16[32,16,320]{2,1,0:T(8,128)(2,1)}), bf16[32,16,320]{2,1,0:T(8,128)(2,1)S(1)}, u32[]{:S(2)}, u32[]{:S(2)}) async-start(bf16[32,16,320]{2,1,0:T(8,128)(2,1)} %broadcast_in_dim.117), calls=%async_computation.2 | async-start | bytes 786432 | tf_op jit(solution)/shard_map/all_to_all | solution.py:25
  79.2 4.0 %collective-permute-start.9 = (f32[384]{0:T(512)S(1)}, f32[384]{0:T(512)S(1)}, u32[]{:S(2)}, u32[]{:S(2)}) collective-permute-start(f32[384]{0:T(512)S(1)} %copy-done.27), channel_id=1, source_target_pairs={{0,64},{64,0},{1,65},{65,1},{2,66},{66,2},{3,67},{67,3},{4,68},{68... | collective-permute-start | bytes 4616 | tf_op jit(solution)/shard_map/ppermute | solution.py:16
  84.0 6.7 %all-to-all-done.2 = bf16[32,16,320]{2,1,0:T(8,128)(2,1)S(1)} async-done(((bf16[32,16,320]{2,1,0:T(8,128)(2,1)}), bf16[32,16,320]{2,1,0:T(8,128)(2,1)S(1)}, u32[]{:S(2)}, u32[]{:S(2)}) %all-to-all-start.2) | async-done | bytes 327712 | tf_op jit(solution)/shard_map/all_to_all | solution.py:25
  96.0 2.5 %collective-permute-done.12 = bf16[128,768]{1,0:T(8,128)(2,1)S(1)} collective-permute-done((bf16[128,768]{1,0:T(8,128)(2,1)S(1)}, bf16[128,768]{1,0:T(8,128)(2,1)S(1)}, u32[]{:S(2)}, u32[]{:S(2)}) %collective-permute-start.12) | collective-permute-done | bytes 196640 | tf_op jit(solution)/shard_map/ppermute | solution.py:21
  98.5 2.8 %collective-permute-done.11 = bf16[128,768]{1,0:T(8,128)(2,1)S(1)} collective-permute-done((bf16[128,768]{1,0:T(8,128)(2,1)S(1)}, bf16[128,768]{1,0:T(8,128)(2,1)S(1)}, u32[]{:S(2)}, u32[]{:S(2)}) %collective-permute-start.11) | collective-permute-done | bytes 196640 | tf_op jit(solution)/shard_map/ppermute | solution.py:21
  105.5 4.6 %all-to-all-start.3 = ((bf16[32,8,640]{2,1,0:T(8,128)(2,1)}), bf16[32,8,640]{2,1,0:T(8,128)(2,1)}, u32[]{:S(2)}, u32[]{:S(2)}) async-start(bf16[32,8,640]{2,1,0:T(8,128)(2,1)} %bitcast.97), calls=%async_computation.3 | async-start | bytes 655360 | tf_op jit(solution)/shard_map/all_to_all | solution.py:25
  111.1 6.5 %collective-permute-start.14 = (bf16[128,1280]{0,1:T(8,128)(2,1)}, bf16[128,1280]{0,1:T(8,128)(2,1)S(1)}, u32[]{:S(2)}, u32[]{:S(2)}) collective-permute-start(bf16[128,1280]{0,1:T(8,128)(2,1)} %bitcast.92), channel_id=1, source_target_pairs={{0,64},{64,0},{1,65},{65,1},{2,66},{66,2},{3,67},{67,3},{4,68},{68... | collective-permute-start | bytes 983048 | tf_op jit(solution)/shard_map/ppermute | solution.py:16
  123.0 9.1 %all-to-all-start.4 = ((bf16[32,8,640]{2,1,0:T(8,128)(2,1)}), bf16[32,8,640]{2,1,0:T(8,128)(2,1)S(1)}, u32[]{:S(2)}, u32[]{:S(2)}) async-start(bf16[32,8,640]{2,1,0:T(8,128)(2,1)} %broadcast_in_dim.118), calls=%async_computation.4 | async-start | bytes 655360 | tf_op jit(solution)/shard_map/all_to_all | solution.py:25
  133.1 3.4 %collective-permute-start.16 = (bf16[64,80]{0,1:T(8,128)(2,1)S(1)}, bf16[64,80]{0,1:T(8,128)(2,1)}, u32[]{:S(2)}, u32[]{:S(2)}) collective-permute-start(bf16[64,80]{0,1:T(8,128)(2,1)S(1)} %pad_maximum_fusion.6), channel_id=1, source_target_pairs={{0,0},{64,1},{128,2},{192,3},{1,64},{65,65},{129,66},{193,67},{2,1... | collective-permute-start | bytes 30728 | tf_op jit(solution)/shard_map/ppermute | solution.py:209
  139.5 3.9 %all-to-all-done.4 = bf16[32,8,640]{2,1,0:T(8,128)(2,1)S(1)} async-done(((bf16[32,8,640]{2,1,0:T(8,128)(2,1)}), bf16[32,8,640]{2,1,0:T(8,128)(2,1)S(1)}, u32[]{:S(2)}, u32[]{:S(2)}) %all-to-all-start.4) | async-done | bytes 327712 | tf_op jit(solution)/shard_map/all_to_all | solution.py:25
  146.4 2.9 %collective-permute-done.19 = bf16[128,768]{1,0:T(8,128)(2,1)S(1)} collective-permute-done((bf16[128,768]{1,0:T(8,128)(2,1)S(1)}, bf16[128,768]{1,0:T(8,128)(2,1)S(1)}, u32[]{:S(2)}, u32[]{:S(2)}) %collective-permute-start.19) | collective-permute-done | bytes 196640 | tf_op jit(solution)/shard_map/ppermute | solution.py:21
  153.5 6.2 %collective-permute-start.20 = (bf16[128,384]{1,0:T(8,128)(2,1)S(1)}, bf16[128,384]{1,0:T(8,128)(2,1)S(1)}, u32[]{:S(2)}, u32[]{:S(2)}) collective-permute-start(bf16[128,384]{1,0:T(8,128)(2,1)S(1)} %get-tuple-element.62), channel_id=1, source_target_pairs={{0,64},{64,0},{1,65},{65,1},{2,66},{66,2},{3,67},{67,3},{4,68},{68... | collective-permute-start | bytes 294920 | tf_op jit(solution)/shard_map/ppermute | solution.py:16
  (164 shorter events, 51.7 us)
Async XLA Ops:
  2.9 12.1 %collective-permute-start.2 = (bf16[128,256]{1,0:T(8,128)(2,1)S(1)}, bf16[128,256]{1,0:T(8,128)(2,1)S(1)}, u32[]{:S(2)}, u32[]{:S(2)}) collective-permute-start(bf16[128,256]{1,0:T(8,128)(2,1)S(1)} %get-tuple-element.58), channel_id=1, source_target_pairs={{0,48},{16,0},{32,16},{48,32},{1,49},{17,1},{33,17},{49,33},{2,50}... | collective-permute-start | bytes 196616 | tf_op jit(solution)/shard_map/ppermute | solution.py:21
  9.8 7.2 %collective-permute-start.1 = (bf16[128,256]{1,0:T(8,128)(2,1)S(1)}, bf16[128,256]{1,0:T(8,128)(2,1)S(1)}, u32[]{:S(2)}, u32[]{:S(2)}) collective-permute-start(bf16[128,256]{1,0:T(8,128)(2,1)S(1)} %get-tuple-element.59), channel_id=1, source_target_pairs={{0,32},{16,48},{32,0},{48,16},{1,33},{17,49},{33,1},{49,17},{2,34}... | collective-permute-start | bytes 196616 | tf_op jit(solution)/shard_map/ppermute | solution.py:21
  10.8 6.9 %collective-permute-start = (bf16[128,256]{1,0:T(8,128)(2,1)S(1)}, bf16[128,256]{1,0:T(8,128)(2,1)S(1)}, u32[]{:S(2)}, u32[]{:S(2)}) collective-permute-start(bf16[128,256]{1,0:T(8,128)(2,1)S(1)} %get-tuple-element.60), channel_id=1, source_target_pairs={{0,16},{16,32},{32,48},{48,0},{1,17},{17,33},{33,49},{49,1},{2,18}... | collective-permute-start | bytes 196616 | tf_op jit(solution)/shard_map/ppermute | solution.py:21
  17.8 5.1 %collective-permute-start.3 = (bf16[4,128,256]{2,1,0:T(8,128)(2,1)S(1)}, bf16[4,128,256]{2,1,0:T(8,128)(2,1)S(1)}, u32[]{:S(2)}, u32[]{:S(2)}) collective-permute-start(bf16[4,128,256]{2,1,0:T(8,128)(2,1)S(1)} %pad_maximum_fusion.3.kv_ref), channel_id=1, source_target_pairs={{0,64},{64,0},{1,65},{65,1},{2,66},{66,2},{3,67},{67,3},{4,68},{68... | collective-permute-start | bytes 786440 | tf_op jit(solution)/shard_map/ppermute | solution.py:16
  26.7 15.3 %all-to-all-start = ((bf16[8,160,256]{2,1,0:T(8,128)(2,1)}), bf16[8,160,256]{2,1,0:T(8,128)(2,1)S(1)}, u32[]{:S(2)}, u32[]{:S(2)}) async-start(bf16[8,160,256]{2,1,0:T(8,128)(2,1)} %attend.1), calls=%async_computation | async-start | bytes 1310720 | tf_op jit(solution)/shard_map/all_to_all | solution.py:25
  42.1 12.1 %collective-permute-start.7 = (bf16[8,96,256]{2,1,0:T(8,128)(2,1)S(1)}, bf16[8,96,256]{2,1,0:T(8,128)(2,1)S(1)}, u32[]{:S(2)}, u32[]{:S(2)}) collective-permute-start(bf16[8,96,256]{2,1,0:T(8,128)(2,1)S(1)} %slice.63), channel_id=1, source_target_pairs={{0,64},{64,0},{1,65},{65,1},{2,66},{66,2},{3,67},{67,3},{4,68},{68... | collective-permute-start | bytes 1179656 | tf_op jit(solution)/shard_map/ppermute | solution.py:16
  45.2 10.0 %collective-permute-start.4 = (bf16[32,256]{1,0:T(8,128)(2,1)}, bf16[32,256]{1,0:T(8,128)(2,1)S(1)}, u32[]{:S(2)}, u32[]{:S(2)}) collective-permute-start(bf16[32,256]{1,0:T(8,128)(2,1)} %combine.1.a_ref), channel_id=1, source_target_pairs={{0,16},{16,32},{32,48},{48,0},{1,17},{17,33},{33,49},{49,1},{2,18}... | collective-permute-start | bytes 49160 | tf_op jit(solution)/shard_map/ppermute | solution.py:21
  45.6 9.7 %collective-permute-start.5 = (bf16[32,256]{1,0:T(8,128)(2,1)}, bf16[32,256]{1,0:T(8,128)(2,1)S(1)}, u32[]{:S(2)}, u32[]{:S(2)}) collective-permute-start(bf16[32,256]{1,0:T(8,128)(2,1)} %combine.1.a_ref), channel_id=1, source_target_pairs={{0,32},{16,48},{32,0},{48,16},{1,33},{17,49},{33,1},{49,17},{2,34}... | collective-permute-start | bytes 49160 | tf_op jit(solution)/shard_map/ppermute | solution.py:21
  49.5 5.7 %collective-permute-start.6 = (bf16[32,256]{1,0:T(8,128)(2,1)}, bf16[32,256]{1,0:T(8,128)(2,1)S(1)}, u32[]{:S(2)}, u32[]{:S(2)}) collective-permute-start(bf16[32,256]{1,0:T(8,128)(2,1)} %combine.1.a_ref), channel_id=1, source_target_pairs={{0,48},{16,0},{32,16},{48,32},{1,49},{17,1},{33,17},{49,33},{2,50}... | collective-permute-start | bytes 49160 | tf_op jit(solution)/shard_map/ppermute | solution.py:21
  58.3 15.0 %all-to-all-start.1 = ((bf16[32,16,320]{2,1,0:T(8,128)(2,1)}), bf16[32,16,320]{2,1,0:T(8,128)(2,1)S(1)}, u32[]{:S(2)}, u32[]{:S(2)}) async-start(bf16[32,16,320]{2,1,0:T(8,128)(2,1)} %bitcast.96), calls=%async_computation.1 | async-start | bytes 786432 | tf_op jit(solution)/shard_map/all_to_all | solution.py:25
  64.8 19.2 %collective-permute-start.8 = (bf16[1280,384]{1,0:T(8,128)(2,1)}, bf16[1280,384]{1,0:T(8,128)(2,1)}, u32[]{:S(2)}, u32[]{:S(2)}) collective-permute-start(bf16[1280,384]{1,0:T(8,128)(2,1)} %param.18), channel_id=1, source_target_pairs={{0,64},{64,0},{1,65},{65,1},{2,66},{66,2},{3,67},{67,3},{4,68},{68... | collective-permute-start | bytes 2949128 | tf_op jit(solution)/shard_map/ppermute | solution.py:16
  74.2 16.4 %all-to-all-start.2 = ((bf16[32,16,320]{2,1,0:T(8,128)(2,1)}), bf16[32,16,320]{2,1,0:T(8,128)(2,1)S(1)}, u32[]{:S(2)}, u32[]{:S(2)}) async-start(bf16[32,16,320]{2,1,0:T(8,128)(2,1)} %broadcast_in_dim.117), calls=%async_computation.2 | async-start | bytes 786432 | tf_op jit(solution)/shard_map/all_to_all | solution.py:25
  79.2 4.8 %collective-permute-start.9 = (f32[384]{0:T(512)S(1)}, f32[384]{0:T(512)S(1)}, u32[]{:S(2)}, u32[]{:S(2)}) collective-permute-start(f32[384]{0:T(512)S(1)} %copy-done.27), channel_id=1, source_target_pairs={{0,64},{64,0},{1,65},{65,1},{2,66},{66,2},{3,67},{67,3},{4,68},{68... | collective-permute-start | bytes 4616 | tf_op jit(solution)/shard_map/ppermute | solution.py:16
  83.2 21.0 %collective-permute-start.13 = (bf16[384,1280]{1,0:T(8,128)(2,1)S(1)}, bf16[384,1280]{1,0:T(8,128)(2,1)S(1)}, u32[]{:S(2)}, u32[]{:S(2)}) collective-permute-start(bf16[384,1280]{1,0:T(8,128)(2,1)S(1)} %copy-done.2), channel_id=1, source_target_pairs={{0,64},{64,0},{1,65},{65,1},{2,66},{66,2},{3,67},{67,3},{4,68},{68... | collective-permute-start | bytes 2949128 | tf_op jit(solution)/shard_map/ppermute | solution.py:16
  93.9 4.6 %collective-permute-start.12 = (bf16[128,768]{1,0:T(8,128)(2,1)S(1)}, bf16[128,768]{1,0:T(8,128)(2,1)S(1)}, u32[]{:S(2)}, u32[]{:S(2)}) collective-permute-start(bf16[128,768]{1,0:T(8,128)(2,1)S(1)} %fusion.21), channel_id=1, source_target_pairs={{0,3},{1,0},{2,1},{3,2},{4,7},{5,4},{6,5},{7,6},{8,11},{9,8},{10,9... | collective-permute-start | bytes 589832 | tf_op jit(solution)/shard_map/ppermute | solution.py:21
  95.1 6.1 %collective-permute-start.11 = (bf16[128,768]{1,0:T(8,128)(2,1)S(1)}, bf16[128,768]{1,0:T(8,128)(2,1)S(1)}, u32[]{:S(2)}, u32[]{:S(2)}) collective-permute-start(bf16[128,768]{1,0:T(8,128)(2,1)S(1)} %fusion.21), channel_id=1, source_target_pairs={{0,2},{1,3},{2,0},{3,1},{4,6},{5,7},{6,4},{7,5},{8,10},{9,11},{10,... | collective-permute-start | bytes 589832 | tf_op jit(solution)/shard_map/ppermute | solution.py:21
  95.8 7.4 %collective-permute-start.10 = (bf16[128,768]{1,0:T(8,128)(2,1)S(1)}, bf16[128,768]{1,0:T(8,128)(2,1)S(1)}, u32[]{:S(2)}, u32[]{:S(2)}) collective-permute-start(bf16[128,768]{1,0:T(8,128)(2,1)S(1)} %fusion.21), channel_id=1, source_target_pairs={{0,1},{1,2},{2,3},{3,0},{4,5},{5,6},{6,7},{7,4},{8,9},{9,10},{10,1... | collective-permute-start | bytes 589832 | tf_op jit(solution)/shard_map/ppermute | solution.py:21
  105.5 15.6 %all-to-all-start.3 = ((bf16[32,8,640]{2,1,0:T(8,128)(2,1)}), bf16[32,8,640]{2,1,0:T(8,128)(2,1)}, u32[]{:S(2)}, u32[]{:S(2)}) async-start(bf16[32,8,640]{2,1,0:T(8,128)(2,1)} %bitcast.97), calls=%async_computation.3 | async-start | bytes 655360 | tf_op jit(solution)/shard_map/all_to_all | solution.py:25
  111.1 11.0 %collective-permute-start.14 = (bf16[128,1280]{0,1:T(8,128)(2,1)}, bf16[128,1280]{0,1:T(8,128)(2,1)S(1)}, u32[]{:S(2)}, u32[]{:S(2)}) collective-permute-start(bf16[128,1280]{0,1:T(8,128)(2,1)} %bitcast.92), channel_id=1, source_target_pairs={{0,64},{64,0},{1,65},{65,1},{2,66},{66,2},{3,67},{67,3},{4,68},{68... | collective-permute-start | bytes 983048 | tf_op jit(solution)/shard_map/ppermute | solution.py:16
  123.0 20.4 %all-to-all-start.4 = ((bf16[32,8,640]{2,1,0:T(8,128)(2,1)}), bf16[32,8,640]{2,1,0:T(8,128)(2,1)S(1)}, u32[]{:S(2)}, u32[]{:S(2)}) async-start(bf16[32,8,640]{2,1,0:T(8,128)(2,1)} %broadcast_in_dim.118), calls=%async_computation.4 | async-start | bytes 655360 | tf_op jit(solution)/shard_map/all_to_all | solution.py:25
  133.1 6.3 %collective-permute-start.16 = (bf16[64,80]{0,1:T(8,128)(2,1)S(1)}, bf16[64,80]{0,1:T(8,128)(2,1)}, u32[]{:S(2)}, u32[]{:S(2)}) collective-permute-start(bf16[64,80]{0,1:T(8,128)(2,1)S(1)} %pad_maximum_fusion.6), channel_id=1, source_target_pairs={{0,0},{64,1},{128,2},{192,3},{1,64},{65,65},{129,66},{193,67},{2,1... | collective-permute-start | bytes 30728 | tf_op jit(solution)/shard_map/ppermute | solution.py:209
  145.0 6.1 %collective-permute-start.18 = (bf16[128,768]{1,0:T(8,128)(2,1)S(1)}, bf16[128,768]{1,0:T(8,128)(2,1)S(1)}, u32[]{:S(2)}, u32[]{:S(2)}) collective-permute-start(bf16[128,768]{1,0:T(8,128)(2,1)S(1)} %fusion.20), channel_id=1, source_target_pairs={{0,2},{1,3},{2,0},{3,1},{4,6},{5,7},{6,4},{7,5},{8,10},{9,11},{10,... | collective-permute-start | bytes 589832 | tf_op jit(solution)/shard_map/ppermute | solution.py:21
  145.8 7.3 %collective-permute-start.17 = (bf16[128,768]{1,0:T(8,128)(2,1)S(1)}, bf16[128,768]{1,0:T(8,128)(2,1)S(1)}, u32[]{:S(2)}, u32[]{:S(2)}) collective-permute-start(bf16[128,768]{1,0:T(8,128)(2,1)S(1)} %fusion.20), channel_id=1, source_target_pairs={{0,1},{1,2},{2,3},{3,0},{4,5},{5,6},{6,7},{7,4},{8,9},{9,10},{10,1... | collective-permute-start | bytes 589832 | tf_op jit(solution)/shard_map/ppermute | solution.py:21
  153.5 7.7 %collective-permute-start.20 = (bf16[128,384]{1,0:T(8,128)(2,1)S(1)}, bf16[128,384]{1,0:T(8,128)(2,1)S(1)}, u32[]{:S(2)}, u32[]{:S(2)}) collective-permute-start(bf16[128,384]{1,0:T(8,128)(2,1)S(1)} %get-tuple-element.62), channel_id=1, source_target_pairs={{0,64},{64,0},{1,65},{65,1},{2,66},{66,2},{3,67},{67,3},{4,68},{68... | collective-permute-start | bytes 294920 | tf_op jit(solution)/shard_map/ppermute | solution.py:16
  (32 other events, 243.5 us)

commit v5 on v4

--- a/solution.py
+++ b/solution.py
@@ -151,7 +151,13 @@
         out_shape=jax.ShapeDtypeStruct((8, 2 * half + proj.shape[1], 2 * HD), BF16),
         name="attend",
     )(q, kv, kv_other, key_pos.reshape(1, -1), row_pos, proj)
+    message, enc_ready, bias_ready = lax.optimization_barrier(
+        (message, enc_weight, enc_bias)
+    )
+    enc_other = other_core(enc_ready)
+    bias_other = other_core(bias_ready)
     message = exchanged(message, (ZL, Y))
+    message, enc_other, bias_other = lax.optimization_barrier((message, enc_other, bias_other))
     proj_mine = message[:, 2 * half :]
     proj_other = other_core(proj_mine)
     at = zl * 4 + y
@@ -174,12 +180,8 @@
         + [pl.BlockSpec(memory_space=pltpu.VMEM)] * 8,
         name="project",
     )(jnp.stack([zh, co]), *ring, message, proj_other, res_mine, res_other)
-    part, enc_ready, dec_ready, bias_ready = lax.optimization_barrier(
-        (part, enc_weight, dec_weight, enc_bias)
-    )
-    enc_other = other_core(enc_ready)
+    part, dec_ready = lax.optimization_barrier((part, dec_weight))
     dec_other = other_core(dec_ready)
-    bias_other = other_core(bias_ready)
     part = exchanged(part.reshape(32, half // 2, 4 * cols), (ZL, Y, X))
     piece = jnp.sum(part.astype(F32), axis=0).astype(BF16)
 

time: 167 us -> 166 us (level)
  blocking collectives: 0 us -> 15 us
  starting transfers between devices: 77.1 us -> 69.6 us
  waiting for transfers between devices: 46.2 us -> 38.8 us
    all_to_all x0 -> x1, blocking collectives: none -> 15 us  [exchanged(): return lax.all_to_all(a, axes, 0, 0, tiled=True)]
    all_to_all x5 -> x4, waiting for transfers between devices: 28.6 us -> 19.8 us  [exchanged(): return lax.all_to_all(a, axes, 0, 0, tiled=True)]
    all_to_all x5 -> x4, starting transfers between devices: 30 us -> 23.6 us  [exchanged(): return lax.all_to_all(a, axes, 0, 0, tiled=True)]
  transfers between devices with their start and end apart: 27 -> 26, of which waited for: 14 -> 14; matrix products, arithmetic and copies ran while one was open for 14% -> 13% of each run, Pallas kernels for 1% -> 1%
where the time goes in v5:
time: 166 us; the launch traced here: 165 us
  starting transfers between devices  69.6 us (42%)
  waiting for transfers between devices  38.8 us (23%)
  local copies, waits for them, and re-layouts  15.3 us (9%)
  blocking collectives  15 us (9%)
  other arithmetic  10.1 us (6%)
  Pallas kernels  7.48 us (5%)
  matrix products  7.07 us (4%)
    all_to_all x4, starting transfers between devices, exchanged(): return lax.all_to_all(a, axes, 0, 0, tiled=True)  23.6 us
    ppermute x12, starting transfers between devices, shifted(): return lax.ppermute(a, axis, [(i, (i + k) % n) for i in range(n)])  21.4 us
    ppermute x9, starting transfers between devices, other_core(): return lax.ppermute(a, CO, [(0, 1), (1, 0)])  21.1 us
    all_to_all x4, waiting for transfers between devices, exchanged(): return lax.all_to_all(a, axes, 0, 0, tiled=True)  19.8 us
    ppermute x12, waiting for transfers between devices, shifted(): return lax.ppermute(a, axis, [(i, (i + k) % n) for i in range(n)])  16.8 us
    all_to_all x1, blocking collectives, exchanged(): return lax.all_to_all(a, axes, 0, 0, tiled=True)  15 us
    dot_general x10, matrix products, dot(): lax.dot_general(a, b, (contract, ((), ())), preferred_element_type=F32)  5.09 us
    ppermute x1, starting transfers between devices, body(): lax.ppermute(jnp.concatenate(halves, axis=0), (ZL, CO, X), [(b * 4 + a, a...  3.45 us
  transfers between devices with their start and end apart: 26, of which 14 were waited for; matrix products, arithmetic and copies ran while one was open for 13% of the time, Pallas kernels for 1%

profile of v5, /device:TPU:1, one launch (start us, length us, event | category | flops | bytes accessed | tf_op | source)
XLA Modules:
  0.0 164.7 jit_solution(17921994808102809199)
XLA Ops:
  2.9 6.9 %collective-permute-start.2 = (bf16[128,256]{1,0:T(8,128)(2,1)S(1)}, bf16[128,256]{1,0:T(8,128)(2,1)S(1)}, u32[]{:S(2)}, u32[]{:S(2)}) collective-permute-start(bf16[128,256]{1,0:T(8,128)(2,1)S(1)} %get-tuple-element.66), channel_id=1, source_target_pairs={{0,48},{16,0},{32,16},{48,32},{1,49},{17,1},{33,17},{49,33},{2,50}... | collective-permute-start | bytes 196616 | tf_op jit(solution)/shard_map/ppermute | solution.py:21
  10.8 2.3 %collective-permute-start = (bf16[128,256]{1,0:T(8,128)(2,1)S(1)}, bf16[128,256]{1,0:T(8,128)(2,1)S(1)}, u32[]{:S(2)}, u32[]{:S(2)}) collective-permute-start(bf16[128,256]{1,0:T(8,128)(2,1)S(1)} %get-tuple-element.68), channel_id=1, source_target_pairs={{0,16},{16,32},{32,48},{48,0},{1,17},{17,33},{33,49},{49,1},{2,18}... | collective-permute-start | bytes 196616 | tf_op jit(solution)/shard_map/ppermute | solution.py:21
  15.0 2.1 %collective-permute-done.1 = bf16[128,256]{1,0:T(8,128)(2,1)S(1)} collective-permute-done((bf16[128,256]{1,0:T(8,128)(2,1)S(1)}, bf16[128,256]{1,0:T(8,128)(2,1)S(1)}, u32[]{:S(2)}, u32[]{:S(2)}) %collective-permute-start.1) | collective-permute-done | bytes 65568 | tf_op jit(solution)/shard_map/ppermute | solution.py:21
  17.8 2.7 %collective-permute-start.3 = (bf16[4,128,256]{2,1,0:T(8,128)(2,1)S(1)}, bf16[4,128,256]{2,1,0:T(8,128)(2,1)S(1)}, u32[]{:S(2)}, u32[]{:S(2)}) collective-permute-start(bf16[4,128,256]{2,1,0:T(8,128)(2,1)S(1)} %pad_maximum_fusion.3.kv_ref), channel_id=1, source_target_pairs={{0,64},{64,0},{1,65},{65,1},{2,66},{66,2},{3,67},{67,3},{4,68},{68... | collective-permute-start | bytes 786440 | tf_op jit(solution)/shard_map/ppermute | solution.py:16
  23.7 3.1 %attend.1 = bf16[8,160,256]{2,1,0:T(8,128)(2,1)} custom-call(bf16[2,256,128]{2,1,0:T(8,128)(2,1)} %bitcast.100, bf16[4,128,256]{2,1,0:T(8,128)(2,1)} %copy-done.9, bf16[4,128,256]{2,1,0:T(8,128)(2,1)} %copy-done.21, s32[1,512]{1,0:T(1,128)} %select_n.145.key_ref, s32[256,1]{1,0:T(8,128)} %reshape.261.row_ref, bf16[8,96,256]{2,1,0:T(8,128)(2,1)} %fusion.17.proj_ref), custom_call_target="tpu_custom_call" | custom-call | tf_op jit(solution)/shard_map/attend/pallas_call | solution.py:149
  26.7 4.9 %all-to-all-start = ((bf16[8,160,256]{2,1,0:T(8,128)(2,1)}), bf16[8,160,256]{2,1,0:T(8,128)(2,1)S(1)}, u32[]{:S(2)}, u32[]{:S(2)}) async-start(bf16[8,160,256]{2,1,0:T(8,128)(2,1)} %attend.1), calls=%async_computation | async-start | bytes 1310720 | tf_op jit(solution)/shard_map/all_to_all | solution.py:25
  32.3 2.0 %collective-permute-done.5 = f32[384]{0:T(512)S(1)} collective-permute-done((f32[384]{0:T(512)S(1)}, f32[384]{0:T(512)S(1)}, u32[]{:S(2)}, u32[]{:S(2)}) %collective-permute-start.5) | collective-permute-done | bytes 1568 | tf_op jit(solution)/shard_map/ppermute | solution.py:16
  34.5 7.7 %all-to-all-done.message_ref.mine_ref = bf16[8,160,256]{2,1,0:T(8,128)(2,1)S(1)} async-done(((bf16[8,160,256]{2,1,0:T(8,128)(2,1)}), bf16[8,160,256]{2,1,0:T(8,128)(2,1)S(1)}, u32[]{:S(2)}, u32[]{:S(2)}) %all-to-all-start) | async-done | bytes 655392 | tf_op jit(solution)/shard_map/all_to_all | solution.py:25
  45.7 4.0 %collective-permute-start.7 = (bf16[32,256]{1,0:T(8,128)(2,1)}, bf16[32,256]{1,0:T(8,128)(2,1)S(1)}, u32[]{:S(2)}, u32[]{:S(2)}) collective-permute-start(bf16[32,256]{1,0:T(8,128)(2,1)} %combine.1.a_ref), channel_id=1, source_target_pairs={{0,32},{16,48},{32,0},{48,16},{1,33},{17,49},{33,1},{49,17},{2,34}... | collective-permute-start | bytes 49160 | tf_op jit(solution)/shard_map/ppermute | solution.py:21
  49.7 3.1 %collective-permute-start.8 = (bf16[32,256]{1,0:T(8,128)(2,1)}, bf16[32,256]{1,0:T(8,128)(2,1)S(1)}, u32[]{:S(2)}, u32[]{:S(2)}) collective-permute-start(bf16[32,256]{1,0:T(8,128)(2,1)} %combine.1.a_ref), channel_id=1, source_target_pairs={{0,48},{16,0},{32,16},{48,32},{1,49},{17,1},{33,17},{49,33},{2,50}... | collective-permute-start | bytes 49160 | tf_op jit(solution)/shard_map/ppermute | solution.py:21
  56.0 2.5 %project.1 = bf16[8,4,16,320]{3,2,1,0:T(8,128)(2,1)} custom-call(s32[2]{0:T(128)} %pad_add_fusion.at_ref, bf16[32,256]{1,0:T(8,128)(2,1)} %combine.1.a_ref, bf16[32,256]{1,0:T(8,128)(2,1)} %copy-done.24, bf16[32,256]{1,0:T(8,128)(2,1)} %copy-done.25, bf16[32,256]{1,0:T(8,128)(2,1)} %copy-done.26, bf16[8,160,256]{2,1,0:T(8,128)(2,1)} %copy-done.1, ...), custom_call_target="tpu_custom_call" | custom-call | tf_op jit(solution)/shard_map/project/pallas_call | solution.py:176
  58.5 15.0 %all_to_all.25 = bf16[32,16,320]{2,1,0:T(8,128)(2,1)S(1)} all-to-all(bf16[32,16,320]{2,1,0:T(8,128)(2,1)} %bitcast.96), channel_id=1, replica_groups=mesh['zl'=2,'co'=2,'zh'=4,'y'=4,'x'=4] {'zl','y','x'}, dimensions={0} | all-to-all | bytes 655360 | tf_op jit(solution)/shard_map/all_to_all | solution.py:25
  74.4 5.0 %all-to-all-start.2 = ((bf16[32,16,320]{2,1,0:T(8,128)(2,1)}), bf16[32,16,320]{2,1,0:T(8,128)(2,1)S(1)}, u32[]{:S(2)}, u32[]{:S(2)}) async-start(bf16[32,16,320]{2,1,0:T(8,128)(2,1)} %broadcast_in_dim.117), calls=%async_computation.2 | async-start | bytes 786432 | tf_op jit(solution)/shard_map/all_to_all | solution.py:25
  79.3 4.0 %collective-permute-start.13 = (bf16[384,1280]{1,0:T(8,128)(2,1)S(1)}, bf16[384,1280]{1,0:T(8,128)(2,1)S(1)}, u32[]{:S(2)}, u32[]{:S(2)}) collective-permute-start(bf16[384,1280]{1,0:T(8,128)(2,1)S(1)} %copy-done.2), channel_id=1, source_target_pairs={{0,64},{64,0},{1,65},{65,1},{2,66},{66,2},{3,67},{67,3},{4,68},{68... | collective-permute-start | bytes 2949128 | tf_op jit(solution)/shard_map/ppermute | solution.py:16
  83.3 7.5 %all-to-all-done.2 = bf16[32,16,320]{2,1,0:T(8,128)(2,1)S(1)} async-done(((bf16[32,16,320]{2,1,0:T(8,128)(2,1)}), bf16[32,16,320]{2,1,0:T(8,128)(2,1)S(1)}, u32[]{:S(2)}, u32[]{:S(2)}) %all-to-all-start.2) | async-done | bytes 327712 | tf_op jit(solution)/shard_map/all_to_all | solution.py:25
  94.9 2.5 %collective-permute-done.12 = bf16[128,768]{1,0:T(8,128)(2,1)S(1)} collective-permute-done((bf16[128,768]{1,0:T(8,128)(2,1)S(1)}, bf16[128,768]{1,0:T(8,128)(2,1)S(1)}, u32[]{:S(2)}, u32[]{:S(2)}) %collective-permute-start.12) | collective-permute-done | bytes 196640 | tf_op jit(solution)/shard_map/ppermute | solution.py:21
  97.4 2.8 %collective-permute-done.11 = bf16[128,768]{1,0:T(8,128)(2,1)S(1)} collective-permute-done((bf16[128,768]{1,0:T(8,128)(2,1)S(1)}, bf16[128,768]{1,0:T(8,128)(2,1)S(1)}, u32[]{:S(2)}, u32[]{:S(2)}) %collective-permute-start.11) | collective-permute-done | bytes 196640 | tf_op jit(solution)/shard_map/ppermute | solution.py:21
  104.5 4.6 %all-to-all-start.3 = ((bf16[32,8,640]{2,1,0:T(8,128)(2,1)}), bf16[32,8,640]{2,1,0:T(8,128)(2,1)}, u32[]{:S(2)}, u32[]{:S(2)}) async-start(bf16[32,8,640]{2,1,0:T(8,128)(2,1)} %bitcast.97), calls=%async_computation.3 | async-start | bytes 655360 | tf_op jit(solution)/shard_map/all_to_all | solution.py:25
  110.1 6.5 %collective-permute-start.14 = (bf16[128,1280]{0,1:T(8,128)(2,1)}, bf16[128,1280]{0,1:T(8,128)(2,1)S(1)}, u32[]{:S(2)}, u32[]{:S(2)}) collective-permute-start(bf16[128,1280]{0,1:T(8,128)(2,1)} %bitcast.92), channel_id=1, source_target_pairs={{0,64},{64,0},{1,65},{65,1},{2,66},{66,2},{3,67},{67,3},{4,68},{68... | collective-permute-start | bytes 983048 | tf_op jit(solution)/shard_map/ppermute | solution.py:16
  122.0 9.1 %all-to-all-start.4 = ((bf16[32,8,640]{2,1,0:T(8,128)(2,1)}), bf16[32,8,640]{2,1,0:T(8,128)(2,1)S(1)}, u32[]{:S(2)}, u32[]{:S(2)}) async-start(bf16[32,8,640]{2,1,0:T(8,128)(2,1)} %broadcast_in_dim.118), calls=%async_computation.4 | async-start | bytes 655360 | tf_op jit(solution)/shard_map/all_to_all | solution.py:25
  132.1 3.4 %collective-permute-start.16 = (bf16[64,80]{0,1:T(8,128)(2,1)S(1)}, bf16[64,80]{0,1:T(8,128)(2,1)}, u32[]{:S(2)}, u32[]{:S(2)}) collective-permute-start(bf16[64,80]{0,1:T(8,128)(2,1)S(1)} %pad_maximum_fusion.6), channel_id=1, source_target_pairs={{0,0},{64,1},{128,2},{192,3},{1,64},{65,65},{129,66},{193,67},{2,1... | collective-permute-start | bytes 30728 | tf_op jit(solution)/shard_map/ppermute | solution.py:211
  138.5 3.9 %all-to-all-done.4 = bf16[32,8,640]{2,1,0:T(8,128)(2,1)S(1)} async-done(((bf16[32,8,640]{2,1,0:T(8,128)(2,1)}), bf16[32,8,640]{2,1,0:T(8,128)(2,1)S(1)}, u32[]{:S(2)}, u32[]{:S(2)}) %all-to-all-start.4) | async-done | bytes 327712 | tf_op jit(solution)/shard_map/all_to_all | solution.py:25
  145.4 2.9 %collective-permute-done.19 = bf16[128,768]{1,0:T(8,128)(2,1)S(1)} collective-permute-done((bf16[128,768]{1,0:T(8,128)(2,1)S(1)}, bf16[128,768]{1,0:T(8,128)(2,1)S(1)}, u32[]{:S(2)}, u32[]{:S(2)}) %collective-permute-start.19) | collective-permute-done | bytes 196640 | tf_op jit(solution)/shard_map/ppermute | solution.py:21
  152.5 6.2 %collective-permute-start.20 = (bf16[128,384]{1,0:T(8,128)(2,1)S(1)}, bf16[128,384]{1,0:T(8,128)(2,1)S(1)}, u32[]{:S(2)}, u32[]{:S(2)}) collective-permute-start(bf16[128,384]{1,0:T(8,128)(2,1)S(1)} %get-tuple-element.70), channel_id=1, source_target_pairs={{0,64},{64,0},{1,65},{65,1},{2,66},{66,2},{3,67},{67,3},{4,68},{68... | collective-permute-start | bytes 294920 | tf_op jit(solution)/shard_map/ppermute | solution.py:16
  (167 shorter events, 48.9 us)
Async XLA Ops:
  2.9 12.1 %collective-permute-start.2 = (bf16[128,256]{1,0:T(8,128)(2,1)S(1)}, bf16[128,256]{1,0:T(8,128)(2,1)S(1)}, u32[]{:S(2)}, u32[]{:S(2)}) collective-permute-start(bf16[128,256]{1,0:T(8,128)(2,1)S(1)} %get-tuple-element.66), channel_id=1, source_target_pairs={{0,48},{16,0},{32,16},{48,32},{1,49},{17,1},{33,17},{49,33},{2,50}... | collective-permute-start | bytes 196616 | tf_op jit(solution)/shard_map/ppermute | solution.py:21
  9.8 7.2 %collective-permute-start.1 = (bf16[128,256]{1,0:T(8,128)(2,1)S(1)}, bf16[128,256]{1,0:T(8,128)(2,1)S(1)}, u32[]{:S(2)}, u32[]{:S(2)}) collective-permute-start(bf16[128,256]{1,0:T(8,128)(2,1)S(1)} %get-tuple-element.67), channel_id=1, source_target_pairs={{0,32},{16,48},{32,0},{48,16},{1,33},{17,49},{33,1},{49,17},{2,34}... | collective-permute-start | bytes 196616 | tf_op jit(solution)/shard_map/ppermute | solution.py:21
  10.8 6.9 %collective-permute-start = (bf16[128,256]{1,0:T(8,128)(2,1)S(1)}, bf16[128,256]{1,0:T(8,128)(2,1)S(1)}, u32[]{:S(2)}, u32[]{:S(2)}) collective-permute-start(bf16[128,256]{1,0:T(8,128)(2,1)S(1)} %get-tuple-element.68), channel_id=1, source_target_pairs={{0,16},{16,32},{32,48},{48,0},{1,17},{17,33},{33,49},{49,1},{2,18}... | collective-permute-start | bytes 196616 | tf_op jit(solution)/shard_map/ppermute | solution.py:21
  17.8 5.1 %collective-permute-start.3 = (bf16[4,128,256]{2,1,0:T(8,128)(2,1)S(1)}, bf16[4,128,256]{2,1,0:T(8,128)(2,1)S(1)}, u32[]{:S(2)}, u32[]{:S(2)}) collective-permute-start(bf16[4,128,256]{2,1,0:T(8,128)(2,1)S(1)} %pad_maximum_fusion.3.kv_ref), channel_id=1, source_target_pairs={{0,64},{64,0},{1,65},{65,1},{2,66},{66,2},{3,67},{67,3},{4,68},{68... | collective-permute-start | bytes 786440 | tf_op jit(solution)/shard_map/ppermute | solution.py:16
  26.7 15.5 %all-to-all-start = ((bf16[8,160,256]{2,1,0:T(8,128)(2,1)}), bf16[8,160,256]{2,1,0:T(8,128)(2,1)S(1)}, u32[]{:S(2)}, u32[]{:S(2)}) async-start(bf16[8,160,256]{2,1,0:T(8,128)(2,1)} %attend.1), calls=%async_computation | async-start | bytes 1310720 | tf_op jit(solution)/shard_map/all_to_all | solution.py:25
  31.7 2.8 %collective-permute-start.4 = (bf16[1280,384]{1,0:T(8,128)(2,1)S(1)}, bf16[1280,384]{1,0:T(8,128)(2,1)}, u32[]{:S(2)}, u32[]{:S(2)}) collective-permute-start(bf16[1280,384]{1,0:T(8,128)(2,1)S(1)} %copy-done.10), channel_id=1, source_target_pairs={{0,64},{64,0},{1,65},{65,1},{2,66},{66,2},{3,67},{67,3},{4,68},{68... | collective-permute-start | bytes 2949128 | tf_op jit(solution)/shard_map/ppermute | solution.py:16
  42.2 12.1 %collective-permute-start.9 = (bf16[8,96,256]{2,1,0:T(8,128)(2,1)S(1)}, bf16[8,96,256]{2,1,0:T(8,128)(2,1)S(1)}, u32[]{:S(2)}, u32[]{:S(2)}) collective-permute-start(bf16[8,96,256]{2,1,0:T(8,128)(2,1)S(1)} %slice.50), channel_id=1, source_target_pairs={{0,64},{64,0},{1,65},{65,1},{2,66},{66,2},{3,67},{67,3},{4,68},{68... | collective-permute-start | bytes 1179656 | tf_op jit(solution)/shard_map/ppermute | solution.py:16
  45.3 10.0 %collective-permute-start.6 = (bf16[32,256]{1,0:T(8,128)(2,1)}, bf16[32,256]{1,0:T(8,128)(2,1)S(1)}, u32[]{:S(2)}, u32[]{:S(2)}) collective-permute-start(bf16[32,256]{1,0:T(8,128)(2,1)} %combine.1.a_ref), channel_id=1, source_target_pairs={{0,16},{16,32},{32,48},{48,0},{1,17},{17,33},{33,49},{49,1},{2,18}... | collective-permute-start | bytes 49160 | tf_op jit(solution)/shard_map/ppermute | solution.py:21
  45.7 9.7 %collective-permute-start.7 = (bf16[32,256]{1,0:T(8,128)(2,1)}, bf16[32,256]{1,0:T(8,128)(2,1)S(1)}, u32[]{:S(2)}, u32[]{:S(2)}) collective-permute-start(bf16[32,256]{1,0:T(8,128)(2,1)} %combine.1.a_ref), channel_id=1, source_target_pairs={{0,32},{16,48},{32,0},{48,16},{1,33},{17,49},{33,1},{49,17},{2,34}... | collective-permute-start | bytes 49160 | tf_op jit(solution)/shard_map/ppermute | solution.py:21
  49.7 5.7 %collective-permute-start.8 = (bf16[32,256]{1,0:T(8,128)(2,1)}, bf16[32,256]{1,0:T(8,128)(2,1)S(1)}, u32[]{:S(2)}, u32[]{:S(2)}) collective-permute-start(bf16[32,256]{1,0:T(8,128)(2,1)} %combine.1.a_ref), channel_id=1, source_target_pairs={{0,48},{16,0},{32,16},{48,32},{1,49},{17,1},{33,17},{49,33},{2,50}... | collective-permute-start | bytes 49160 | tf_op jit(solution)/shard_map/ppermute | solution.py:21
  74.4 16.4 %all-to-all-start.2 = ((bf16[32,16,320]{2,1,0:T(8,128)(2,1)}), bf16[32,16,320]{2,1,0:T(8,128)(2,1)S(1)}, u32[]{:S(2)}, u32[]{:S(2)}) async-start(bf16[32,16,320]{2,1,0:T(8,128)(2,1)} %broadcast_in_dim.117), calls=%async_computation.2 | async-start | bytes 786432 | tf_op jit(solution)/shard_map/all_to_all | solution.py:25
  79.3 23.8 %collective-permute-start.13 = (bf16[384,1280]{1,0:T(8,128)(2,1)S(1)}, bf16[384,1280]{1,0:T(8,128)(2,1)S(1)}, u32[]{:S(2)}, u32[]{:S(2)}) collective-permute-start(bf16[384,1280]{1,0:T(8,128)(2,1)S(1)} %copy-done.2), channel_id=1, source_target_pairs={{0,64},{64,0},{1,65},{65,1},{2,66},{66,2},{3,67},{67,3},{4,68},{68... | collective-permute-start | bytes 2949128 | tf_op jit(solution)/shard_map/ppermute | solution.py:16
  92.8 4.6 %collective-permute-start.12 = (bf16[128,768]{1,0:T(8,128)(2,1)S(1)}, bf16[128,768]{1,0:T(8,128)(2,1)S(1)}, u32[]{:S(2)}, u32[]{:S(2)}) collective-permute-start(bf16[128,768]{1,0:T(8,128)(2,1)S(1)} %fusion.21), channel_id=1, source_target_pairs={{0,3},{1,0},{2,1},{3,2},{4,7},{5,4},{6,5},{7,6},{8,11},{9,8},{10,9... | collective-permute-start | bytes 589832 | tf_op jit(solution)/shard_map/ppermute | solution.py:21
  94.1 6.1 %collective-permute-start.11 = (bf16[128,768]{1,0:T(8,128)(2,1)S(1)}, bf16[128,768]{1,0:T(8,128)(2,1)S(1)}, u32[]{:S(2)}, u32[]{:S(2)}) collective-permute-start(bf16[128,768]{1,0:T(8,128)(2,1)S(1)} %fusion.21), channel_id=1, source_target_pairs={{0,2},{1,3},{2,0},{3,1},{4,6},{5,7},{6,4},{7,5},{8,10},{9,11},{10,... | collective-permute-start | bytes 589832 | tf_op jit(solution)/shard_map/ppermute | solution.py:21
  94.8 7.5 %collective-permute-start.10 = (bf16[128,768]{1,0:T(8,128)(2,1)S(1)}, bf16[128,768]{1,0:T(8,128)(2,1)S(1)}, u32[]{:S(2)}, u32[]{:S(2)}) collective-permute-start(bf16[128,768]{1,0:T(8,128)(2,1)S(1)} %fusion.21), channel_id=1, source_target_pairs={{0,1},{1,2},{2,3},{3,0},{4,5},{5,6},{6,7},{7,4},{8,9},{9,10},{10,1... | collective-permute-start | bytes 589832 | tf_op jit(solution)/shard_map/ppermute | solution.py:21
  104.5 15.6 %all-to-all-start.3 = ((bf16[32,8,640]{2,1,0:T(8,128)(2,1)}), bf16[32,8,640]{2,1,0:T(8,128)(2,1)}, u32[]{:S(2)}, u32[]{:S(2)}) async-start(bf16[32,8,640]{2,1,0:T(8,128)(2,1)} %bitcast.97), calls=%async_computation.3 | async-start | bytes 655360 | tf_op jit(solution)/shard_map/all_to_all | solution.py:25
  110.1 11.0 %collective-permute-start.14 = (bf16[128,1280]{0,1:T(8,128)(2,1)}, bf16[128,1280]{0,1:T(8,128)(2,1)S(1)}, u32[]{:S(2)}, u32[]{:S(2)}) collective-permute-start(bf16[128,1280]{0,1:T(8,128)(2,1)} %bitcast.92), channel_id=1, source_target_pairs={{0,64},{64,0},{1,65},{65,1},{2,66},{66,2},{3,67},{67,3},{4,68},{68... | collective-permute-start | bytes 983048 | tf_op jit(solution)/shard_map/ppermute | solution.py:16
  122.0 20.3 %all-to-all-start.4 = ((bf16[32,8,640]{2,1,0:T(8,128)(2,1)}), bf16[32,8,640]{2,1,0:T(8,128)(2,1)S(1)}, u32[]{:S(2)}, u32[]{:S(2)}) async-start(bf16[32,8,640]{2,1,0:T(8,128)(2,1)} %broadcast_in_dim.118), calls=%async_computation.4 | async-start | bytes 655360 | tf_op jit(solution)/shard_map/all_to_all | solution.py:25
  132.1 6.4 %collective-permute-start.16 = (bf16[64,80]{0,1:T(8,128)(2,1)S(1)}, bf16[64,80]{0,1:T(8,128)(2,1)}, u32[]{:S(2)}, u32[]{:S(2)}) collective-permute-start(bf16[64,80]{0,1:T(8,128)(2,1)S(1)} %pad_maximum_fusion.6), channel_id=1, source_target_pairs={{0,0},{64,1},{128,2},{192,3},{1,64},{65,65},{129,66},{193,67},{2,1... | collective-permute-start | bytes 30728 | tf_op jit(solution)/shard_map/ppermute | solution.py:211
  143.6 4.6 %collective-permute-start.19 = (bf16[128,768]{1,0:T(8,128)(2,1)S(1)}, bf16[128,768]{1,0:T(8,128)(2,1)S(1)}, u32[]{:S(2)}, u32[]{:S(2)}) collective-permute-start(bf16[128,768]{1,0:T(8,128)(2,1)S(1)} %fusion.20), channel_id=1, source_target_pairs={{0,3},{1,0},{2,1},{3,2},{4,7},{5,4},{6,5},{7,6},{8,11},{9,8},{10,9... | collective-permute-start | bytes 589832 | tf_op jit(solution)/shard_map/ppermute | solution.py:21
  144.0 6.1 %collective-permute-start.18 = (bf16[128,768]{1,0:T(8,128)(2,1)S(1)}, bf16[128,768]{1,0:T(8,128)(2,1)S(1)}, u32[]{:S(2)}, u32[]{:S(2)}) collective-permute-start(bf16[128,768]{1,0:T(8,128)(2,1)S(1)} %fusion.20), channel_id=1, source_target_pairs={{0,2},{1,3},{2,0},{3,1},{4,6},{5,7},{6,4},{7,5},{8,10},{9,11},{10,... | collective-permute-start | bytes 589832 | tf_op jit(solution)/shard_map/ppermute | solution.py:21
  144.8 7.3 %collective-permute-start.17 = (bf16[128,768]{1,0:T(8,128)(2,1)S(1)}, bf16[128,768]{1,0:T(8,128)(2,1)S(1)}, u32[]{:S(2)}, u32[]{:S(2)}) collective-permute-start(bf16[128,768]{1,0:T(8,128)(2,1)S(1)} %fusion.20), channel_id=1, source_target_pairs={{0,1},{1,2},{2,3},{3,0},{4,5},{5,6},{6,7},{7,4},{8,9},{9,10},{10,1... | collective-permute-start | bytes 589832 | tf_op jit(solution)/shard_map/ppermute | solution.py:21
  152.5 7.7 %collective-permute-start.20 = (bf16[128,384]{1,0:T(8,128)(2,1)S(1)}, bf16[128,384]{1,0:T(8,128)(2,1)S(1)}, u32[]{:S(2)}, u32[]{:S(2)}) collective-permute-start(bf16[128,384]{1,0:T(8,128)(2,1)S(1)} %get-tuple-element.70), channel_id=1, source_target_pairs={{0,64},{64,0},{1,65},{65,1},{2,66},{66,2},{3,67},{67,3},{4,68},{68... | collective-permute-start | bytes 294920 | tf_op jit(solution)/shard_map/ppermute | solution.py:16
  158.7 3.6 %collective-permute-start.21 = (bf16[2,128,640]{2,1,0:T(8,128)(2,1)S(1)}, bf16[2,128,640]{2,1,0:T(8,128)(2,1)S(1)}, u32[]{:S(2)}, u32[]{:S(2)}) collective-permute-start(bf16[2,128,640]{2,1,0:T(8,128)(2,1)S(1)} %bitcast.85), channel_id=1, source_target_pairs={{0,64},{64,0},{1,65},{65,1},{2,66},{66,2},{3,67},{67,3},{4,68},{68... | collective-permute-start | bytes 983048 | tf_op jit(solution)/shard_map/ppermute | solution.py:16
  (33 other events, 223.5 us)

commit v6 on v5

--- a/solution.py
+++ b/solution.py
@@ -74,10 +74,10 @@
     out_ref[:, HD:] = attention[half:].astype(BF16)
 
 
-def project(at_ref, a_ref, b_ref, c_ref, d_ref, mine_ref, other_ref, res_mine_ref, res_other_ref, out_ref):
+def project(a_ref, b_ref, c_ref, d_ref, mine_ref, other_ref, res_mine_ref, res_other_ref, out_ref):
     attention = jnp.concatenate([ref[...] for ref in (a_ref, b_ref, c_ref, d_ref)])
     few, cols = (out_ref.shape[2], out_ref.shape[3] // 4)
-    turn, core = (at_ref[0], at_ref[1])
+    turn, core = (lax.axis_index(ZH), lax.axis_index(CO))
     for high in range(2):
         for ref, res, low in ((mine_ref, res_mine_ref, core), (other_ref, res_other_ref, 1 - core)):
             top = ref.shape[1] - other_ref.shape[1]
@@ -176,10 +176,8 @@
     part = pl.pallas_call(
         project,
         out_shape=jax.ShapeDtypeStruct((8, 4, half // 2, 4 * cols), BF16),
-        in_specs=[pl.BlockSpec(memory_space=pltpu.SMEM)]
-        + [pl.BlockSpec(memory_space=pltpu.VMEM)] * 8,
         name="project",
-    )(jnp.stack([zh, co]), *ring, message, proj_other, res_mine, res_other)
+    )(*ring, message, proj_other, res_mine, res_other)
     part, dec_ready = lax.optimization_barrier((part, dec_weight))
     dec_other = other_core(dec_ready)
     part = exchanged(part.reshape(32, half // 2, 4 * cols), (ZL, Y, X))

time: 166 us -> 166 us (level)
  no operation moved by 1% of the time
where the time goes in v6:
time: 166 us; the launch traced here: 165 us
  starting transfers between devices  70.1 us (42%)
  waiting for transfers between devices  38.8 us (23%)
  local copies, waits for them, and re-layouts  15.3 us (9%)
  blocking collectives  15.1 us (9%)
  other arithmetic  9.52 us (6%)
  Pallas kernels  7.47 us (4%)
  matrix products  7.06 us (4%)
    all_to_all x4, starting transfers between devices, exchanged(): return lax.all_to_all(a, axes, 0, 0, tiled=True)  24.1 us
    ppermute x12, starting transfers between devices, shifted(): return lax.ppermute(a, axis, [(i, (i + k) % n) for i in range(n)])  21.4 us
    ppermute x9, starting transfers between devices, other_core(): return lax.ppermute(a, CO, [(0, 1), (1, 0)])  21.1 us
    all_to_all x4, waiting for transfers between devices, exchanged(): return lax.all_to_all(a, axes, 0, 0, tiled=True)  19.8 us
    ppermute x12, waiting for transfers between devices, shifted(): return lax.ppermute(a, axis, [(i, (i + k) % n) for i in range(n)])  16.8 us
    all_to_all x1, blocking collectives, exchanged(): return lax.all_to_all(a, axes, 0, 0, tiled=True)  15.1 us
    dot_general x10, matrix products, dot(): lax.dot_general(a, b, (contract, ((), ())), preferred_element_type=F32)  5.08 us
    ppermute x1, starting transfers between devices, body(): lax.ppermute(jnp.concatenate(halves, axis=0), (ZL, CO, X), [(b * 4 + a, a...  3.47 us
  transfers between devices with their start and end apart: 26, of which 14 were waited for; matrix products, arithmetic and copies ran while one was open for 13% of the time, Pallas kernels for 1%

profile of v6, /device:TPU:1, one launch (start us, length us, event | category | flops | bytes accessed | tf_op | source)
XLA Modules:
  0.0 164.7 jit_solution(14686000398260451741)
XLA Ops:
  2.9 6.9 %collective-permute-start.2 = (bf16[128,256]{1,0:T(8,128)(2,1)S(1)}, bf16[128,256]{1,0:T(8,128)(2,1)S(1)}, u32[]{:S(2)}, u32[]{:S(2)}) collective-permute-start(bf16[128,256]{1,0:T(8,128)(2,1)S(1)} %get-tuple-element.66), channel_id=1, source_target_pairs={{0,48},{16,0},{32,16},{48,32},{1,49},{17,1},{33,17},{49,33},{2,50}... | collective-permute-start | bytes 196616 | tf_op jit(solution)/shard_map/ppermute | solution.py:21
  10.8 2.3 %collective-permute-start = (bf16[128,256]{1,0:T(8,128)(2,1)S(1)}, bf16[128,256]{1,0:T(8,128)(2,1)S(1)}, u32[]{:S(2)}, u32[]{:S(2)}) collective-permute-start(bf16[128,256]{1,0:T(8,128)(2,1)S(1)} %get-tuple-element.68), channel_id=1, source_target_pairs={{0,16},{16,32},{32,48},{48,0},{1,17},{17,33},{33,49},{49,1},{2,18}... | collective-permute-start | bytes 196616 | tf_op jit(solution)/shard_map/ppermute | solution.py:21
  15.0 2.1 %collective-permute-done.1 = bf16[128,256]{1,0:T(8,128)(2,1)S(1)} collective-permute-done((bf16[128,256]{1,0:T(8,128)(2,1)S(1)}, bf16[128,256]{1,0:T(8,128)(2,1)S(1)}, u32[]{:S(2)}, u32[]{:S(2)}) %collective-permute-start.1) | collective-permute-done | bytes 65568 | tf_op jit(solution)/shard_map/ppermute | solution.py:21
  17.8 2.7 %collective-permute-start.3 = (bf16[4,128,256]{2,1,0:T(8,128)(2,1)S(1)}, bf16[4,128,256]{2,1,0:T(8,128)(2,1)S(1)}, u32[]{:S(2)}, u32[]{:S(2)}) collective-permute-start(bf16[4,128,256]{2,1,0:T(8,128)(2,1)S(1)} %pad_maximum_fusion.3.kv_ref), channel_id=1, source_target_pairs={{0,64},{64,0},{1,65},{65,1},{2,66},{66,2},{3,67},{67,3},{4,68},{68... | collective-permute-start | bytes 786440 | tf_op jit(solution)/shard_map/ppermute | solution.py:16
  23.7 3.1 %attend.1 = bf16[8,160,256]{2,1,0:T(8,128)(2,1)} custom-call(bf16[2,256,128]{2,1,0:T(8,128)(2,1)} %bitcast.99, bf16[4,128,256]{2,1,0:T(8,128)(2,1)} %copy-done.9, bf16[4,128,256]{2,1,0:T(8,128)(2,1)} %copy-done.21, s32[1,512]{1,0:T(1,128)} %select_n.145.key_ref, s32[256,1]{1,0:T(8,128)} %reshape.261.row_ref, bf16[8,96,256]{2,1,0:T(8,128)(2,1)} %fusion.17.proj_ref), custom_call_target="tpu_custom_call" | custom-call | tf_op jit(solution)/shard_map/attend/pallas_call | solution.py:149
  26.7 4.9 %all-to-all-start = ((bf16[8,160,256]{2,1,0:T(8,128)(2,1)}), bf16[8,160,256]{2,1,0:T(8,128)(2,1)S(1)}, u32[]{:S(2)}, u32[]{:S(2)}) async-start(bf16[8,160,256]{2,1,0:T(8,128)(2,1)} %attend.1), calls=%async_computation | async-start | bytes 1310720 | tf_op jit(solution)/shard_map/all_to_all | solution.py:25
  32.3 2.0 %collective-permute-done.5 = f32[384]{0:T(512)S(1)} collective-permute-done((f32[384]{0:T(512)S(1)}, f32[384]{0:T(512)S(1)}, u32[]{:S(2)}, u32[]{:S(2)}) %collective-permute-start.5) | collective-permute-done | bytes 1568 | tf_op jit(solution)/shard_map/ppermute | solution.py:16
  34.5 7.7 %all-to-all-done.message_ref.mine_ref = bf16[8,160,256]{2,1,0:T(8,128)(2,1)S(1)} async-done(((bf16[8,160,256]{2,1,0:T(8,128)(2,1)}), bf16[8,160,256]{2,1,0:T(8,128)(2,1)S(1)}, u32[]{:S(2)}, u32[]{:S(2)}) %all-to-all-start) | async-done | bytes 655392 | tf_op jit(solution)/shard_map/all_to_all | solution.py:25
  45.6 4.0 %collective-permute-start.7 = (bf16[32,256]{1,0:T(8,128)(2,1)}, bf16[32,256]{1,0:T(8,128)(2,1)S(1)}, u32[]{:S(2)}, u32[]{:S(2)}) collective-permute-start(bf16[32,256]{1,0:T(8,128)(2,1)} %combine.1.a_ref), channel_id=1, source_target_pairs={{0,32},{16,48},{32,0},{48,16},{1,33},{17,49},{33,1},{49,17},{2,34}... | collective-permute-start | bytes 49160 | tf_op jit(solution)/shard_map/ppermute | solution.py:21
  49.6 3.1 %collective-permute-start.8 = (bf16[32,256]{1,0:T(8,128)(2,1)}, bf16[32,256]{1,0:T(8,128)(2,1)S(1)}, u32[]{:S(2)}, u32[]{:S(2)}) collective-permute-start(bf16[32,256]{1,0:T(8,128)(2,1)} %combine.1.a_ref), channel_id=1, source_target_pairs={{0,48},{16,0},{32,16},{48,32},{1,49},{17,1},{33,17},{49,33},{2,50}... | collective-permute-start | bytes 49160 | tf_op jit(solution)/shard_map/ppermute | solution.py:21
  55.4 2.5 %project.1 = bf16[8,4,16,320]{3,2,1,0:T(8,128)(2,1)} custom-call(bf16[32,256]{1,0:T(8,128)(2,1)} %combine.1.a_ref, bf16[32,256]{1,0:T(8,128)(2,1)} %copy-done.25, bf16[32,256]{1,0:T(8,128)(2,1)} %copy-done.26, bf16[32,256]{1,0:T(8,128)(2,1)} %copy-done.27, bf16[8,160,256]{2,1,0:T(8,128)(2,1)} %copy-done.1, bf16[8,96,256]{2,1,0:T(8,128)(2,1)} %copy-done.18, ...), custom_call_target="tpu_custom_call" | custom-call | tf_op jit(solution)/shard_map/project/pallas_call | solution.py:176
  57.9 15.1 %all_to_all.25 = bf16[32,16,320]{2,1,0:T(8,128)(2,1)S(1)} all-to-all(bf16[32,16,320]{2,1,0:T(8,128)(2,1)} %bitcast.95), channel_id=1, replica_groups=mesh['zl'=2,'co'=2,'zh'=4,'y'=4,'x'=4] {'zl','y','x'}, dimensions={0} | all-to-all | bytes 655360 | tf_op jit(solution)/shard_map/all_to_all | solution.py:25
  73.8 5.5 %all-to-all-start.2 = ((bf16[32,16,320]{2,1,0:T(8,128)(2,1)}), bf16[32,16,320]{2,1,0:T(8,128)(2,1)S(1)}, u32[]{:S(2)}, u32[]{:S(2)}) async-start(bf16[32,16,320]{2,1,0:T(8,128)(2,1)} %broadcast_in_dim.117), calls=%async_computation.2 | async-start | bytes 786432 | tf_op jit(solution)/shard_map/all_to_all | solution.py:25
  79.3 4.0 %collective-permute-start.13 = (bf16[384,1280]{1,0:T(8,128)(2,1)S(1)}, bf16[384,1280]{1,0:T(8,128)(2,1)S(1)}, u32[]{:S(2)}, u32[]{:S(2)}) collective-permute-start(bf16[384,1280]{1,0:T(8,128)(2,1)S(1)} %copy-done.2), channel_id=1, source_target_pairs={{0,64},{64,0},{1,65},{65,1},{2,66},{66,2},{3,67},{67,3},{4,68},{68... | collective-permute-start | bytes 2949128 | tf_op jit(solution)/shard_map/ppermute | solution.py:16
  83.3 7.5 %all-to-all-done.2 = bf16[32,16,320]{2,1,0:T(8,128)(2,1)S(1)} async-done(((bf16[32,16,320]{2,1,0:T(8,128)(2,1)}), bf16[32,16,320]{2,1,0:T(8,128)(2,1)S(1)}, u32[]{:S(2)}, u32[]{:S(2)}) %all-to-all-start.2) | async-done | bytes 327712 | tf_op jit(solution)/shard_map/all_to_all | solution.py:25
  94.9 2.5 %collective-permute-done.12 = bf16[128,768]{1,0:T(8,128)(2,1)S(1)} collective-permute-done((bf16[128,768]{1,0:T(8,128)(2,1)S(1)}, bf16[128,768]{1,0:T(8,128)(2,1)S(1)}, u32[]{:S(2)}, u32[]{:S(2)}) %collective-permute-start.12) | collective-permute-done | bytes 196640 | tf_op jit(solution)/shard_map/ppermute | solution.py:21
  97.4 2.7 %collective-permute-done.11 = bf16[128,768]{1,0:T(8,128)(2,1)S(1)} collective-permute-done((bf16[128,768]{1,0:T(8,128)(2,1)S(1)}, bf16[128,768]{1,0:T(8,128)(2,1)S(1)}, u32[]{:S(2)}, u32[]{:S(2)}) %collective-permute-start.11) | collective-permute-done | bytes 196640 | tf_op jit(solution)/shard_map/ppermute | solution.py:21
  104.5 4.6 %all-to-all-start.3 = ((bf16[32,8,640]{2,1,0:T(8,128)(2,1)}), bf16[32,8,640]{2,1,0:T(8,128)(2,1)}, u32[]{:S(2)}, u32[]{:S(2)}) async-start(bf16[32,8,640]{2,1,0:T(8,128)(2,1)} %bitcast.96), calls=%async_computation.3 | async-start | bytes 655360 | tf_op jit(solution)/shard_map/all_to_all | solution.py:25
  110.1 6.5 %collective-permute-start.14 = (bf16[128,1280]{0,1:T(8,128)(2,1)}, bf16[128,1280]{0,1:T(8,128)(2,1)S(1)}, u32[]{:S(2)}, u32[]{:S(2)}) collective-permute-start(bf16[128,1280]{0,1:T(8,128)(2,1)} %bitcast.91), channel_id=1, source_target_pairs={{0,64},{64,0},{1,65},{65,1},{2,66},{66,2},{3,67},{67,3},{4,68},{68... | collective-permute-start | bytes 983048 | tf_op jit(solution)/shard_map/ppermute | solution.py:16
  122.0 9.1 %all-to-all-start.4 = ((bf16[32,8,640]{2,1,0:T(8,128)(2,1)}), bf16[32,8,640]{2,1,0:T(8,128)(2,1)S(1)}, u32[]{:S(2)}, u32[]{:S(2)}) async-start(bf16[32,8,640]{2,1,0:T(8,128)(2,1)} %broadcast_in_dim.118), calls=%async_computation.4 | async-start | bytes 655360 | tf_op jit(solution)/shard_map/all_to_all | solution.py:25
  132.1 3.5 %collective-permute-start.16 = (bf16[64,80]{0,1:T(8,128)(2,1)S(1)}, bf16[64,80]{0,1:T(8,128)(2,1)}, u32[]{:S(2)}, u32[]{:S(2)}) collective-permute-start(bf16[64,80]{0,1:T(8,128)(2,1)S(1)} %pad_maximum_fusion.6), channel_id=1, source_target_pairs={{0,0},{64,1},{128,2},{192,3},{1,64},{65,65},{129,66},{193,67},{2,1... | collective-permute-start | bytes 30728 | tf_op jit(solution)/shard_map/ppermute | solution.py:209
  138.5 3.9 %all-to-all-done.4 = bf16[32,8,640]{2,1,0:T(8,128)(2,1)S(1)} async-done(((bf16[32,8,640]{2,1,0:T(8,128)(2,1)}), bf16[32,8,640]{2,1,0:T(8,128)(2,1)S(1)}, u32[]{:S(2)}, u32[]{:S(2)}) %all-to-all-start.4) | async-done | bytes 327712 | tf_op jit(solution)/shard_map/all_to_all | solution.py:25
  145.4 2.8 %collective-permute-done.19 = bf16[128,768]{1,0:T(8,128)(2,1)S(1)} collective-permute-done((bf16[128,768]{1,0:T(8,128)(2,1)S(1)}, bf16[128,768]{1,0:T(8,128)(2,1)S(1)}, u32[]{:S(2)}, u32[]{:S(2)}) %collective-permute-start.19) | collective-permute-done | bytes 196640 | tf_op jit(solution)/shard_map/ppermute | solution.py:21
  152.4 6.2 %collective-permute-start.20 = (bf16[128,384]{1,0:T(8,128)(2,1)S(1)}, bf16[128,384]{1,0:T(8,128)(2,1)S(1)}, u32[]{:S(2)}, u32[]{:S(2)}) collective-permute-start(bf16[128,384]{1,0:T(8,128)(2,1)S(1)} %get-tuple-element.70), channel_id=1, source_target_pairs={{0,64},{64,0},{1,65},{65,1},{2,66},{66,2},{3,67},{67,3},{4,68},{68... | collective-permute-start | bytes 294920 | tf_op jit(solution)/shard_map/ppermute | solution.py:16
  (166 shorter events, 48.3 us)
Async XLA Ops:
  2.9 12.1 %collective-permute-start.2 = (bf16[128,256]{1,0:T(8,128)(2,1)S(1)}, bf16[128,256]{1,0:T(8,128)(2,1)S(1)}, u32[]{:S(2)}, u32[]{:S(2)}) collective-permute-start(bf16[128,256]{1,0:T(8,128)(2,1)S(1)} %get-tuple-element.66), channel_id=1, source_target_pairs={{0,48},{16,0},{32,16},{48,32},{1,49},{17,1},{33,17},{49,33},{2,50}... | collective-permute-start | bytes 196616 | tf_op jit(solution)/shard_map/ppermute | solution.py:21
  9.8 7.2 %collective-permute-start.1 = (bf16[128,256]{1,0:T(8,128)(2,1)S(1)}, bf16[128,256]{1,0:T(8,128)(2,1)S(1)}, u32[]{:S(2)}, u32[]{:S(2)}) collective-permute-start(bf16[128,256]{1,0:T(8,128)(2,1)S(1)} %get-tuple-element.67), channel_id=1, source_target_pairs={{0,32},{16,48},{32,0},{48,16},{1,33},{17,49},{33,1},{49,17},{2,34}... | collective-permute-start | bytes 196616 | tf_op jit(solution)/shard_map/ppermute | solution.py:21
  10.8 6.9 %collective-permute-start = (bf16[128,256]{1,0:T(8,128)(2,1)S(1)}, bf16[128,256]{1,0:T(8,128)(2,1)S(1)}, u32[]{:S(2)}, u32[]{:S(2)}) collective-permute-start(bf16[128,256]{1,0:T(8,128)(2,1)S(1)} %get-tuple-element.68), channel_id=1, source_target_pairs={{0,16},{16,32},{32,48},{48,0},{1,17},{17,33},{33,49},{49,1},{2,18}... | collective-permute-start | bytes 196616 | tf_op jit(solution)/shard_map/ppermute | solution.py:21
  17.8 5.1 %collective-permute-start.3 = (bf16[4,128,256]{2,1,0:T(8,128)(2,1)S(1)}, bf16[4,128,256]{2,1,0:T(8,128)(2,1)S(1)}, u32[]{:S(2)}, u32[]{:S(2)}) collective-permute-start(bf16[4,128,256]{2,1,0:T(8,128)(2,1)S(1)} %pad_maximum_fusion.3.kv_ref), channel_id=1, source_target_pairs={{0,64},{64,0},{1,65},{65,1},{2,66},{66,2},{3,67},{67,3},{4,68},{68... | collective-permute-start | bytes 786440 | tf_op jit(solution)/shard_map/ppermute | solution.py:16
  26.7 15.5 %all-to-all-start = ((bf16[8,160,256]{2,1,0:T(8,128)(2,1)}), bf16[8,160,256]{2,1,0:T(8,128)(2,1)S(1)}, u32[]{:S(2)}, u32[]{:S(2)}) async-start(bf16[8,160,256]{2,1,0:T(8,128)(2,1)} %attend.1), calls=%async_computation | async-start | bytes 1310720 | tf_op jit(solution)/shard_map/all_to_all | solution.py:25
  31.7 2.8 %collective-permute-start.4 = (bf16[1280,384]{1,0:T(8,128)(2,1)S(1)}, bf16[1280,384]{1,0:T(8,128)(2,1)}, u32[]{:S(2)}, u32[]{:S(2)}) collective-permute-start(bf16[1280,384]{1,0:T(8,128)(2,1)S(1)} %copy-done.10), channel_id=1, source_target_pairs={{0,64},{64,0},{1,65},{65,1},{2,66},{66,2},{3,67},{67,3},{4,68},{68... | collective-permute-start | bytes 2949128 | tf_op jit(solution)/shard_map/ppermute | solution.py:16
  42.2 11.5 %collective-permute-start.9 = (bf16[8,96,256]{2,1,0:T(8,128)(2,1)S(1)}, bf16[8,96,256]{2,1,0:T(8,128)(2,1)S(1)}, u32[]{:S(2)}, u32[]{:S(2)}) collective-permute-start(bf16[8,96,256]{2,1,0:T(8,128)(2,1)S(1)} %slice.50), channel_id=1, source_target_pairs={{0,64},{64,0},{1,65},{65,1},{2,66},{66,2},{3,67},{67,3},{4,68},{68... | collective-permute-start | bytes 1179656 | tf_op jit(solution)/shard_map/ppermute | solution.py:16
  45.3 9.5 %collective-permute-start.6 = (bf16[32,256]{1,0:T(8,128)(2,1)}, bf16[32,256]{1,0:T(8,128)(2,1)S(1)}, u32[]{:S(2)}, u32[]{:S(2)}) collective-permute-start(bf16[32,256]{1,0:T(8,128)(2,1)} %combine.1.a_ref), channel_id=1, source_target_pairs={{0,16},{16,32},{32,48},{48,0},{1,17},{17,33},{33,49},{49,1},{2,18}... | collective-permute-start | bytes 49160 | tf_op jit(solution)/shard_map/ppermute | solution.py:21
  45.6 9.2 %collective-permute-start.7 = (bf16[32,256]{1,0:T(8,128)(2,1)}, bf16[32,256]{1,0:T(8,128)(2,1)S(1)}, u32[]{:S(2)}, u32[]{:S(2)}) collective-permute-start(bf16[32,256]{1,0:T(8,128)(2,1)} %combine.1.a_ref), channel_id=1, source_target_pairs={{0,32},{16,48},{32,0},{48,16},{1,33},{17,49},{33,1},{49,17},{2,34}... | collective-permute-start | bytes 49160 | tf_op jit(solution)/shard_map/ppermute | solution.py:21
  49.6 5.2 %collective-permute-start.8 = (bf16[32,256]{1,0:T(8,128)(2,1)}, bf16[32,256]{1,0:T(8,128)(2,1)S(1)}, u32[]{:S(2)}, u32[]{:S(2)}) collective-permute-start(bf16[32,256]{1,0:T(8,128)(2,1)} %combine.1.a_ref), channel_id=1, source_target_pairs={{0,48},{16,0},{32,16},{48,32},{1,49},{17,1},{33,17},{49,33},{2,50}... | collective-permute-start | bytes 49160 | tf_op jit(solution)/shard_map/ppermute | solution.py:21
  73.8 16.9 %all-to-all-start.2 = ((bf16[32,16,320]{2,1,0:T(8,128)(2,1)}), bf16[32,16,320]{2,1,0:T(8,128)(2,1)S(1)}, u32[]{:S(2)}, u32[]{:S(2)}) async-start(bf16[32,16,320]{2,1,0:T(8,128)(2,1)} %broadcast_in_dim.117), calls=%async_computation.2 | async-start | bytes 786432 | tf_op jit(solution)/shard_map/all_to_all | solution.py:25
  79.3 23.8 %collective-permute-start.13 = (bf16[384,1280]{1,0:T(8,128)(2,1)S(1)}, bf16[384,1280]{1,0:T(8,128)(2,1)S(1)}, u32[]{:S(2)}, u32[]{:S(2)}) collective-permute-start(bf16[384,1280]{1,0:T(8,128)(2,1)S(1)} %copy-done.2), channel_id=1, source_target_pairs={{0,64},{64,0},{1,65},{65,1},{2,66},{66,2},{3,67},{67,3},{4,68},{68... | collective-permute-start | bytes 2949128 | tf_op jit(solution)/shard_map/ppermute | solution.py:16
  92.8 4.6 %collective-permute-start.12 = (bf16[128,768]{1,0:T(8,128)(2,1)S(1)}, bf16[128,768]{1,0:T(8,128)(2,1)S(1)}, u32[]{:S(2)}, u32[]{:S(2)}) collective-permute-start(bf16[128,768]{1,0:T(8,128)(2,1)S(1)} %fusion.21), channel_id=1, source_target_pairs={{0,3},{1,0},{2,1},{3,2},{4,7},{5,4},{6,5},{7,6},{8,11},{9,8},{10,9... | collective-permute-start | bytes 589832 | tf_op jit(solution)/shard_map/ppermute | solution.py:21
  94.0 6.1 %collective-permute-start.11 = (bf16[128,768]{1,0:T(8,128)(2,1)S(1)}, bf16[128,768]{1,0:T(8,128)(2,1)S(1)}, u32[]{:S(2)}, u32[]{:S(2)}) collective-permute-start(bf16[128,768]{1,0:T(8,128)(2,1)S(1)} %fusion.21), channel_id=1, source_target_pairs={{0,2},{1,3},{2,0},{3,1},{4,6},{5,7},{6,4},{7,5},{8,10},{9,11},{10,... | collective-permute-start | bytes 589832 | tf_op jit(solution)/shard_map/ppermute | solution.py:21
  94.8 7.4 %collective-permute-start.10 = (bf16[128,768]{1,0:T(8,128)(2,1)S(1)}, bf16[128,768]{1,0:T(8,128)(2,1)S(1)}, u32[]{:S(2)}, u32[]{:S(2)}) collective-permute-start(bf16[128,768]{1,0:T(8,128)(2,1)S(1)} %fusion.21), channel_id=1, source_target_pairs={{0,1},{1,2},{2,3},{3,0},{4,5},{5,6},{6,7},{7,4},{8,9},{9,10},{10,1... | collective-permute-start | bytes 589832 | tf_op jit(solution)/shard_map/ppermute | solution.py:21
  104.5 15.6 %all-to-all-start.3 = ((bf16[32,8,640]{2,1,0:T(8,128)(2,1)}), bf16[32,8,640]{2,1,0:T(8,128)(2,1)}, u32[]{:S(2)}, u32[]{:S(2)}) async-start(bf16[32,8,640]{2,1,0:T(8,128)(2,1)} %bitcast.96), calls=%async_computation.3 | async-start | bytes 655360 | tf_op jit(solution)/shard_map/all_to_all | solution.py:25
  110.1 11.0 %collective-permute-start.14 = (bf16[128,1280]{0,1:T(8,128)(2,1)}, bf16[128,1280]{0,1:T(8,128)(2,1)S(1)}, u32[]{:S(2)}, u32[]{:S(2)}) collective-permute-start(bf16[128,1280]{0,1:T(8,128)(2,1)} %bitcast.91), channel_id=1, source_target_pairs={{0,64},{64,0},{1,65},{65,1},{2,66},{66,2},{3,67},{67,3},{4,68},{68... | collective-permute-start | bytes 983048 | tf_op jit(solution)/shard_map/ppermute | solution.py:16
  122.0 20.3 %all-to-all-start.4 = ((bf16[32,8,640]{2,1,0:T(8,128)(2,1)}), bf16[32,8,640]{2,1,0:T(8,128)(2,1)S(1)}, u32[]{:S(2)}, u32[]{:S(2)}) async-start(bf16[32,8,640]{2,1,0:T(8,128)(2,1)} %broadcast_in_dim.118), calls=%async_computation.4 | async-start | bytes 655360 | tf_op jit(solution)/shard_map/all_to_all | solution.py:25
  132.1 6.4 %collective-permute-start.16 = (bf16[64,80]{0,1:T(8,128)(2,1)S(1)}, bf16[64,80]{0,1:T(8,128)(2,1)}, u32[]{:S(2)}, u32[]{:S(2)}) collective-permute-start(bf16[64,80]{0,1:T(8,128)(2,1)S(1)} %pad_maximum_fusion.6), channel_id=1, source_target_pairs={{0,0},{64,1},{128,2},{192,3},{1,64},{65,65},{129,66},{193,67},{2,1... | collective-permute-start | bytes 30728 | tf_op jit(solution)/shard_map/ppermute | solution.py:209
  143.6 4.6 %collective-permute-start.19 = (bf16[128,768]{1,0:T(8,128)(2,1)S(1)}, bf16[128,768]{1,0:T(8,128)(2,1)S(1)}, u32[]{:S(2)}, u32[]{:S(2)}) collective-permute-start(bf16[128,768]{1,0:T(8,128)(2,1)S(1)} %fusion.20), channel_id=1, source_target_pairs={{0,3},{1,0},{2,1},{3,2},{4,7},{5,4},{6,5},{7,6},{8,11},{9,8},{10,9... | collective-permute-start | bytes 589832 | tf_op jit(solution)/shard_map/ppermute | solution.py:21
  144.0 6.1 %collective-permute-start.18 = (bf16[128,768]{1,0:T(8,128)(2,1)S(1)}, bf16[128,768]{1,0:T(8,128)(2,1)S(1)}, u32[]{:S(2)}, u32[]{:S(2)}) collective-permute-start(bf16[128,768]{1,0:T(8,128)(2,1)S(1)} %fusion.20), channel_id=1, source_target_pairs={{0,2},{1,3},{2,0},{3,1},{4,6},{5,7},{6,4},{7,5},{8,10},{9,11},{10,... | collective-permute-start | bytes 589832 | tf_op jit(solution)/shard_map/ppermute | solution.py:21
  144.8 7.3 %collective-permute-start.17 = (bf16[128,768]{1,0:T(8,128)(2,1)S(1)}, bf16[128,768]{1,0:T(8,128)(2,1)S(1)}, u32[]{:S(2)}, u32[]{:S(2)}) collective-permute-start(bf16[128,768]{1,0:T(8,128)(2,1)S(1)} %fusion.20), channel_id=1, source_target_pairs={{0,1},{1,2},{2,3},{3,0},{4,5},{5,6},{6,7},{7,4},{8,9},{9,10},{10,1... | collective-permute-start | bytes 589832 | tf_op jit(solution)/shard_map/ppermute | solution.py:21
  152.4 7.7 %collective-permute-start.20 = (bf16[128,384]{1,0:T(8,128)(2,1)S(1)}, bf16[128,384]{1,0:T(8,128)(2,1)S(1)}, u32[]{:S(2)}, u32[]{:S(2)}) collective-permute-start(bf16[128,384]{1,0:T(8,128)(2,1)S(1)} %get-tuple-element.70), channel_id=1, source_target_pairs={{0,64},{64,0},{1,65},{65,1},{2,66},{66,2},{3,67},{67,3},{4,68},{68... | collective-permute-start | bytes 294920 | tf_op jit(solution)/shard_map/ppermute | solution.py:16
  158.6 3.6 %collective-permute-start.21 = (bf16[2,128,640]{2,1,0:T(8,128)(2,1)S(1)}, bf16[2,128,640]{2,1,0:T(8,128)(2,1)S(1)}, u32[]{:S(2)}, u32[]{:S(2)}) collective-permute-start(bf16[2,128,640]{2,1,0:T(8,128)(2,1)S(1)} %bitcast.84), channel_id=1, source_target_pairs={{0,64},{64,0},{1,65},{65,1},{2,66},{66,2},{3,67},{67,3},{4,68},{68... | collective-permute-start | bytes 983048 | tf_op jit(solution)/shard_map/ppermute | solution.py:16
  (33 other events, 223.9 us)
